TPU v7x, 256 devices: a whole 4x4x8 slice. The times are simulated.
256 devices in a mesh: rows: 64 (over z_hi, y, x, core), ch: 4 (over z_lo).
Axes of the slice: x: 4, y: 4, z: 8 (z_hi: 2, z_lo: 4; z = z_hi * 4 + z_lo), core: 2. Of those that a mesh axis runs over, the one named last changes fastest.
Arguments:
- pixels: bfloat16 [256, 96, 2048], P('rows', 'ch'), may hold values from -6 to 6
- depth_weight: float32 [96, 9], P('ch'), may hold values from -2 to 2
- mix_weight: bfloat16 [96, 96], replicated, may hold values from -0.625 to 0.625
- spectral_real: bfloat16 [256, 96, 1024], P(None, 'ch', 'rows'), may hold values from -4 to 4
- spectral_imag: bfloat16 [256, 96, 1024], P(None, 'ch', 'rows'), may hold values from -4 to 4
- query_weight: bfloat16 [96, 128], P('ch'), may hold values from -0.625 to 0.625
- key_weight: bfloat16 [96, 128], P('ch'), may hold values from -0.625 to 0.625
- query_pixels: int32 [4096], P('rows'), may hold values from 0 to 8191
- key_pixels: int32 [16384], P('rows'), may hold values from 0 to 8191
- positives: int32 [4096], P('rows'), may hold values from 0 to 16383
Outputs:
- encoded: bfloat16 [256, 96, 2048], P('rows', 'ch')
- losses: float32 [4096], P(('rows', 'ch'))
Inputs may be any that keep to these rules, and one draw needn't show every extreme that they name: `query_pixels`: each entry is r * 2048 + x for a pixel at row r and column x of the query's own slab of 4 rows. `key_pixels`: each entry is r * 2048 + x for a pixel at row r and column x of the key's own slab of 4 rows. `positives`: the number of the positive key among all 16384 keys, numbered slab by slab in the order of key_pixels.
All inputs are finite; a program needn't handle non-finite values.
Results may differ from a plain program's by a relative error of at most 0.0065.
Values may be sent and summed in bfloat16 or wider, within the bound.
A program may use at most 64 MiB of HBM per device.

v0:
```python
import jax
import jax.numpy as jnp
from jax import lax
from jax.sharding import PartitionSpec as P

DILATION = 2


score_scale = 10.0
exact = lax.Precision.HIGHEST


def extended(cells, sides, width):
    for axis, dim in sides:
        count = lax.axis_size(axis)
        ends = count - 1
        head = lax.slice_in_dim(cells, 0, width, axis=dim)
        tail = lax.slice_in_dim(cells, cells.shape[dim] - width, cells.shape[dim], axis=dim)
        cells = jnp.concatenate(
            [
                lax.ppermute(tail, axis, [(i, (i + 1) % count) for i in range(ends)]),
                cells,
                lax.ppermute(head, axis, [((i + 1) % count, i) for i in range(ends)]),
            ],
            axis=dim,
        )
    return cells


def ring_pieces(values, axis):
    count = lax.axis_size(axis)
    pieces = [values]
    for shift in range(1, count):
        pieces.append(
            lax.ppermute(values, axis, [(i, (i + shift) % count) for i in range(count)])
        )
    return pieces


def unit_rows(values):
    return values * lax.rsqrt(jnp.sum(values * values, axis=1, keepdims=True) + 1e-06)


def cos_sin(turns, length):
    angles = turns.astype(jnp.float32) * (2.0 * jnp.pi / length)
    return (jnp.cos(angles), jnp.sin(angles))


def split_bf16(table):
    high = table.astype(jnp.bfloat16)
    low = (table - high.astype(jnp.float32)).astype(jnp.bfloat16)
    return (high, low)


def row_factors(columns, kept):
    outer = 32
    inner = columns // outer
    a = lax.broadcasted_iota(jnp.int32, (outer, kept), 0)
    k = lax.broadcasted_iota(jnp.int32, (outer, kept), 1)
    cos_a, sin_a = cos_sin(a * k % outer, outer)
    b = lax.broadcasted_iota(jnp.int32, (inner, kept), 0)
    kb = lax.broadcasted_iota(jnp.int32, (inner, kept), 1)
    cos_b, sin_b = cos_sin(b * kb % columns, columns)
    return (cos_a, sin_a, cos_b, sin_b)


def row_tables(factors):
    cos_a, sin_a, cos_b, sin_b = factors
    columns = cos_a.shape[0] * cos_b.shape[0]
    kept = cos_a.shape[1]
    cos_t = cos_a[:, None, :] * cos_b[None, :, :] - sin_a[:, None, :] * sin_b[None, :, :]
    sin_t = sin_a[:, None, :] * cos_b[None, :, :] + cos_a[:, None, :] * sin_b[None, :, :]
    table = jnp.concatenate([cos_t, -sin_t], axis=2).reshape(columns, 2 * kept)
    return split_bf16(table)


def two_pass(eq, left, right_pair):
    return sum(
        jnp.einsum(eq, left, part, preferred_element_type=jnp.float32) for part in right_pair
    )


def column_tables(height):
    m = lax.broadcasted_iota(jnp.int32, (height, height), 0)
    y = lax.broadcasted_iota(jnp.int32, (height, height), 1)
    return cos_sin(m * y % height, height)


def block_complex(cos_t, sin_t, sign):
    return jnp.concatenate(
        [
            jnp.concatenate([cos_t, -sign * sin_t], axis=1),
            jnp.concatenate([sign * sin_t, cos_t], axis=1),
        ],
        axis=0,
    )


def score_fold(query_unit, targets, key_number):

    def add_block(carried, shard_piece, offset):
        scores = (
            jnp.einsum("qd,kd->qk", query_unit, shard_piece, preferred_element_type=jnp.float32)
            * score_scale
        )
        numbers = key_number(lax.broadcasted_iota(jnp.int32, (1, shard_piece.shape[0]), 1))
        exp_sums = jnp.sum(jnp.exp(scores), axis=1)
        picked = jnp.sum(jnp.where(targets[:, None] == numbers, scores, 0.0), axis=1)
        return (exp_sums, picked)

    return add_block


def same_number(gathered):
    return gathered


def body(
    pixels,
    depth_weight,
    mix_weight,
    spectral_real,
    spectral_imag,
    query_weight,
    key_weight,
    query_pixels,
    key_pixels,
    positives,
):
    slab_rows, groups, columns = pixels.shape
    half_cols = columns // 2
    channel = lax.axis_index("ch")
    group_count = lax.axis_size("ch")
    padded = extended(pixels, (("rows", 0),), DILATION)
    padded = jnp.pad(padded, ((0, 0), (0, 0), (DILATION, DILATION)))
    summed = pixels.astype(jnp.float32)
    for tap_row in range(3):
        for tap_col in range(3):
            shifted = padded[
                tap_row * DILATION : tap_row * DILATION + slab_rows,
                :,
                tap_col * DILATION : tap_col * DILATION + columns,
            ]
            summed = summed + depth_weight[:, 3 * tap_row + tap_col][
                None, :, None
            ] * shifted.astype(jnp.float32)
    conv_out = summed.astype(jnp.bfloat16)
    conv_out, factors = lax.optimization_barrier((conv_out, row_factors(columns, half_cols)))
    local_columns = lax.dynamic_slice_in_dim(mix_weight, channel * groups, groups, 1)
    ordered_rows = jnp.concatenate(
        [
            lax.dynamic_slice_in_dim(
                local_columns, (channel - shift) % group_count * groups, groups, 0
            )
            for shift in range(group_count)
        ],
        axis=0,
    )
    mixture = jnp.einsum(
        "rcw,cd->rdw",
        jnp.concatenate(ring_pieces(conv_out, "ch"), axis=1),
        ordered_rows,
        preferred_element_type=jnp.float32,
    )
    hidden = jax.nn.gelu(mixture).astype(jnp.bfloat16)
    table_pair = row_tables(factors)
    slabs = lax.axis_size("rows")
    spectrum = two_pass("rcx,xk->rck", hidden, table_pair)
    width = half_cols // slabs
    wire = spectrum.reshape(slab_rows, groups, 2, slabs, width)
    wire = jnp.transpose(wire, (2, 3, 0, 1, 4)).reshape(2, slabs, slab_rows, groups * width)
    columns_both = lax.all_to_all(
        wire.astype(jnp.bfloat16), "rows", split_axis=1, concat_axis=1, tiled=True
    )
    lanes = groups * width
    height = slabs * slab_rows
    column_cos, column_sin = column_tables(height)
    forward_pair = split_bf16(block_complex(column_cos, column_sin, -1.0))
    full = sum(
        jnp.einsum("my,yn->mn", part, columns_both.reshape(2 * height, lanes),
                   preferred_element_type=jnp.float32)
        for part in forward_pair
    )
    full_real, full_imag = full[:height], full[height:]
    kernel_real = spectral_real.astype(jnp.float32).reshape(height, lanes)
    kernel_imag = spectral_imag.astype(jnp.float32).reshape(height, lanes)
    product = jnp.concatenate(
        [full_real * kernel_real - full_imag * kernel_imag,
         full_real * kernel_imag + full_imag * kernel_real],
        axis=0,
    )
    back = jnp.einsum(
        "ym,mn->yn", block_complex(column_cos, column_sin, 1.0), product,
        precision=exact, preferred_element_type=jnp.float32,
    )
    back = (back * (1.0 / height)).astype(jnp.bfloat16)
    rows_both = lax.all_to_all(
        back.reshape(2, slabs, slab_rows, lanes), "rows", split_axis=1, concat_axis=1, tiled=True
    ).reshape(2, slabs, slab_rows, groups, width)
    rows_both = jnp.transpose(rows_both, (2, 3, 0, 1, 4)).reshape(slab_rows, groups, columns)
    doubling = jnp.where(lax.broadcasted_iota(jnp.int32, (1, 1, columns), 2) % half_cols == 0, 1.0, 2.0)
    weighting = doubling * (1.0 / columns)
    row_both = (rows_both.astype(jnp.float32) * weighting).astype(jnp.bfloat16)
    spatial = two_pass("rck,xk->rcx", row_both, table_pair)
    encoded = (hidden.astype(jnp.float32) + spatial).astype(jnp.bfloat16)
    key_count = key_pixels.shape[0]
    query_count = query_pixels.shape[0]
    quarter = query_count // group_count
    slab = lax.axis_index("rows")
    weights_all = jnp.concatenate([key_weight, query_weight], axis=1)
    weights_all = lax.all_to_all(
        jnp.broadcast_to(weights_all[None], (group_count,) + weights_all.shape),
        "ch", split_axis=0, concat_axis=0, tiled=True,
    ).reshape(group_count * groups, -1)
    sampled = jnp.concatenate([key_pixels, query_pixels])
    features = encoded[sampled // columns, :, sampled % columns]
    features = lax.all_to_all(
        jnp.broadcast_to(features[None], (group_count,) + features.shape),
        "ch", split_axis=0, concat_axis=0, tiled=True,
    )
    features = jnp.transpose(features, (1, 0, 2)).reshape(features.shape[1], -1)
    key_dim = key_weight.shape[1]
    key_unit = unit_rows(
        jnp.dot(features[:key_count], weights_all[:, :key_dim], preferred_element_type=jnp.float32)
    ).astype(jnp.bfloat16)
    own_queries = lax.dynamic_slice_in_dim(features, key_count + channel * quarter, quarter, 0)
    query_unit = unit_rows(
        jnp.dot(own_queries, weights_all[:, key_dim:], preferred_element_type=jnp.float32)
    ).astype(jnp.bfloat16)
    targets = lax.dynamic_slice_in_dim(positives, channel * quarter, quarter, 0)
    coded = jnp.concatenate([targets // 128, targets % 128]).astype(jnp.bfloat16)
    coded = jnp.pad(coded, (0, key_dim - 2 * quarter))[None, :]
    packet = jnp.concatenate([query_unit, coded], axis=0)
    gathered = lax.all_to_all(
        jnp.broadcast_to(packet[None], (slabs,) + packet.shape),
        "rows",
        split_axis=0,
        concat_axis=0,
        tiled=True,
    )
    all_queries = gathered[:, :quarter, :].reshape(-1, key_dim)
    coded_all = gathered[:, quarter, :].astype(jnp.int32)
    all_targets = (coded_all[:, :quarter] * 128 + coded_all[:, quarter : 2 * quarter]).reshape(-1)
    scores = (
        jnp.einsum("qd,kd->qk", all_queries, key_unit, preferred_element_type=jnp.float32)
        * score_scale
    )
    numbers = slab * key_count + lax.broadcasted_iota(jnp.int32, (1, key_count), 1)
    exp_sums = jnp.sum(jnp.exp(scores), axis=1)
    picked = jnp.sum(jnp.where(all_targets[:, None] == numbers, scores, 0.0), axis=1)
    reduced = lax.all_to_all(
        jnp.stack([exp_sums, picked], axis=1).reshape(slabs, quarter, 2),
        "rows",
        split_axis=0,
        concat_axis=0,
        tiled=True,
    ).sum(axis=0)
    losses = jnp.log(reduced[:, 0]) - reduced[:, 1]
    return (encoded, losses)


def solution(mesh):
    placed = (
        P("rows", "ch", None),
        P("ch", None),
        P(),
        P(None, "ch", "rows"),
        P(None, "ch", "rows"),
        P("ch", None),
        P("ch", None),
        P("rows"),
        P("rows"),
        P("rows"),
    )
    return jax.shard_map(
        body,
        mesh=mesh,
        in_specs=placed,
        out_specs=(P("rows", "ch", None), P(("rows", "ch"))),
        check_vma=False,
    )
```

profile of v0, /device:TPU:1, one launch (start us, length us, event | category | flops | bytes accessed | tf_op | source)
XLA Modules:
  0.0 212.6 jit_solution(1086939703033129499)
XLA Ops:
  0.6 1.1 fusion.118
  1.7 4.5 %collective-permute-start = (bf16[2,24,2048]{2,1,0:T(8,128)(2,1)S(1)}, bf16[2,24,2048]{2,1,0:T(8,128)(2,1)S(1)}, u32[]{:S(2)}, u32[]{:S(2)}) collective-permute-start(bf16[2,24,2048]{2,1,0:T(8,128)(2,1)S(1)} %get-tuple-element.20), channel_id=1, source_target_pairs={{0,4},{4,8},{8,12},{12,16},{16,20},{20,24},{24,28},{28,32},{32,36}... | collective-permute-start | bytes 589832 | tf_op jit(solution)/shard_map/ppermute | solution.py:21
  6.2 1.9 collective-permute-start.1
  8.1 1.0 fusion.76
  9.2 0.5 fusion.82
  9.8 0.9 fusion.119
  11.0 1.0 slice_bitcast_fusion.8
  12.0 1.2 collective-permute-done.1
  13.2 1.3 fusion.30
  14.5 2.3 %fusion.39 = bf16[4,24,2048]{2,1,0:T(8,128)(2,1)S(1)} fusion(bf16[4,24,2048]{2,1,0:T(8,128)(2,1)} %param.10, bf16[8,24,2052]{2,1,0:T(8,128)(2,1)S(1)} %fusion.30, bf16[2,24,2048]{2,1,0:T(8,128)(2,1)S(1)} %collective-permute-done.1, bf16[2,24,2048]{2,1,0:T(8,128)(2,1)S(1)} %collective-permute-done, f32[24]{0:T(128)S(1)} %get-tuple-element.33, ...), kind=kLoop, calls=%fused_computation.58 | loop fusion | flops 5898240 | bytes 3539808 | tf_op jit(solution)/shard_map/convert_element_type | solution.py:147
  16.8 1.7 collective-permute-start.2
  18.5 3.0 %collective-permute-start.3 = (bf16[4,24,2048]{2,1,0:T(8,128)(2,1)S(1)}, bf16[4,24,2048]{2,1,0:T(8,128)(2,1)S(1)}, u32[]{:S(2)}, u32[]{:S(2)}) collective-permute-start(bf16[4,24,2048]{2,1,0:T(8,128)(2,1)S(1)} %fusion.39), channel_id=1, source_target_pairs={{0,2},{1,3},{2,0},{3,1},{4,6},{5,7},{6,4},{7,5},{8,10},{9,11},{10,... | collective-permute-start | bytes 1179656 | tf_op jit(solution)/shard_map/ppermute | solution.py:35
  21.5 0.7 collective-permute-start.4
  22.2 2.5 %multiply_subtract_fusion = (f32[32,64,1024]{2,1,0:T(8,128)S(1)}, f32[32,64,1024]{2,1,0:T(8,128)S(1)}) fusion(f32[64,1024]{1,0:T(8,128)S(1)} %get-tuple-element.11, f32[32,1024]{1,0:T(8,128)S(1)} %get-tuple-element.10, f32[64,1024]{1,0:T(8,128)S(1)} %get-tuple-element.9, f32[32,1024]{1,0:T(8,128)S(1)} %get-tuple-element.8), kind=kLoop, calls=%fused_computation.7 | loop fusion | flops 14680064 | bytes 17563648 | tf_op jit(solution)/shard_map/sub | solution.py:71
  24.7 7.0 %collective-permute-done.2 = bf16[4,24,2048]{2,1,0:T(8,128)(2,1)S(1)} collective-permute-done((bf16[4,24,2048]{2,1,0:T(8,128)(2,1)S(1)}, bf16[4,24,2048]{2,1,0:T(8,128)(2,1)S(1)}, u32[]{:S(2)}, u32[]{:S(2)}) %collective-permute-start.2) | collective-permute-done | bytes 393248 | tf_op jit(solution)/shard_map/ppermute | solution.py:35
  31.7 15.7 %collective-permute-done.3 = bf16[4,24,2048]{2,1,0:T(8,128)(2,1)S(1)} collective-permute-done((bf16[4,24,2048]{2,1,0:T(8,128)(2,1)S(1)}, bf16[4,24,2048]{2,1,0:T(8,128)(2,1)S(1)}, u32[]{:S(2)}, u32[]{:S(2)}) %collective-permute-start.3) | collective-permute-done | bytes 393248 | tf_op jit(solution)/shard_map/ppermute | solution.py:35
  47.3 0.5 fusion.49
  47.9 1.5 fusion.19
  49.4 1.5 fusion.4
  50.9 2.5 %convert_element_type.154 = bf16[4,24,2,64,16]{4,3,2,1,0:T(8,128)(2,1)S(1)} reshape(bf16[4,24,2048]{2,1,0:T(8,128)(2,1)S(1)} %fusion.4) | data formatting | bytes 786432 | tf_op jit(solution)/shard_map/convert_element_type | solution.py:173
  53.5 2.2 %copy.71 = bf16[2,64,4,24,16]{1,4,3,2,0:T(8,128)(2,1)} copy(bf16[2,64,4,24,16]{4,1,0,3,2:T(8,128)(2,1)S(1)} %bitcast.78) | data formatting | bytes 786432 | tf_op jit(solution)/shard_map/convert_element_type | solution.py:173
  55.7 2.2 %copy.72 = bf16[2,64,4,384]{3,2,0,1:T(4,128)(2,1)} copy(bf16[2,64,4,384]{1,3,2,0:T(8,128)(2,1)} %bitcast.80) | data formatting | bytes 786432 | tf_op jit(solution)/shard_map/convert_element_type | solution.py:173
  57.9 13.6 %all-to-all-start = ((bf16[2,64,4,384]{3,2,0,1:T(4,128)(2,1)}), bf16[2,64,4,384]{3,2,0,1:T(4,128)(2,1)S(1)}, u32[]{:S(2)}, u32[]{:S(2)}) async-start(bf16[2,64,4,384]{3,2,0,1:T(4,128)(2,1)} %copy.72), calls=%async_computation | async-start | bytes 786432 | tf_op jit(solution)/shard_map/all_to_all | solution.py:172
  71.5 1.0 bitcast_convert_fusion
  72.6 1.0 bitcast_convert_fusion.1
  73.8 1.0 fusion.75
  74.8 1.0 broadcast_multiply_fusion
  75.8 10.6 %all-to-all-done = bf16[2,64,4,384]{3,2,0,1:T(4,128)(2,1)S(1)} async-done(((bf16[2,64,4,384]{3,2,0,1:T(4,128)(2,1)}), bf16[2,64,4,384]{3,2,0,1:T(4,128)(2,1)S(1)}, u32[]{:S(2)}, u32[]{:S(2)}) %all-to-all-start) | async-done | bytes 393248 | tf_op jit(solution)/shard_map/all_to_all | solution.py:172
  87.6 1.8 fusion.14
  89.5 0.9 copy.78
  90.4 4.6 %all-to-all-start.1 = ((bf16[2,64,4,384]{3,2,0,1:T(4,128)(2,1)}), bf16[2,64,4,384]{3,2,0,1:T(4,128)(2,1)S(1)}, u32[]{:S(2)}, u32[]{:S(2)}) async-start(bf16[2,64,4,384]{3,2,0,1:T(4,128)(2,1)} %copy.78), calls=%async_computation.1 | async-start | bytes 786432 | tf_op jit(solution)/shard_map/all_to_all | solution.py:197
  95.2 14.6 %all-to-all-done.1 = bf16[2,64,4,384]{3,2,0,1:T(4,128)(2,1)S(1)} async-done(((bf16[2,64,4,384]{3,2,0,1:T(4,128)(2,1)}), bf16[2,64,4,384]{3,2,0,1:T(4,128)(2,1)S(1)}, u32[]{:S(2)}, u32[]{:S(2)}) %all-to-all-start.1) | async-done | bytes 393248 | tf_op jit(solution)/shard_map/all_to_all | solution.py:197
  109.8 0.6 broadcast_in_dim.22
  110.5 16.7 %all-to-all-start.3 = ((bf16[4,24,256]{2,1,0:T(8,128)(2,1)}), bf16[4,24,256]{2,1,0:T(8,128)(2,1)S(1)}, u32[]{:S(2)}, u32[]{:S(2)}) async-start(bf16[4,24,256]{2,1,0:T(8,128)(2,1)} %broadcast_in_dim.22), calls=%async_computation.3 | async-start | bytes 98304 | tf_op jit(solution)/shard_map/all_to_all | solution.py:211
  127.8 4.1 %copy.80 = f32[4,24,2,64,16]{4,3,2,1,0:T(8,128)} copy(f32[4,24,2,64,16]{3,4,1,0,2:T(8,128)S(1)} %convert_bitcast_fusion) | data formatting | bytes 1572864 | tf_op jit(solution)/shard_map/convert_element_type | solution.py:203
  131.8 6.3 %reshape.356 = f32[4,24,2048]{2,1,0:T(8,128)S(1)} reshape(f32[4,24,2,64,16]{4,3,2,1,0:T(8,128)} %copy.80) | data formatting | bytes 1572864 | tf_op jit(solution)/shard_map/convert_element_type | solution.py:203
  138.1 7.3 %fusion.17 = f32[4,24,2048]{2,1,0:T(8,128)S(1)} fusion(f32[2048,1024]{1,0:T(8,128)} %bitcast.76, f32[2048,1024]{1,0:T(8,128)} %bitcast.72, f32[4,24,2048]{2,1,0:T(8,128)S(1)} %reshape.356, f32[2048]{0:T(1024)S(1)} %select_multiply_fusion), kind=kOutput, calls=%fused_computation.33 | convolution fusion | flops 822476800 | bytes 18358272 | tf_op jit(solution)/shard_map/rck,xk->rcx/dot_general | solution.py:79
  145.5 8.5 %fusion.5 = bf16[4,24,2048]{2,1,0:T(8,128)(2,1)S(1)} fusion(f32[4,24,2048]{2,1,0:T(8,128)S(1)} %fusion.17, f32[2048,1024]{1,0:T(8,128)} %bitcast.77, f32[2048,1024]{1,0:T(8,128)} %bitcast.73, bf16[4,24,2048]{2,1,0:T(8,128)(2,1)S(1)} %copy-done.4, f32[4,24,2048]{2,1,0:T(8,128)S(1)} %reshape.356, f32[2048]{0:T(1024)S(1)} %select_multiply_fusion), kind=kOutput, calls=%fused_computation.15 | convolution fusion | flops 827457536 | bytes 19144704 | tf_op jit(solution)/shard_map/rck,xk->rcx/dot_general | solution.py:79
  154.0 1.1 copy.81
  155.1 4.9 %gather_fusion = bf16[320,24]{1,0:T(8,128)(2,1)S(1)} fusion(bf16[4,24,2048]{1,2,0:T(8,128)(2,1)S(1)} %copy.81, s32[320]{0:T(512)S(1)} %fusion.104), kind=kCustom, calls=%fused_computation | custom fusion | bytes 33280 | tf_op jit(solution)/shard_map/gather | solution.py:216
  160.1 0.6 broadcast_in_dim.21
  160.7 4.5 %all-to-all-start.2 = ((bf16[4,320,24]{1,2,0:T(8,128)(2,1)}), bf16[4,320,24]{1,2,0:T(8,128)(2,1)S(1)}, u32[]{:S(2)}, u32[]{:S(2)}) async-start(bf16[4,320,24]{1,2,0:T(8,128)(2,1)} %broadcast_in_dim.21), calls=%async_computation.2 | async-start | bytes 147456 | tf_op jit(solution)/shard_map/all_to_all | solution.py:217
  165.3 4.5 %all-to-all-done.2 = bf16[4,320,24]{1,2,0:T(8,128)(2,1)S(1)} async-done(((bf16[4,320,24]{1,2,0:T(8,128)(2,1)}), bf16[4,320,24]{1,2,0:T(8,128)(2,1)S(1)}, u32[]{:S(2)}, u32[]{:S(2)}) %all-to-all-start.2) | async-done | bytes 61472 | tf_op jit(solution)/shard_map/all_to_all | solution.py:217
  170.3 0.8 broadcast_in_dim.24
  171.1 6.5 %all-to-all-start.4 = ((bf16[64,17,128]{2,1,0:T(8,128)(2,1)}), bf16[64,17,128]{2,1,0:T(8,128)(2,1)S(1)}, u32[]{:S(2)}, u32[]{:S(2)}) async-start(bf16[64,17,128]{2,1,0:T(8,128)(2,1)} %broadcast_in_dim.24), calls=%async_computation.4 | async-start | bytes 786432 | tf_op jit(solution)/shard_map/all_to_all | solution.py:234
  177.9 16.4 %all-to-all-done.4 = bf16[64,17,128]{2,1,0:T(8,128)(2,1)S(1)} async-done(((bf16[64,17,128]{2,1,0:T(8,128)(2,1)}), bf16[64,17,128]{2,1,0:T(8,128)(2,1)S(1)}, u32[]{:S(2)}, u32[]{:S(2)}) %all-to-all-start.4) | async-done | bytes 278560 | tf_op jit(solution)/shard_map/all_to_all | solution.py:234
  195.2 16.8 %all_to_all.30 = f32[64,16,2]{1,2,0:T(2,128)S(1)} all-to-all(f32[64,16,2]{1,2,0:T(2,128)S(1)} %copy.83), channel_id=1, replica_groups=mesh['rows'=64,'ch'=4] {'rows'}, dimensions={0} | all-to-all | bytes 16384 | tf_op jit(solution)/shard_map/all_to_all | solution.py:251
  212.1 0.5 subtract_bitcast_fusion
  (62 shorter events, 4.6 us)
Async XLA Ops:
  1.7 10.3 %collective-permute-start = (bf16[2,24,2048]{2,1,0:T(8,128)(2,1)S(1)}, bf16[2,24,2048]{2,1,0:T(8,128)(2,1)S(1)}, u32[]{:S(2)}, u32[]{:S(2)}) collective-permute-start(bf16[2,24,2048]{2,1,0:T(8,128)(2,1)S(1)} %get-tuple-element.20), channel_id=1, source_target_pairs={{0,4},{4,8},{8,12},{12,16},{16,20},{20,24},{24,28},{28,32},{32,36}... | collective-permute-start | bytes 589832 | tf_op jit(solution)/shard_map/ppermute | solution.py:21
  6.2 7.0 %collective-permute-start.1 = (bf16[2,24,2048]{2,1,0:T(8,128)(2,1)S(1)}, bf16[2,24,2048]{2,1,0:T(8,128)(2,1)S(1)}, u32[]{:S(2)}, u32[]{:S(2)}) collective-permute-start(bf16[2,24,2048]{2,1,0:T(8,128)(2,1)S(1)} %get-tuple-element.21), channel_id=1, source_target_pairs={{4,0},{8,4},{12,8},{16,12},{20,16},{24,20},{28,24},{32,28},{36,32}... | collective-permute-start | bytes 589832 | tf_op jit(solution)/shard_map/ppermute | solution.py:23
  16.8 14.9 %collective-permute-start.2 = (bf16[4,24,2048]{2,1,0:T(8,128)(2,1)S(1)}, bf16[4,24,2048]{2,1,0:T(8,128)(2,1)S(1)}, u32[]{:S(2)}, u32[]{:S(2)}) collective-permute-start(bf16[4,24,2048]{2,1,0:T(8,128)(2,1)S(1)} %fusion.39), channel_id=1, source_target_pairs={{0,1},{1,2},{2,3},{3,0},{4,5},{5,6},{6,7},{7,4},{8,9},{9,10},{10,1... | collective-permute-start | bytes 1179656 | tf_op jit(solution)/shard_map/ppermute | solution.py:35
  18.5 28.9 %collective-permute-start.3 = (bf16[4,24,2048]{2,1,0:T(8,128)(2,1)S(1)}, bf16[4,24,2048]{2,1,0:T(8,128)(2,1)S(1)}, u32[]{:S(2)}, u32[]{:S(2)}) collective-permute-start(bf16[4,24,2048]{2,1,0:T(8,128)(2,1)S(1)} %fusion.39), channel_id=1, source_target_pairs={{0,2},{1,3},{2,0},{3,1},{4,6},{5,7},{6,4},{7,5},{8,10},{9,11},{10,... | collective-permute-start | bytes 1179656 | tf_op jit(solution)/shard_map/ppermute | solution.py:35
  21.5 25.9 %collective-permute-start.4 = (bf16[4,24,2048]{2,1,0:T(8,128)(2,1)S(1)}, bf16[4,24,2048]{2,1,0:T(8,128)(2,1)S(1)}, u32[]{:S(2)}, u32[]{:S(2)}) collective-permute-start(bf16[4,24,2048]{2,1,0:T(8,128)(2,1)S(1)} %fusion.39), channel_id=1, source_target_pairs={{0,3},{1,0},{2,1},{3,2},{4,7},{5,4},{6,5},{7,6},{8,11},{9,8},{10,9... | collective-permute-start | bytes 1179656 | tf_op jit(solution)/shard_map/ppermute | solution.py:35
  24.7 24.7 %copy-start = (f32[32,64,1024]{2,1,0:T(8,128)}, f32[32,64,1024]{2,1,0:T(8,128)S(1)}, u32[]{:S(2)}) copy-start(f32[32,64,1024]{2,1,0:T(8,128)S(1)} %get-tuple-element.18) | copy-start | bytes 25165828
  24.7 24.7 %copy-start.1 = (f32[32,64,1024]{2,1,0:T(8,128)}, f32[32,64,1024]{2,1,0:T(8,128)S(1)}, u32[]{:S(2)}) copy-start(f32[32,64,1024]{2,1,0:T(8,128)S(1)} %get-tuple-element.19) | copy-start | bytes 25165828
  47.9 1.5 copy-start.3
  57.9 28.5 %all-to-all-start = ((bf16[2,64,4,384]{3,2,0,1:T(4,128)(2,1)}), bf16[2,64,4,384]{3,2,0,1:T(4,128)(2,1)S(1)}, u32[]{:S(2)}, u32[]{:S(2)}) async-start(bf16[2,64,4,384]{3,2,0,1:T(4,128)(2,1)} %copy.72), calls=%async_computation | async-start | bytes 786432 | tf_op jit(solution)/shard_map/all_to_all | solution.py:172
  73.6 21.4 %copy-start.7 = (s32[256]{0:T(256)S(1)}, s32[256]{0:T(256)}, u32[]{:S(2)}) copy-start(s32[256]{0:T(256)} %param.18) | copy-start | bytes 3076
  73.6 21.4 %copy-start.8 = (s32[64]{0:T(128)S(1)}, s32[64]{0:T(128)}, u32[]{:S(2)}) copy-start(s32[64]{0:T(128)} %param.17) | copy-start | bytes 772
  73.6 21.5 %copy-start.9 = (s32[64]{0:T(128)S(1)}, s32[64]{0:T(128)}, u32[]{:S(2)}) copy-start(s32[64]{0:T(128)} %param.19) | copy-start | bytes 772
  73.6 21.5 %copy-start.5 = (bf16[24,128]{1,0:T(8,128)(2,1)S(1)}, bf16[24,128]{1,0:T(8,128)(2,1)}, u32[]{:S(2)}) copy-start(bf16[24,128]{1,0:T(8,128)(2,1)} %param.15) | copy-start | bytes 18436
  73.6 21.5 %copy-start.6 = (bf16[24,128]{1,0:T(8,128)(2,1)S(1)}, bf16[24,128]{1,0:T(8,128)(2,1)}, u32[]{:S(2)}) copy-start(bf16[24,128]{1,0:T(8,128)(2,1)} %param.16) | copy-start | bytes 18436
  90.4 19.5 %all-to-all-start.1 = ((bf16[2,64,4,384]{3,2,0,1:T(4,128)(2,1)}), bf16[2,64,4,384]{3,2,0,1:T(4,128)(2,1)S(1)}, u32[]{:S(2)}, u32[]{:S(2)}) async-start(bf16[2,64,4,384]{3,2,0,1:T(4,128)(2,1)} %copy.78), calls=%async_computation.1 | async-start | bytes 786432 | tf_op jit(solution)/shard_map/all_to_all | solution.py:197
  110.5 49.6 %all-to-all-start.3 = ((bf16[4,24,256]{2,1,0:T(8,128)(2,1)}), bf16[4,24,256]{2,1,0:T(8,128)(2,1)S(1)}, u32[]{:S(2)}, u32[]{:S(2)}) async-start(bf16[4,24,256]{2,1,0:T(8,128)(2,1)} %broadcast_in_dim.22), calls=%async_computation.3 | async-start | bytes 98304 | tf_op jit(solution)/shard_map/all_to_all | solution.py:211
  138.1 7.4 %copy-start.4 = (bf16[4,24,2048]{2,1,0:T(8,128)(2,1)S(1)}, bf16[4,24,2048]{2,1,0:T(8,128)(2,1)}, u32[]{:S(2)}) copy-start(bf16[4,24,2048]{2,1,0:T(8,128)(2,1)} %copy-done.3) | copy-start | bytes 1179652
  154.0 58.6 %copy-start.2 = (bf16[4,24,2048]{2,1,0:T(8,128)(2,1)}, bf16[4,24,2048]{2,1,0:T(8,128)(2,1)S(1)}, u32[]{:S(2)}) copy-start(bf16[4,24,2048]{2,1,0:T(8,128)(2,1)S(1)} %fusion.5) | copy-start | bytes 1179652
  160.7 9.2 %all-to-all-start.2 = ((bf16[4,320,24]{1,2,0:T(8,128)(2,1)}), bf16[4,320,24]{1,2,0:T(8,128)(2,1)S(1)}, u32[]{:S(2)}, u32[]{:S(2)}) async-start(bf16[4,320,24]{1,2,0:T(8,128)(2,1)} %broadcast_in_dim.21), calls=%async_computation.2 | async-start | bytes 147456 | tf_op jit(solution)/shard_map/all_to_all | solution.py:217
  171.1 23.2 %all-to-all-start.4 = ((bf16[64,17,128]{2,1,0:T(8,128)(2,1)}), bf16[64,17,128]{2,1,0:T(8,128)(2,1)S(1)}, u32[]{:S(2)}, u32[]{:S(2)}) async-start(bf16[64,17,128]{2,1,0:T(8,128)(2,1)} %broadcast_in_dim.24), calls=%async_computation.4 | async-start | bytes 786432 | tf_op jit(solution)/shard_map/all_to_all | solution.py:234
where the time goes:
time: 213 us
  waiting for transfers between devices  70 us (33%)
  starting transfers between devices  57.8 us (27%)
  local copies, waits for them, and re-layouts  31 us (15%)
  matrix products  23.1 us (11%)
  blocking collectives  16.8 us (8%)
  other arithmetic  12.7 us (6%)
    ppermute x3, waiting for transfers between devices, ring_pieces(): lax.ppermute(values, axis, [(i, (i + shift) % count) for i in range(count)])  22.7 us
    dot_general x4, matrix products, two_pass(): jnp.einsum(eq, left, part, preferred_element_type=jnp.float32)  18.8 us
    all_to_all x1, blocking collectives, body(): lax.all_to_all(jnp.stack([exp_sums, picked], axis=1).reshape(slabs, quart...  16.8 us
    all_to_all x1, starting transfers between devices, body(): lax.all_to_all(jnp.broadcast_to(weights_all[None], (group_count,) + weigh...  16.7 us
    all_to_all x1, waiting for transfers between devices, body(): lax.all_to_all(jnp.broadcast_to(packet[None], (slabs,) + packet.shape), '...  16.4 us
    all_to_all x1, waiting for transfers between devices, body(): lax.all_to_all(back.reshape(2, slabs, slab_rows, lanes), 'rows', split_ax...  14.6 us
    all_to_all x1, starting transfers between devices, body(): lax.all_to_all(wire.astype(jnp.bfloat16), 'rows', split_axis=1, concat_ax...  13.6 us
    all_to_all x1, waiting for transfers between devices, body(): lax.all_to_all(wire.astype(jnp.bfloat16), 'rows', split_axis=1, concat_ax...  10.6 us
  transfers between devices with their start and end apart: 10, of which 7 were waited for; matrix products, arithmetic and copies ran while one was open for 21% of the time, Pallas kernels for 0%

commit v1 on v0

--- a/solution.py
+++ b/solution.py
@@ -200,18 +200,16 @@
     rows_both = jnp.transpose(rows_both, (2, 3, 0, 1, 4)).reshape(slab_rows, groups, columns)
     doubling = jnp.where(lax.broadcasted_iota(jnp.int32, (1, 1, columns), 2) % half_cols == 0, 1.0, 2.0)
     weighting = doubling * (1.0 / columns)
-    row_both = (rows_both.astype(jnp.float32) * weighting).astype(jnp.bfloat16)
+    row_both = lax.optimization_barrier(rows_both * weighting.astype(jnp.bfloat16))
     spatial = two_pass("rck,xk->rcx", row_both, table_pair)
     encoded = (hidden.astype(jnp.float32) + spatial).astype(jnp.bfloat16)
     key_count = key_pixels.shape[0]
     query_count = query_pixels.shape[0]
     quarter = query_count // group_count
     slab = lax.axis_index("rows")
-    weights_all = jnp.concatenate([key_weight, query_weight], axis=1)
-    weights_all = lax.all_to_all(
-        jnp.broadcast_to(weights_all[None], (group_count,) + weights_all.shape),
-        "ch", split_axis=0, concat_axis=0, tiled=True,
-    ).reshape(group_count * groups, -1)
+    weight_pieces = jnp.stack(ring_pieces(jnp.concatenate([key_weight, query_weight], axis=1), "ch"))
+    owners = (channel - jnp.arange(group_count)) % group_count
+    weights_all = jnp.take(weight_pieces, owners, axis=0).reshape(group_count * groups, -1)
     sampled = jnp.concatenate([key_pixels, query_pixels])
     features = encoded[sampled // columns, :, sampled % columns]
     features = lax.all_to_all(

time: 213 us -> 208 us (0.977)
  starting transfers between devices: 57.8 us -> 55 us
  matrix products: 23.1 us -> 20.7 us
    all_to_all x1 -> x0, starting transfers between devices: 16.7 us -> none  [body(): lax.all_to_all(jnp.broadcast_to(weights_all[None], (group_count,) + weigh...]
    all_to_all x1, starting transfers between devices: 4.53 us -> 16.3 us  [body(): lax.all_to_all(jnp.broadcast_to(features[None], (group_count,) + features...]
    convert_element_type x2 -> x0, local copies, waits for them, and re-layouts: 10.4 us -> none  [body(): row_both = (rows_both.astype(jnp.float32) * weighting).astype(jnp.bfloat16)]
    reshape x0 -> x1, local copies, waits for them, and re-layouts: none -> 6.43 us  [body(): jnp.transpose(rows_both, (2, 3, 0, 1, 4))]
    ppermute x3 -> x6, starting transfers between devices: 5.43 us -> 8.79 us  [ring_pieces(): lax.ppermute(values, axis, [(i, (i + shift) % count) for i in range(count)])]
    transpose x0 -> x1, local copies, waits for them, and re-layouts: none -> 2.79 us  [body(): jnp.transpose(rows_both, (2, 3, 0, 1, 4))]
    dot_general x4, matrix products: 18.8 us -> 16.4 us  [two_pass(): jnp.einsum(eq, left, part, preferred_element_type=jnp.float32)]
    ppermute x3 -> x6, waiting for transfers between devices: 22.7 us -> 23.1 us  [ring_pieces(): lax.ppermute(values, axis, [(i, (i + shift) % count) for i in range(count)])]
  transfers between devices with their start and end apart: 10 -> 12, of which waited for: 7 -> 7; matrix products, arithmetic and copies ran while one was open for 21% -> 15% of each run, Pallas kernels for 0% -> 0%
where the time goes in v1:
time: 208 us; the launch traced here: 207 us
  waiting for transfers between devices  68.8 us (33%)
  starting transfers between devices  55 us (26%)
  local copies, waits for them, and re-layouts  31.4 us (15%)
  matrix products  20.7 us (10%)
  blocking collectives  16.8 us (8%)
  other arithmetic  13.5 us (6%)
    ppermute x6, waiting for transfers between devices, ring_pieces(): lax.ppermute(values, axis, [(i, (i + shift) % count) for i in range(count)])  23.1 us
    all_to_all x1, blocking collectives, body(): lax.all_to_all(jnp.stack([exp_sums, picked], axis=1).reshape(slabs, quart...  16.8 us
    dot_general x4, matrix products, two_pass(): jnp.einsum(eq, left, part, preferred_element_type=jnp.float32)  16.4 us
    all_to_all x1, waiting for transfers between devices, body(): lax.all_to_all(jnp.broadcast_to(packet[None], (slabs,) + packet.shape), '...  16.4 us
    all_to_all x1, starting transfers between devices, body(): lax.all_to_all(jnp.broadcast_to(features[None], (group_count,) + features...  16.3 us
    all_to_all x1, starting transfers between devices, body(): lax.all_to_all(wire.astype(jnp.bfloat16), 'rows', split_axis=1, concat_ax...  13.2 us
    all_to_all x1, waiting for transfers between devices, body(): lax.all_to_all(back.reshape(2, slabs, slab_rows, lanes), 'rows', split_ax...  13.2 us
    all_to_all x1, waiting for transfers between devices, body(): lax.all_to_all(wire.astype(jnp.bfloat16), 'rows', split_axis=1, concat_ax...  10.5 us
  transfers between devices with their start and end apart: 12, of which 7 were waited for; matrix products, arithmetic and copies ran while one was open for 15% of the time, Pallas kernels for 0%

profile of v1, /device:TPU:1, one launch (start us, length us, event | category | flops | bytes accessed | tf_op | source)
XLA Modules:
  0.0 207.4 jit_solution(9686128568229019561)
XLA Ops:
  0.6 0.7 constant_dynamic-update-slice_fusion.1
  1.3 0.7 constant_dynamic-update-slice_fusion
  2.0 2.5 %collective-permute-start.5 = (bf16[24,256]{1,0:T(8,128)(2,1)S(1)}, bf16[24,256]{1,0:T(8,128)(2,1)}, u32[]{:S(2)}, u32[]{:S(2)}) collective-permute-start(bf16[24,256]{1,0:T(8,128)(2,1)S(1)} %constant_dynamic-update-slice_fusion), channel_id=1, source_target_pairs={{0,1},{1,2},{2,3},{3,0},{4,5},{5,6},{6,7},{7,4},{8,9},{9,10},{10,1... | collective-permute-start | bytes 36872 | tf_op jit(solution)/shard_map/ppermute | solution.py:35
  4.5 3.0 %collective-permute-start.6 = (bf16[24,256]{1,0:T(8,128)(2,1)S(1)}, bf16[24,256]{1,0:T(8,128)(2,1)}, u32[]{:S(2)}, u32[]{:S(2)}) collective-permute-start(bf16[24,256]{1,0:T(8,128)(2,1)S(1)} %constant_dynamic-update-slice_fusion), channel_id=1, source_target_pairs={{0,2},{1,3},{2,0},{3,1},{4,6},{5,7},{6,4},{7,5},{8,10},{9,11},{10,... | collective-permute-start | bytes 36872 | tf_op jit(solution)/shard_map/ppermute | solution.py:35
  7.5 1.0 fusion.121
  8.5 4.2 %collective-permute-start = (bf16[2,24,2048]{2,1,0:T(8,128)(2,1)S(1)}, bf16[2,24,2048]{2,1,0:T(8,128)(2,1)S(1)}, u32[]{:S(2)}, u32[]{:S(2)}) collective-permute-start(bf16[2,24,2048]{2,1,0:T(8,128)(2,1)S(1)} %get-tuple-element.20), channel_id=1, source_target_pairs={{0,4},{4,8},{8,12},{12,16},{16,20},{20,24},{24,28},{28,32},{32,36}... | collective-permute-start | bytes 589832 | tf_op jit(solution)/shard_map/ppermute | solution.py:21
  12.8 1.9 collective-permute-start.1
  14.7 1.0 fusion.76
  16.4 0.9 fusion.122
  17.6 1.0 slice_bitcast_fusion.8
  18.6 1.2 collective-permute-done.1
  19.8 1.3 fusion.30
  21.1 2.3 %fusion.39 = bf16[4,24,2048]{2,1,0:T(8,128)(2,1)S(1)} fusion(bf16[4,24,2048]{2,1,0:T(8,128)(2,1)} %param.10, bf16[8,24,2052]{2,1,0:T(8,128)(2,1)S(1)} %fusion.30, bf16[2,24,2048]{2,1,0:T(8,128)(2,1)S(1)} %collective-permute-done.1, bf16[2,24,2048]{2,1,0:T(8,128)(2,1)S(1)} %collective-permute-done, f32[24]{0:T(128)S(1)} %get-tuple-element.33, ...), kind=kLoop, calls=%fused_computation.58 | loop fusion | flops 5898240 | bytes 3539808 | tf_op jit(solution)/shard_map/convert_element_type | solution.py:147
  23.4 1.0 collective-permute-start.3
  24.4 2.3 %collective-permute-start.4 = (bf16[4,24,2048]{2,1,0:T(8,128)(2,1)S(1)}, bf16[4,24,2048]{2,1,0:T(8,128)(2,1)S(1)}, u32[]{:S(2)}, u32[]{:S(2)}) collective-permute-start(bf16[4,24,2048]{2,1,0:T(8,128)(2,1)S(1)} %fusion.39), channel_id=1, source_target_pairs={{0,3},{1,0},{2,1},{3,2},{4,7},{5,4},{6,5},{7,6},{8,11},{9,8},{10,9... | collective-permute-start | bytes 1179656 | tf_op jit(solution)/shard_map/ppermute | solution.py:35
  26.7 2.5 %multiply_subtract_fusion = (f32[32,64,1024]{2,1,0:T(8,128)S(1)}, f32[32,64,1024]{2,1,0:T(8,128)S(1)}) fusion(f32[64,1024]{1,0:T(8,128)S(1)} %get-tuple-element.11, f32[32,1024]{1,0:T(8,128)S(1)} %get-tuple-element.10, f32[64,1024]{1,0:T(8,128)S(1)} %get-tuple-element.9, f32[32,1024]{1,0:T(8,128)S(1)} %get-tuple-element.8), kind=kLoop, calls=%fused_computation.8 | loop fusion | flops 14680064 | bytes 17563648 | tf_op jit(solution)/shard_map/sub | solution.py:71
  29.2 7.1 %collective-permute-done.2 = bf16[4,24,2048]{2,1,0:T(8,128)(2,1)S(1)} collective-permute-done((bf16[4,24,2048]{2,1,0:T(8,128)(2,1)S(1)}, bf16[4,24,2048]{2,1,0:T(8,128)(2,1)S(1)}, u32[]{:S(2)}, u32[]{:S(2)}) %collective-permute-start.2) | collective-permute-done | bytes 393248 | tf_op jit(solution)/shard_map/ppermute | solution.py:35
  36.3 16.0 %collective-permute-done.3 = bf16[4,24,2048]{2,1,0:T(8,128)(2,1)S(1)} collective-permute-done((bf16[4,24,2048]{2,1,0:T(8,128)(2,1)S(1)}, bf16[4,24,2048]{2,1,0:T(8,128)(2,1)S(1)}, u32[]{:S(2)}, u32[]{:S(2)}) %collective-permute-start.3) | collective-permute-done | bytes 393248 | tf_op jit(solution)/shard_map/ppermute | solution.py:35
  52.7 1.5 fusion.19
  54.3 1.5 fusion.4
  55.8 2.5 %convert_element_type.147 = bf16[4,24,2,64,16]{4,3,2,1,0:T(8,128)(2,1)S(1)} reshape(bf16[4,24,2048]{2,1,0:T(8,128)(2,1)S(1)} %fusion.4) | data formatting | bytes 786432 | tf_op jit(solution)/shard_map/convert_element_type | solution.py:173
  58.3 2.3 %copy.71 = bf16[2,64,4,24,16]{1,4,3,2,0:T(8,128)(2,1)} copy(bf16[2,64,4,24,16]{4,1,0,3,2:T(8,128)(2,1)S(1)} %bitcast.88) | data formatting | bytes 786432 | tf_op jit(solution)/shard_map/convert_element_type | solution.py:173
  60.6 2.2 %copy.72 = bf16[2,64,4,384]{3,2,0,1:T(4,128)(2,1)} copy(bf16[2,64,4,384]{1,3,2,0:T(8,128)(2,1)} %bitcast.89) | data formatting | bytes 786432 | tf_op jit(solution)/shard_map/convert_element_type | solution.py:173
  62.8 13.2 %all-to-all-start = ((bf16[2,64,4,384]{3,2,0,1:T(4,128)(2,1)}), bf16[2,64,4,384]{3,2,0,1:T(4,128)(2,1)S(1)}, u32[]{:S(2)}, u32[]{:S(2)}) async-start(bf16[2,64,4,384]{3,2,0,1:T(4,128)(2,1)} %copy.72), calls=%async_computation | async-start | bytes 786432 | tf_op jit(solution)/shard_map/all_to_all | solution.py:172
  76.0 1.0 bitcast_convert_fusion
  77.2 1.0 bitcast_convert_fusion.1
  78.4 1.0 fusion.75
  79.4 1.0 broadcast_multiply_fusion.1
  80.4 10.5 %all-to-all-done = bf16[2,64,4,384]{3,2,0,1:T(4,128)(2,1)S(1)} async-done(((bf16[2,64,4,384]{3,2,0,1:T(4,128)(2,1)}), bf16[2,64,4,384]{3,2,0,1:T(4,128)(2,1)S(1)}, u32[]{:S(2)}, u32[]{:S(2)}) %all-to-all-start) | async-done | bytes 393248 | tf_op jit(solution)/shard_map/all_to_all | solution.py:172
  92.1 1.8 fusion.14
  94.0 0.9 copy.78
  94.9 4.6 %all-to-all-start.1 = ((bf16[2,64,4,384]{3,2,0,1:T(4,128)(2,1)}), bf16[2,64,4,384]{3,2,0,1:T(4,128)(2,1)S(1)}, u32[]{:S(2)}, u32[]{:S(2)}) async-start(bf16[2,64,4,384]{3,2,0,1:T(4,128)(2,1)} %copy.78), calls=%async_computation.1 | async-start | bytes 786432 | tf_op jit(solution)/shard_map/all_to_all | solution.py:197
  99.9 0.8 pad_maximum_fusion.9
  100.7 0.5 gather_fusion.1
  101.2 13.2 %all-to-all-done.1 = bf16[2,64,4,384]{3,2,0,1:T(4,128)(2,1)S(1)} async-done(((bf16[2,64,4,384]{3,2,0,1:T(4,128)(2,1)}), bf16[2,64,4,384]{3,2,0,1:T(4,128)(2,1)S(1)}, u32[]{:S(2)}, u32[]{:S(2)}) %all-to-all-start.1) | async-done | bytes 393248 | tf_op jit(solution)/shard_map/all_to_all | solution.py:197
  114.9 2.8 %copy.80 = bf16[4,24,2,64,16]{4,3,2,1,0:T(8,128)(2,1)} copy(bf16[4,24,2,64,16]{3,4,1,0,2:T(8,128)(2,1)S(1)} %bitcast.90) | data formatting | bytes 786432 | tf_op jit(solution)/shard_map/transpose | solution.py:200
  117.6 6.4 %reshape.405 = bf16[4,24,2048]{2,1,0:T(8,128)(2,1)S(1)} reshape(bf16[4,24,2,64,16]{4,3,2,1,0:T(8,128)(2,1)} %copy.80) | data formatting | bytes 786432 | tf_op jit(solution)/shard_map/reshape | solution.py:200
  124.2 8.3 %fusion.17 = f32[4,24,2048]{2,1,0:T(8,128)S(1)} fusion(bf16[4,24,2048]{2,1,0:T(8,128)(2,1)S(1)} %broadcast_multiply_fusion, f32[2048,1024]{1,0:T(8,128)} %bitcast.86, f32[2048,1024]{1,0:T(8,128)} %bitcast.80), kind=kOutput, calls=%fused_computation.33 | convolution fusion | flops 822083584 | bytes 17956864 | tf_op jit(solution)/shard_map/rck,xk->rcx/dot_general | solution.py:79
  132.5 5.1 %fusion.5 = bf16[4,24,2048]{2,1,0:T(8,128)(2,1)S(1)} fusion(f32[4,24,2048]{2,1,0:T(8,128)S(1)} %fusion.17, bf16[4,24,2048]{2,1,0:T(8,128)(2,1)S(1)} %broadcast_multiply_fusion, f32[2048,1024]{1,0:T(8,128)} %bitcast.87, f32[2048,1024]{1,0:T(8,128)S(1)} %bitcast.83, bf16[4,24,2048]{2,1,0:T(8,128)(2,1)S(1)} %copy-done.4), kind=kOutput, calls=%fused_computation.16 | convolution fusion | flops 827064320 | bytes 18743296 | tf_op jit(solution)/shard_map/rck,xk->rcx/dot_general | solution.py:79
  137.7 1.0 copy.81
  138.7 4.9 %gather_fusion = bf16[320,24]{1,0:T(8,128)(2,1)S(1)} fusion(bf16[4,24,2048]{1,2,0:T(8,128)(2,1)S(1)} %copy.81, s32[320]{0:T(512)S(1)} %fusion.104), kind=kCustom, calls=%fused_computation | custom fusion | bytes 33280 | tf_op jit(solution)/shard_map/gather | solution.py:214
  143.6 0.7 broadcast_in_dim.55
  144.3 16.3 %all-to-all-start.2 = ((bf16[4,320,24]{1,2,0:T(8,128)(2,1)}), bf16[4,320,24]{1,2,0:T(8,128)(2,1)S(1)}, u32[]{:S(2)}, u32[]{:S(2)}) async-start(bf16[4,320,24]{1,2,0:T(8,128)(2,1)} %broadcast_in_dim.55), calls=%async_computation.2 | async-start | bytes 147456 | tf_op jit(solution)/shard_map/all_to_all | solution.py:215
  160.7 4.5 %all-to-all-done.2 = bf16[4,320,24]{1,2,0:T(8,128)(2,1)S(1)} async-done(((bf16[4,320,24]{1,2,0:T(8,128)(2,1)}), bf16[4,320,24]{1,2,0:T(8,128)(2,1)S(1)}, u32[]{:S(2)}, u32[]{:S(2)}) %all-to-all-start.2) | async-done | bytes 61472 | tf_op jit(solution)/shard_map/all_to_all | solution.py:215
  165.7 0.8 broadcast_in_dim.61
  166.5 5.9 %all-to-all-start.3 = ((bf16[64,17,128]{2,1,0:T(8,128)(2,1)}), bf16[64,17,128]{2,1,0:T(8,128)(2,1)S(1)}, u32[]{:S(2)}, u32[]{:S(2)}) async-start(bf16[64,17,128]{2,1,0:T(8,128)(2,1)} %broadcast_in_dim.61), calls=%async_computation.3 | async-start | bytes 786432 | tf_op jit(solution)/shard_map/all_to_all | solution.py:232
  172.7 16.4 %all-to-all-done.3 = bf16[64,17,128]{2,1,0:T(8,128)(2,1)S(1)} async-done(((bf16[64,17,128]{2,1,0:T(8,128)(2,1)}), bf16[64,17,128]{2,1,0:T(8,128)(2,1)S(1)}, u32[]{:S(2)}, u32[]{:S(2)}) %all-to-all-start.3) | async-done | bytes 278560 | tf_op jit(solution)/shard_map/all_to_all | solution.py:232
  190.0 16.8 %all_to_all.25 = f32[64,16,2]{1,2,0:T(2,128)S(1)} all-to-all(f32[64,16,2]{1,2,0:T(2,128)S(1)} %copy.83), channel_id=1, replica_groups=mesh['rows'=64,'ch'=4] {'rows'}, dimensions={0} | all-to-all | bytes 16384 | tf_op jit(solution)/shard_map/all_to_all | solution.py:249
  (75 shorter events, 6.4 us)
Async XLA Ops:
  2.0 97.9 %collective-permute-start.5 = (bf16[24,256]{1,0:T(8,128)(2,1)S(1)}, bf16[24,256]{1,0:T(8,128)(2,1)}, u32[]{:S(2)}, u32[]{:S(2)}) collective-permute-start(bf16[24,256]{1,0:T(8,128)(2,1)S(1)} %constant_dynamic-update-slice_fusion), channel_id=1, source_target_pairs={{0,1},{1,2},{2,3},{3,0},{4,5},{5,6},{6,7},{7,4},{8,9},{9,10},{10,1... | collective-permute-start | bytes 36872 | tf_op jit(solution)/shard_map/ppermute | solution.py:35
  4.5 95.4 %collective-permute-start.6 = (bf16[24,256]{1,0:T(8,128)(2,1)S(1)}, bf16[24,256]{1,0:T(8,128)(2,1)}, u32[]{:S(2)}, u32[]{:S(2)}) collective-permute-start(bf16[24,256]{1,0:T(8,128)(2,1)S(1)} %constant_dynamic-update-slice_fusion), channel_id=1, source_target_pairs={{0,2},{1,3},{2,0},{3,1},{4,6},{5,7},{6,4},{7,5},{8,10},{9,11},{10,... | collective-permute-start | bytes 36872 | tf_op jit(solution)/shard_map/ppermute | solution.py:35
  8.5 10.0 %collective-permute-start = (bf16[2,24,2048]{2,1,0:T(8,128)(2,1)S(1)}, bf16[2,24,2048]{2,1,0:T(8,128)(2,1)S(1)}, u32[]{:S(2)}, u32[]{:S(2)}) collective-permute-start(bf16[2,24,2048]{2,1,0:T(8,128)(2,1)S(1)} %get-tuple-element.20), channel_id=1, source_target_pairs={{0,4},{4,8},{8,12},{12,16},{16,20},{20,24},{24,28},{28,32},{32,36}... | collective-permute-start | bytes 589832 | tf_op jit(solution)/shard_map/ppermute | solution.py:21
  12.8 7.0 %collective-permute-start.1 = (bf16[2,24,2048]{2,1,0:T(8,128)(2,1)S(1)}, bf16[2,24,2048]{2,1,0:T(8,128)(2,1)S(1)}, u32[]{:S(2)}, u32[]{:S(2)}) collective-permute-start(bf16[2,24,2048]{2,1,0:T(8,128)(2,1)S(1)} %get-tuple-element.21), channel_id=1, source_target_pairs={{4,0},{8,4},{12,8},{16,12},{20,16},{24,20},{28,24},{32,28},{36,32}... | collective-permute-start | bytes 589832 | tf_op jit(solution)/shard_map/ppermute | solution.py:23
  23.3 12.9 %collective-permute-start.2 = (bf16[4,24,2048]{2,1,0:T(8,128)(2,1)S(1)}, bf16[4,24,2048]{2,1,0:T(8,128)(2,1)S(1)}, u32[]{:S(2)}, u32[]{:S(2)}) collective-permute-start(bf16[4,24,2048]{2,1,0:T(8,128)(2,1)S(1)} %fusion.39), channel_id=1, source_target_pairs={{0,1},{1,2},{2,3},{3,0},{4,5},{5,6},{6,7},{7,4},{8,9},{9,10},{10,1... | collective-permute-start | bytes 1179656 | tf_op jit(solution)/shard_map/ppermute | solution.py:35
  23.4 28.8 %collective-permute-start.3 = (bf16[4,24,2048]{2,1,0:T(8,128)(2,1)S(1)}, bf16[4,24,2048]{2,1,0:T(8,128)(2,1)S(1)}, u32[]{:S(2)}, u32[]{:S(2)}) collective-permute-start(bf16[4,24,2048]{2,1,0:T(8,128)(2,1)S(1)} %fusion.39), channel_id=1, source_target_pairs={{0,2},{1,3},{2,0},{3,1},{4,6},{5,7},{6,4},{7,5},{8,10},{9,11},{10,... | collective-permute-start | bytes 1179656 | tf_op jit(solution)/shard_map/ppermute | solution.py:35
  24.4 27.8 %collective-permute-start.4 = (bf16[4,24,2048]{2,1,0:T(8,128)(2,1)S(1)}, bf16[4,24,2048]{2,1,0:T(8,128)(2,1)S(1)}, u32[]{:S(2)}, u32[]{:S(2)}) collective-permute-start(bf16[4,24,2048]{2,1,0:T(8,128)(2,1)S(1)} %fusion.39), channel_id=1, source_target_pairs={{0,3},{1,0},{2,1},{3,2},{4,7},{5,4},{6,5},{7,6},{8,11},{9,8},{10,9... | collective-permute-start | bytes 1179656 | tf_op jit(solution)/shard_map/ppermute | solution.py:35
  29.1 25.1 %copy-start = (f32[32,64,1024]{2,1,0:T(8,128)}, f32[32,64,1024]{2,1,0:T(8,128)S(1)}, u32[]{:S(2)}) copy-start(f32[32,64,1024]{2,1,0:T(8,128)S(1)} %get-tuple-element.18) | copy-start | bytes 25165828
  29.2 25.1 %copy-start.1 = (f32[32,64,1024]{2,1,0:T(8,128)}, f32[32,64,1024]{2,1,0:T(8,128)S(1)}, u32[]{:S(2)}) copy-start(f32[32,64,1024]{2,1,0:T(8,128)S(1)} %get-tuple-element.19) | copy-start | bytes 25165828
  36.3 63.7 %collective-permute-start.7 = (bf16[24,256]{1,0:T(8,128)(2,1)S(1)}, bf16[24,256]{1,0:T(8,128)(2,1)}, u32[]{:S(2)}, u32[]{:S(2)}) collective-permute-start(bf16[24,256]{1,0:T(8,128)(2,1)S(1)} %constant_dynamic-update-slice_fusion), channel_id=1, source_target_pairs={{0,3},{1,0},{2,1},{3,2},{4,7},{5,4},{6,5},{7,6},{8,11},{9,8},{10,9... | collective-permute-start | bytes 36872 | tf_op jit(solution)/shard_map/ppermute | solution.py:35
  52.7 1.5 copy-start.3
  55.8 22.6 %copy-start.7 = (s32[64]{0:T(128)S(1)}, s32[64]{0:T(128)}, u32[]{:S(2)}) copy-start(s32[64]{0:T(128)} %param.19) | copy-start | bytes 772
  62.8 28.1 %all-to-all-start = ((bf16[2,64,4,384]{3,2,0,1:T(4,128)(2,1)}), bf16[2,64,4,384]{3,2,0,1:T(4,128)(2,1)S(1)}, u32[]{:S(2)}, u32[]{:S(2)}) async-start(bf16[2,64,4,384]{3,2,0,1:T(4,128)(2,1)} %copy.72), calls=%async_computation | async-start | bytes 786432 | tf_op jit(solution)/shard_map/all_to_all | solution.py:172
  78.1 21.7 %copy-start.5 = (s32[256]{0:T(256)S(1)}, s32[256]{0:T(256)}, u32[]{:S(2)}) copy-start(s32[256]{0:T(256)} %param.18) | copy-start | bytes 3076
  78.1 21.7 %copy-start.6 = (s32[64]{0:T(128)S(1)}, s32[64]{0:T(128)}, u32[]{:S(2)}) copy-start(s32[64]{0:T(128)} %param.17) | copy-start | bytes 772
  94.9 19.5 %all-to-all-start.1 = ((bf16[2,64,4,384]{3,2,0,1:T(4,128)(2,1)}), bf16[2,64,4,384]{3,2,0,1:T(4,128)(2,1)S(1)}, u32[]{:S(2)}, u32[]{:S(2)}) async-start(bf16[2,64,4,384]{3,2,0,1:T(4,128)(2,1)} %copy.78), calls=%async_computation.1 | async-start | bytes 786432 | tf_op jit(solution)/shard_map/all_to_all | solution.py:197
  124.1 8.4 %slice-start = ((s8[8388608]{0:T(1024)(128)(4,1)}), s8[4194304]{0:T(1024)(128)(4,1)S(1)}, s32[]{:S(2)}) async-start(s8[8388608]{0:T(1024)(128)(4,1)} %bitcast.81), calls=%async_computation.5 | async-start | bytes 8388608
  124.1 8.4 %slice-start.1 = ((s8[8388608]{0:T(1024)(128)(4,1)}), s8[4194304]{0:T(1024)(128)(4,1)S(1)}, s32[]{:S(2)}) async-start(s8[8388608]{0:T(1024)(128)(4,1)} %bitcast.81), calls=%async_computation.6 | async-start | bytes 8388608
  124.1 8.4 %copy-start.4 = (bf16[4,24,2048]{2,1,0:T(8,128)(2,1)S(1)}, bf16[4,24,2048]{2,1,0:T(8,128)(2,1)}, u32[]{:S(2)}) copy-start(bf16[4,24,2048]{2,1,0:T(8,128)(2,1)} %copy-done.3) | copy-start | bytes 1179652
  137.6 69.7 %copy-start.2 = (bf16[4,24,2048]{2,1,0:T(8,128)(2,1)}, bf16[4,24,2048]{2,1,0:T(8,128)(2,1)S(1)}, u32[]{:S(2)}) copy-start(bf16[4,24,2048]{2,1,0:T(8,128)(2,1)S(1)} %fusion.5) | copy-start | bytes 1179652
  144.3 20.9 %all-to-all-start.2 = ((bf16[4,320,24]{1,2,0:T(8,128)(2,1)}), bf16[4,320,24]{1,2,0:T(8,128)(2,1)S(1)}, u32[]{:S(2)}, u32[]{:S(2)}) async-start(bf16[4,320,24]{1,2,0:T(8,128)(2,1)} %broadcast_in_dim.55), calls=%async_computation.2 | async-start | bytes 147456 | tf_op jit(solution)/shard_map/all_to_all | solution.py:215
  166.5 22.6 %all-to-all-start.3 = ((bf16[64,17,128]{2,1,0:T(8,128)(2,1)}), bf16[64,17,128]{2,1,0:T(8,128)(2,1)S(1)}, u32[]{:S(2)}, u32[]{:S(2)}) async-start(bf16[64,17,128]{2,1,0:T(8,128)(2,1)} %broadcast_in_dim.61), calls=%async_computation.3 | async-start | bytes 786432 | tf_op jit(solution)/shard_map/all_to_all | solution.py:232

commit v2 on v1

--- a/solution.py
+++ b/solution.py
@@ -71,6 +71,16 @@
     cos_t = cos_a[:, None, :] * cos_b[None, :, :] - sin_a[:, None, :] * sin_b[None, :, :]
     sin_t = sin_a[:, None, :] * cos_b[None, :, :] + cos_a[:, None, :] * sin_b[None, :, :]
     table = jnp.concatenate([cos_t, -sin_t], axis=2).reshape(columns, 2 * kept)
+    return split_bf16(table)
+
+
+def inverse_row_tables(factors):
+    cos_a, sin_a, cos_b, sin_b = (part.T for part in factors)
+    columns = cos_a.shape[1] * cos_b.shape[1]
+    kept = cos_a.shape[0]
+    cos_t = cos_a[:, :, None] * cos_b[:, None, :] - sin_a[:, :, None] * sin_b[:, None, :]
+    sin_t = sin_a[:, :, None] * cos_b[:, None, :] + cos_a[:, :, None] * sin_b[:, None, :]
+    table = jnp.concatenate([cos_t, -sin_t], axis=0).reshape(2 * kept, columns)
     return split_bf16(table)
 
 
@@ -201,22 +211,18 @@
     doubling = jnp.where(lax.broadcasted_iota(jnp.int32, (1, 1, columns), 2) % half_cols == 0, 1.0, 2.0)
     weighting = doubling * (1.0 / columns)
     row_both = lax.optimization_barrier(rows_both * weighting.astype(jnp.bfloat16))
-    spatial = two_pass("rck,xk->rcx", row_both, table_pair)
+    spatial = two_pass("rck,kx->rcx", row_both, inverse_row_tables(factors))
     encoded = (hidden.astype(jnp.float32) + spatial).astype(jnp.bfloat16)
     key_count = key_pixels.shape[0]
     query_count = query_pixels.shape[0]
     quarter = query_count // group_count
     slab = lax.axis_index("rows")
-    weight_pieces = jnp.stack(ring_pieces(jnp.concatenate([key_weight, query_weight], axis=1), "ch"))
-    owners = (channel - jnp.arange(group_count)) % group_count
-    weights_all = jnp.take(weight_pieces, owners, axis=0).reshape(group_count * groups, -1)
+    weights_all = jnp.concatenate(
+        ring_pieces(jnp.concatenate([key_weight, query_weight], axis=1), "ch"), axis=0
+    )
     sampled = jnp.concatenate([key_pixels, query_pixels])
     features = encoded[sampled // columns, :, sampled % columns]
-    features = lax.all_to_all(
-        jnp.broadcast_to(features[None], (group_count,) + features.shape),
-        "ch", split_axis=0, concat_axis=0, tiled=True,
-    )
-    features = jnp.transpose(features, (1, 0, 2)).reshape(features.shape[1], -1)
+    features = jnp.concatenate(ring_pieces(features, "ch"), axis=1)
     key_dim = key_weight.shape[1]
     key_unit = unit_rows(
         jnp.dot(features[:key_count], weights_all[:, :key_dim], preferred_element_type=jnp.float32)

time: 208 us -> 232 us (1.12)
  local copies, waits for them, and re-layouts: 31.4 us -> 50.7 us
  other arithmetic: 13.5 us -> 25.2 us
  waiting for transfers between devices: 68.8 us -> 57.2 us
    all_to_all x1 -> x0, starting transfers between devices: 16.3 us -> none  [body(): lax.all_to_all(jnp.broadcast_to(features[None], (group_count,) + features...]
    all_to_all x1, waiting for transfers between devices: 13.2 us -> 0.01 us  [body(): lax.all_to_all(back.reshape(2, slabs, slab_rows, lanes), 'rows', split_ax...]
    ppermute x6 -> x9, waiting for transfers between devices: 23.1 us -> 33.1 us  [ring_pieces(): lax.ppermute(values, axis, [(i, (i + shift) % count) for i in range(count)])]
    neg x0 -> x1, local copies, waits for them, and re-layouts: none -> 9.26 us  [inverse_row_tables(): table = jnp.concatenate([cos_t, -sin_t], axis=0).reshape(2 * kept, columns)]
    sub x0 -> x1, local copies, waits for them, and re-layouts: none -> 9.16 us  [inverse_row_tables(): cos_a[:, :, None] * cos_b[:, None, :]]
    all_to_all x1, starting transfers between devices: 5.91 us -> 15 us  [body(): lax.all_to_all(jnp.broadcast_to(packet[None], (slabs,) + packet.shape), '...]
    sub x0 -> x1, other arithmetic: none -> 7.02 us  [inverse_row_tables(): cos_a[:, :, None] * cos_b[:, None, :]]
    ppermute x6 -> x9, starting transfers between devices: 8.79 us -> 15.2 us  [ring_pieces(): lax.ppermute(values, axis, [(i, (i + shift) % count) for i in range(count)])]
  transfers between devices with their start and end apart: 12 -> 14, of which waited for: 7 -> 6; matrix products, arithmetic and copies ran while one was open for 15% -> 41% of each run, Pallas kernels for 0% -> 0%
where the time goes in v2:
time: 232 us; the launch traced here: 230 us
  waiting for transfers between devices  57.2 us (25%)
  starting transfers between devices  55.8 us (24%)
  local copies, waits for them, and re-layouts  50.7 us (22%)
  other arithmetic  25.2 us (11%)
  matrix products  22.8 us (10%)
  blocking collectives  17.5 us (8%)
    ppermute x9, waiting for transfers between devices, ring_pieces(): lax.ppermute(values, axis, [(i, (i + shift) % count) for i in range(count)])  33.1 us
    all_to_all x1, blocking collectives, body(): lax.all_to_all(jnp.stack([exp_sums, picked], axis=1).reshape(slabs, quart...  17.5 us
    all_to_all x1, waiting for transfers between devices, body(): lax.all_to_all(jnp.broadcast_to(packet[None], (slabs,) + packet.shape), '...  16.2 us
    dot_general x4, matrix products, two_pass(): jnp.einsum(eq, left, part, preferred_element_type=jnp.float32)  15.8 us
    ppermute x9, starting transfers between devices, ring_pieces(): lax.ppermute(values, axis, [(i, (i + shift) % count) for i in range(count)])  15.2 us
    all_to_all x1, starting transfers between devices, body(): lax.all_to_all(jnp.broadcast_to(packet[None], (slabs,) + packet.shape), '...  15 us
    all_to_all x1, starting transfers between devices, body(): lax.all_to_all(wire.astype(jnp.bfloat16), 'rows', split_axis=1, concat_ax...  12.4 us
    neg x1, local copies, waits for them, and re-layouts, inverse_row_tables(): table = jnp.concatenate([cos_t, -sin_t], axis=0).reshape(2 * kept, columns)  9.26 us
  transfers between devices with their start and end apart: 14, of which 6 were waited for; matrix products, arithmetic and copies ran while one was open for 41% of the time, Pallas kernels for 0%

profile of v2, /device:TPU:1, one launch (start us, length us, event | category | flops | bytes accessed | tf_op | source)
XLA Modules:
  0.0 230.4 jit_solution(15409835761130892959)
XLA Ops:
  2.0 5.2 %collective-permute-start.10 = (bf16[24,256]{1,0:T(8,128)(2,1)S(1)}, bf16[24,256]{1,0:T(8,128)(2,1)}, u32[]{:S(2)}, u32[]{:S(2)}) collective-permute-start(bf16[24,256]{1,0:T(8,128)(2,1)S(1)} %constant_dynamic-update-slice_fusion), channel_id=1, source_target_pairs={{0,3},{1,0},{2,1},{3,2},{4,7},{5,4},{6,5},{7,6},{8,11},{9,8},{10,9... | collective-permute-start | bytes 36872 | tf_op jit(solution)/shard_map/ppermute | solution.py:35
  7.2 1.0 fusion.136
  8.2 2.9 %collective-permute-start.1 = (bf16[2,24,2048]{2,1,0:T(8,128)(2,1)S(1)}, bf16[2,24,2048]{2,1,0:T(8,128)(2,1)S(1)}, u32[]{:S(2)}, u32[]{:S(2)}) collective-permute-start(bf16[2,24,2048]{2,1,0:T(8,128)(2,1)S(1)} %get-tuple-element.23), channel_id=1, source_target_pairs={{4,0},{8,4},{12,8},{16,12},{20,16},{24,20},{28,24},{32,28},{36,32}... | collective-permute-start | bytes 589832 | tf_op jit(solution)/shard_map/ppermute | solution.py:23
  11.1 3.0 %collective-permute-start = (bf16[2,24,2048]{2,1,0:T(8,128)(2,1)S(1)}, bf16[2,24,2048]{2,1,0:T(8,128)(2,1)S(1)}, u32[]{:S(2)}, u32[]{:S(2)}) collective-permute-start(bf16[2,24,2048]{2,1,0:T(8,128)(2,1)S(1)} %get-tuple-element.22), channel_id=1, source_target_pairs={{0,4},{4,8},{8,12},{12,16},{16,20},{20,24},{24,28},{28,32},{32,36}... | collective-permute-start | bytes 589832 | tf_op jit(solution)/shard_map/ppermute | solution.py:21
  14.7 1.0 fusion.93
  15.8 1.7 bitcast_convert_fusion.1
  18.7 1.0 slice_bitcast_fusion.8
  19.7 1.3 fusion.47
  21.1 2.3 fusion.56
  23.5 2.7 %collective-permute-start.3 = (bf16[4,24,2048]{2,1,0:T(8,128)(2,1)S(1)}, bf16[4,24,2048]{2,1,0:T(8,128)(2,1)S(1)}, u32[]{:S(2)}, u32[]{:S(2)}) collective-permute-start(bf16[4,24,2048]{2,1,0:T(8,128)(2,1)S(1)} %fusion.56), channel_id=1, source_target_pairs={{0,2},{1,3},{2,0},{3,1},{4,6},{5,7},{6,4},{7,5},{8,10},{9,11},{10,... | collective-permute-start | bytes 1179656 | tf_op jit(solution)/shard_map/ppermute | solution.py:35
  26.1 1.4 collective-permute-start.2
  27.5 2.5 %multiply_subtract_fusion.1 = (f32[32,64,1024]{2,1,0:T(8,128)S(1)}, f32[32,64,1024]{2,1,0:T(8,128)S(1)}) fusion(f32[64,1024]{1,0:T(8,128)S(1)} %get-tuple-element.11, f32[32,1024]{1,0:T(8,128)S(1)} %get-tuple-element.10, f32[64,1024]{1,0:T(8,128)S(1)} %get-tuple-element.9, f32[32,1024]{1,0:T(8,128)S(1)} %get-tuple-element.8), kind=kLoop, calls=%fused_computation.14 | loop fusion | flops 14680064 | bytes 17563648 | tf_op jit(solution)/shard_map/sub | solution.py:71
  30.0 4.3 %collective-permute-done.4 = bf16[4,24,2048]{2,1,0:T(8,128)(2,1)S(1)} collective-permute-done((bf16[4,24,2048]{2,1,0:T(8,128)(2,1)S(1)}, bf16[4,24,2048]{2,1,0:T(8,128)(2,1)S(1)}, u32[]{:S(2)}, u32[]{:S(2)}) %collective-permute-start.4) | collective-permute-done | bytes 393248 | tf_op jit(solution)/shard_map/ppermute | solution.py:35
  34.3 1.4 collective-permute-start.8
  35.7 24.9 %collective-permute-done.3 = bf16[4,24,2048]{2,1,0:T(8,128)(2,1)S(1)} collective-permute-done((bf16[4,24,2048]{2,1,0:T(8,128)(2,1)S(1)}, bf16[4,24,2048]{2,1,0:T(8,128)(2,1)S(1)}, u32[]{:S(2)}, u32[]{:S(2)}) %collective-permute-start.3) | collective-permute-done | bytes 393248 | tf_op jit(solution)/shard_map/ppermute | solution.py:35
  61.1 1.5 fusion.8
  62.6 2.2 fusion.26
  64.8 3.4 %convert_element_type.156 = bf16[4,24,2,64,16]{4,3,2,1,0:T(8,128)(2,1)S(1)} reshape(bf16[4,24,2048]{2,1,0:T(8,128)(2,1)} %fusion.26) | data formatting | bytes 786432 | tf_op jit(solution)/shard_map/convert_element_type | solution.py:183
  68.2 2.3 copy.78
  70.5 2.2 copy.79
  72.6 12.4 %all-to-all-start = ((bf16[2,64,4,384]{3,2,0,1:T(4,128)(2,1)}), bf16[2,64,4,384]{3,2,0,1:T(4,128)(2,1)S(1)}, u32[]{:S(2)}, u32[]{:S(2)}) async-start(bf16[2,64,4,384]{3,2,0,1:T(4,128)(2,1)} %copy.79), calls=%async_computation | async-start | bytes 786432 | tf_op jit(solution)/shard_map/all_to_all | solution.py:182
  85.0 1.0 bitcast_convert_fusion
  86.0 1.2 copy.82
  89.4 1.0 fusion.92
  90.3 1.7 broadcast_multiply_fusion.1
  92.0 7.9 %all-to-all-done = bf16[2,64,4,384]{3,2,0,1:T(4,128)(2,1)S(1)} async-done(((bf16[2,64,4,384]{3,2,0,1:T(4,128)(2,1)}), bf16[2,64,4,384]{3,2,0,1:T(4,128)(2,1)S(1)}, u32[]{:S(2)}, u32[]{:S(2)}) %all-to-all-start) | async-done | bytes 393248 | tf_op jit(solution)/shard_map/all_to_all | solution.py:182
  100.2 1.4 fusion.74
  101.6 1.4 convolution_add_fusion
  103.1 2.8 %fusion.37 = bf16[512,384]{1,0:T(8,128)(2,1)S(1)} fusion(f32[256,256]{1,0:T(8,128)S(1)} %fusion.92, f32[256,256]{1,0:T(8,128)} %get-tuple-element.46, f32[256,256]{1,0:T(8,128)} %copy-done.7, f32[256,384]{1,0:T(8,128)S(1)} %get-tuple-element.17, f32[256,384]{1,0:T(8,128)S(1)} %get-tuple-element.16), kind=kOutput, calls=%fused_computation.42 | convolution fusion | flops 1209335808 | bytes 1966080 | tf_op jit(solution)/shard_map/ym,mn->yn/dot_general | solution.py:202
  106.0 0.9 copy.85
  106.9 7.4 %all-to-all-start.1 = ((bf16[2,64,4,384]{3,2,0,1:T(4,128)(2,1)}), bf16[2,64,4,384]{3,2,0,1:T(4,128)(2,1)S(1)}, u32[]{:S(2)}, u32[]{:S(2)}) async-start(bf16[2,64,4,384]{3,2,0,1:T(4,128)(2,1)} %copy.85), calls=%async_computation.1 | async-start | bytes 786432 | tf_op jit(solution)/shard_map/all_to_all | solution.py:207
  114.9 7.0 %multiply_subtract_fusion = (f32[1024,32,64]{0,2,1:T(8,128)}, f32[1024,32,64]{0,2,1:T(8,128)}) fusion(f32[1024,64]{0,1:T(8,128)S(1)} %bitcast.96, f32[1024,32]{0,1:T(8,128)S(1)} %bitcast.98, f32[1024,64]{0,1:T(8,128)S(1)} %bitcast.97, f32[1024,32]{0,1:T(8,128)S(1)} %bitcast.99), kind=kLoop, calls=%fused_computation.12 | loop fusion | flops 14680064 | bytes 17563648 | tf_op jit(solution)/shard_map/sub | solution.py:81
  121.9 9.3 %copy.89 = f32[1024,2048]{1,0:T(8,128)} copy(f32[1024,2048]{0,1:T(8,128)} %bitcast.92) | data formatting | bytes 16777216 | tf_op jit(solution)/shard_map/neg | solution.py:83
  131.2 9.2 %copy.88 = f32[1024,2048]{1,0:T(8,128)} copy(f32[1024,2048]{0,1:T(8,128)} %bitcast.91) | data formatting | bytes 16777216 | tf_op jit(solution)/shard_map/sub | solution.py:81
  140.4 1.3 copy.86
  141.6 3.0 %copy.87 = bf16[4,24,2,64,16]{4,3,2,1,0:T(8,128)(2,1)S(1)} copy(bf16[4,24,2,64,16]{3,4,1,0,2:T(8,128)(2,1)} %bitcast.95) | data formatting | bytes 786432 | tf_op jit(solution)/shard_map/transpose | solution.py:210
  144.6 5.4 %reshape.365 = bf16[4,24,2048]{2,1,0:T(8,128)(2,1)S(1)} reshape(bf16[4,24,2,64,16]{4,3,2,1,0:T(8,128)(2,1)S(1)} %copy.87) | data formatting | bytes 786432 | tf_op jit(solution)/shard_map/reshape | solution.py:210
  150.9 7.1 %fusion.6 = f32[4,24,2048]{2,1,0:T(8,128)S(1)} fusion(bf16[4,24,2048]{2,1,0:T(8,128)(2,1)S(1)} %broadcast_multiply_fusion, f32[1024,2048]{1,0:T(8,128)} %copy.89, f32[1024,2048]{1,0:T(8,128)} %copy.88), kind=kOutput, calls=%fused_computation.15 | convolution fusion | flops 826277888 | bytes 17956864 | tf_op jit(solution)/shard_map/rck,kx->rcx/dot_general | solution.py:89
  158.6 4.9 %fusion.23 = bf16[4,24,2048]{2,1,0:T(8,128)(2,1)S(1)} fusion(f32[4,24,2048]{2,1,0:T(8,128)S(1)} %fusion.6, bf16[4,24,2048]{2,1,0:T(8,128)(2,1)S(1)} %broadcast_multiply_fusion, f32[1024,2048]{1,0:T(8,128)S(1)} %bitcast.90, f32[1024,2048]{1,0:T(8,128)} %copy.88, bf16[4,24,2048]{2,1,0:T(8,128)(2,1)S(1)} %copy-done.4), kind=kOutput, calls=%fused_computation.25 | convolution fusion | flops 822870016 | bytes 18743296 | tf_op jit(solution)/shard_map/rck,kx->rcx/dot_general | solution.py:89
  163.5 1.1 copy.90
  164.7 4.9 %gather_fusion = bf16[320,24]{1,0:T(8,128)(2,1)S(1)} fusion(bf16[4,24,2048]{1,2,0:T(8,128)(2,1)S(1)} %copy.90, s32[320]{0:T(512)S(1)} %fusion.122), kind=kCustom, calls=%fused_computation | custom fusion | bytes 33280 | tf_op jit(solution)/shard_map/gather | solution.py:224
  169.6 3.0 %collective-permute-start.6 = (bf16[320,24]{1,0:T(8,128)(2,1)S(1)}, bf16[320,24]{1,0:T(8,128)(2,1)S(1)}, u32[]{:S(2)}, u32[]{:S(2)}) collective-permute-start(bf16[320,24]{1,0:T(8,128)(2,1)S(1)} %gather_fusion), channel_id=1, source_target_pairs={{0,2},{1,3},{2,0},{3,1},{4,6},{5,7},{6,4},{7,5},{8,10},{9,11},{10,... | collective-permute-start | bytes 46088 | tf_op jit(solution)/shard_map/ppermute | solution.py:35
  172.6 1.4 collective-permute-start.5
  174.7 2.2 collective-permute-done.6
  176.9 1.8 collective-permute-done.5
  180.0 15.0 %all-to-all-start.2 = ((bf16[64,17,128]{2,1,0:T(8,128)(2,1)}), bf16[64,17,128]{2,1,0:T(8,128)(2,1)S(1)}, u32[]{:S(2)}, u32[]{:S(2)}) async-start(bf16[64,17,128]{2,1,0:T(8,128)(2,1)} %broadcast_in_dim.18), calls=%async_computation.2 | async-start | bytes 786432 | tf_op jit(solution)/shard_map/all_to_all | solution.py:238
  195.2 16.2 %all-to-all-done.2 = bf16[64,17,128]{2,1,0:T(8,128)(2,1)S(1)} async-done(((bf16[64,17,128]{2,1,0:T(8,128)(2,1)}), bf16[64,17,128]{2,1,0:T(8,128)(2,1)S(1)}, u32[]{:S(2)}, u32[]{:S(2)}) %all-to-all-start.2) | async-done | bytes 278560 | tf_op jit(solution)/shard_map/all_to_all | solution.py:238
  212.3 17.5 %all_to_all.20 = f32[64,16,2]{1,2,0:T(2,128)S(1)} all-to-all(f32[64,16,2]{1,2,0:T(2,128)S(1)} %copy.91), channel_id=1, replica_groups=mesh['rows'=64,'ch'=4] {'rows'}, dimensions={0} | all-to-all | bytes 16384 | tf_op jit(solution)/shard_map/all_to_all | solution.py:255
  (77 shorter events, 12.2 us)
Async XLA Ops:
  2.0 170.6 %collective-permute-start.10 = (bf16[24,256]{1,0:T(8,128)(2,1)S(1)}, bf16[24,256]{1,0:T(8,128)(2,1)}, u32[]{:S(2)}, u32[]{:S(2)}) collective-permute-start(bf16[24,256]{1,0:T(8,128)(2,1)S(1)} %constant_dynamic-update-slice_fusion), channel_id=1, source_target_pairs={{0,3},{1,0},{2,1},{3,2},{4,7},{5,4},{6,5},{7,6},{8,11},{9,8},{10,9... | collective-permute-start | bytes 36872 | tf_op jit(solution)/shard_map/ppermute | solution.py:35
  7.2 166.8 %collective-permute-start.9 = (bf16[24,256]{1,0:T(8,128)(2,1)S(1)}, bf16[24,256]{1,0:T(8,128)(2,1)}, u32[]{:S(2)}, u32[]{:S(2)}) collective-permute-start(bf16[24,256]{1,0:T(8,128)(2,1)S(1)} %constant_dynamic-update-slice_fusion), channel_id=1, source_target_pairs={{0,2},{1,3},{2,0},{3,1},{4,6},{5,7},{6,4},{7,5},{8,10},{9,11},{10,... | collective-permute-start | bytes 36872 | tf_op jit(solution)/shard_map/ppermute | solution.py:35
  8.2 11.5 %collective-permute-start.1 = (bf16[2,24,2048]{2,1,0:T(8,128)(2,1)S(1)}, bf16[2,24,2048]{2,1,0:T(8,128)(2,1)S(1)}, u32[]{:S(2)}, u32[]{:S(2)}) collective-permute-start(bf16[2,24,2048]{2,1,0:T(8,128)(2,1)S(1)} %get-tuple-element.23), channel_id=1, source_target_pairs={{4,0},{8,4},{12,8},{16,12},{20,16},{24,20},{28,24},{32,28},{36,32}... | collective-permute-start | bytes 589832 | tf_op jit(solution)/shard_map/ppermute | solution.py:23
  11.1 8.6 %collective-permute-start = (bf16[2,24,2048]{2,1,0:T(8,128)(2,1)S(1)}, bf16[2,24,2048]{2,1,0:T(8,128)(2,1)S(1)}, u32[]{:S(2)}, u32[]{:S(2)}) collective-permute-start(bf16[2,24,2048]{2,1,0:T(8,128)(2,1)S(1)} %get-tuple-element.22), channel_id=1, source_target_pairs={{0,4},{4,8},{8,12},{12,16},{16,20},{20,24},{24,28},{28,32},{32,36}... | collective-permute-start | bytes 589832 | tf_op jit(solution)/shard_map/ppermute | solution.py:21
  14.7 15.3 %copy-start.5 = (f32[32,1024]{1,0:T(8,128)}, f32[32,1024]{1,0:T(8,128)S(1)}, u32[]{:S(2)}) copy-start(f32[32,1024]{1,0:T(8,128)S(1)} %get-tuple-element.8) | copy-start | bytes 393220
  15.7 14.3 %copy-start = (f32[64,1024]{1,0:T(8,128)}, f32[64,1024]{1,0:T(8,128)S(1)}, u32[]{:S(2)}) copy-start(f32[64,1024]{1,0:T(8,128)S(1)} %get-tuple-element.9) | copy-start | bytes 786436
  23.3 11.0 %collective-permute-start.4 = (bf16[4,24,2048]{2,1,0:T(8,128)(2,1)S(1)}, bf16[4,24,2048]{2,1,0:T(8,128)(2,1)S(1)}, u32[]{:S(2)}, u32[]{:S(2)}) collective-permute-start(bf16[4,24,2048]{2,1,0:T(8,128)(2,1)S(1)} %fusion.56), channel_id=1, source_target_pairs={{0,3},{1,0},{2,1},{3,2},{4,7},{5,4},{6,5},{7,6},{8,11},{9,8},{10,9... | collective-permute-start | bytes 1179656 | tf_op jit(solution)/shard_map/ppermute | solution.py:35
  23.5 37.1 %collective-permute-start.3 = (bf16[4,24,2048]{2,1,0:T(8,128)(2,1)S(1)}, bf16[4,24,2048]{2,1,0:T(8,128)(2,1)S(1)}, u32[]{:S(2)}, u32[]{:S(2)}) collective-permute-start(bf16[4,24,2048]{2,1,0:T(8,128)(2,1)S(1)} %fusion.56), channel_id=1, source_target_pairs={{0,2},{1,3},{2,0},{3,1},{4,6},{5,7},{6,4},{7,5},{8,10},{9,11},{10,... | collective-permute-start | bytes 1179656 | tf_op jit(solution)/shard_map/ppermute | solution.py:35
  26.1 34.4 %collective-permute-start.2 = (bf16[4,24,2048]{2,1,0:T(8,128)(2,1)S(1)}, bf16[4,24,2048]{2,1,0:T(8,128)(2,1)S(1)}, u32[]{:S(2)}, u32[]{:S(2)}) collective-permute-start(bf16[4,24,2048]{2,1,0:T(8,128)(2,1)S(1)} %fusion.56), channel_id=1, source_target_pairs={{0,1},{1,2},{2,3},{3,0},{4,5},{5,6},{6,7},{7,4},{8,9},{9,10},{10,1... | collective-permute-start | bytes 1179656 | tf_op jit(solution)/shard_map/ppermute | solution.py:35
  34.3 139.7 %collective-permute-start.8 = (bf16[24,256]{1,0:T(8,128)(2,1)S(1)}, bf16[24,256]{1,0:T(8,128)(2,1)}, u32[]{:S(2)}, u32[]{:S(2)}) collective-permute-start(bf16[24,256]{1,0:T(8,128)(2,1)S(1)} %constant_dynamic-update-slice_fusion), channel_id=1, source_target_pairs={{0,1},{1,2},{2,3},{3,0},{4,5},{5,6},{6,7},{7,4},{8,9},{9,10},{10,1... | collective-permute-start | bytes 36872 | tf_op jit(solution)/shard_map/ppermute | solution.py:35
  61.1 1.5 copy-start.3
  64.8 22.5 %copy-start.8 = (s32[256]{0:T(256)S(1)}, s32[256]{0:T(256)}, u32[]{:S(2)}) copy-start(s32[256]{0:T(256)} %param.18) | copy-start | bytes 3076
  72.6 27.3 %all-to-all-start = ((bf16[2,64,4,384]{3,2,0,1:T(4,128)(2,1)}), bf16[2,64,4,384]{3,2,0,1:T(4,128)(2,1)S(1)}, u32[]{:S(2)}, u32[]{:S(2)}) async-start(bf16[2,64,4,384]{3,2,0,1:T(4,128)(2,1)} %copy.79), calls=%async_computation | async-start | bytes 786432 | tf_op jit(solution)/shard_map/all_to_all | solution.py:182
  87.1 27.8 %copy-start.1 = (f32[64,1024]{1,0:T(8,128)S(1)}, f32[64,1024]{1,0:T(8,128)}, u32[]{:S(2)}) copy-start(f32[64,1024]{1,0:T(8,128)} %copy-done) | copy-start | bytes 786436
  87.2 27.8 %copy-start.6 = (f32[32,1024]{1,0:T(8,128)S(1)}, f32[32,1024]{1,0:T(8,128)}, u32[]{:S(2)}) copy-start(f32[32,1024]{1,0:T(8,128)} %copy-done.5) | copy-start | bytes 393220
  92.0 9.5 %copy-start.7 = (f32[256,256]{1,0:T(8,128)}, f32[256,256]{1,0:T(8,128)S(1)}, u32[]{:S(2)}) copy-start(f32[256,256]{1,0:T(8,128)S(1)} %get-tuple-element.45) | copy-start | bytes 786436
  106.9 33.5 %all-to-all-start.1 = ((bf16[2,64,4,384]{3,2,0,1:T(4,128)(2,1)}), bf16[2,64,4,384]{3,2,0,1:T(4,128)(2,1)S(1)}, u32[]{:S(2)}, u32[]{:S(2)}) async-start(bf16[2,64,4,384]{3,2,0,1:T(4,128)(2,1)} %copy.85), calls=%async_computation.1 | async-start | bytes 786432 | tf_op jit(solution)/shard_map/all_to_all | solution.py:207
  150.1 8.0 %slice-start = ((s8[8388608]{0:T(1024)(128)(4,1)}), s8[4194304]{0:T(1024)(128)(4,1)S(1)}, s32[]{:S(2)}) async-start(s8[8388608]{0:T(1024)(128)(4,1)} %bitcast.89), calls=%async_computation.4 | async-start | bytes 8388608
  150.9 7.7 %slice-start.1 = ((s8[8388608]{0:T(1024)(128)(4,1)}), s8[4194304]{0:T(1024)(128)(4,1)S(1)}, s32[]{:S(2)}) async-start(s8[8388608]{0:T(1024)(128)(4,1)} %bitcast.89), calls=%async_computation.5 | async-start | bytes 8388608
  150.9 7.7 %copy-start.4 = (bf16[4,24,2048]{2,1,0:T(8,128)(2,1)S(1)}, bf16[4,24,2048]{2,1,0:T(8,128)(2,1)}, u32[]{:S(2)}) copy-start(bf16[4,24,2048]{2,1,0:T(8,128)(2,1)} %copy-done.3) | copy-start | bytes 1179652
  158.6 20.6 %copy-start.9 = (bf16[1,128]{1,0:T(2,128)(2,1)S(1)}, bf16[1,128]{1,0:T(2,128)(2,1)}, u32[]{:S(2)}) copy-start(bf16[1,128]{1,0:T(2,128)(2,1)} %fusion.125) | copy-start | bytes 772
  163.5 66.9 %copy-start.2 = (bf16[4,24,2048]{2,1,0:T(8,128)(2,1)}, bf16[4,24,2048]{2,1,0:T(8,128)(2,1)S(1)}, u32[]{:S(2)}) copy-start(bf16[4,24,2048]{2,1,0:T(8,128)(2,1)S(1)} %fusion.23) | copy-start | bytes 1179652
  169.5 5.2 %collective-permute-start.7 = (bf16[320,24]{1,0:T(8,128)(2,1)S(1)}, bf16[320,24]{1,0:T(8,128)(2,1)S(1)}, u32[]{:S(2)}, u32[]{:S(2)}) collective-permute-start(bf16[320,24]{1,0:T(8,128)(2,1)S(1)} %gather_fusion), channel_id=1, source_target_pairs={{0,3},{1,0},{2,1},{3,2},{4,7},{5,4},{6,5},{7,6},{8,11},{9,8},{10,9... | collective-permute-start | bytes 46088 | tf_op jit(solution)/shard_map/ppermute | solution.py:35
  169.6 7.2 %collective-permute-start.6 = (bf16[320,24]{1,0:T(8,128)(2,1)S(1)}, bf16[320,24]{1,0:T(8,128)(2,1)S(1)}, u32[]{:S(2)}, u32[]{:S(2)}) collective-permute-start(bf16[320,24]{1,0:T(8,128)(2,1)S(1)} %gather_fusion), channel_id=1, source_target_pairs={{0,2},{1,3},{2,0},{3,1},{4,6},{5,7},{6,4},{7,5},{8,10},{9,11},{10,... | collective-permute-start | bytes 46088 | tf_op jit(solution)/shard_map/ppermute | solution.py:35
  172.6 6.1 %collective-permute-start.5 = (bf16[320,24]{1,0:T(8,128)(2,1)S(1)}, bf16[320,24]{1,0:T(8,128)(2,1)S(1)}, u32[]{:S(2)}, u32[]{:S(2)}) collective-permute-start(bf16[320,24]{1,0:T(8,128)(2,1)S(1)} %gather_fusion), channel_id=1, source_target_pairs={{0,1},{1,2},{2,3},{3,0},{4,5},{5,6},{6,7},{7,4},{8,9},{9,10},{10,1... | collective-permute-start | bytes 46088 | tf_op jit(solution)/shard_map/ppermute | solution.py:35
  180.0 31.4 %all-to-all-start.2 = ((bf16[64,17,128]{2,1,0:T(8,128)(2,1)}), bf16[64,17,128]{2,1,0:T(8,128)(2,1)S(1)}, u32[]{:S(2)}, u32[]{:S(2)}) async-start(bf16[64,17,128]{2,1,0:T(8,128)(2,1)} %broadcast_in_dim.18), calls=%async_computation.2 | async-start | bytes 786432 | tf_op jit(solution)/shard_map/all_to_all | solution.py:238

commit v3 on v2

--- a/solution.py
+++ b/solution.py
@@ -71,16 +71,6 @@
     cos_t = cos_a[:, None, :] * cos_b[None, :, :] - sin_a[:, None, :] * sin_b[None, :, :]
     sin_t = sin_a[:, None, :] * cos_b[None, :, :] + cos_a[:, None, :] * sin_b[None, :, :]
     table = jnp.concatenate([cos_t, -sin_t], axis=2).reshape(columns, 2 * kept)
-    return split_bf16(table)
-
-
-def inverse_row_tables(factors):
-    cos_a, sin_a, cos_b, sin_b = (part.T for part in factors)
-    columns = cos_a.shape[1] * cos_b.shape[1]
-    kept = cos_a.shape[0]
-    cos_t = cos_a[:, :, None] * cos_b[:, None, :] - sin_a[:, :, None] * sin_b[:, None, :]
-    sin_t = sin_a[:, :, None] * cos_b[:, None, :] + cos_a[:, :, None] * sin_b[:, None, :]
-    table = jnp.concatenate([cos_t, -sin_t], axis=0).reshape(2 * kept, columns)
     return split_bf16(table)
 
 
@@ -211,7 +201,7 @@
     doubling = jnp.where(lax.broadcasted_iota(jnp.int32, (1, 1, columns), 2) % half_cols == 0, 1.0, 2.0)
     weighting = doubling * (1.0 / columns)
     row_both = lax.optimization_barrier(rows_both * weighting.astype(jnp.bfloat16))
-    spatial = two_pass("rck,kx->rcx", row_both, inverse_row_tables(factors))
+    spatial = two_pass("rck,xk->rcx", row_both, table_pair)
     encoded = (hidden.astype(jnp.float32) + spatial).astype(jnp.bfloat16)
     key_count = key_pixels.shape[0]
     query_count = query_pixels.shape[0]

time: 232 us -> 204 us (0.88)
  local copies, waits for them, and re-layouts: 50.7 us -> 28.5 us
  other arithmetic: 25.2 us -> 12.7 us
  starting transfers between devices: 55.8 us -> 66.3 us
    ppermute x9, starting transfers between devices: 15.2 us -> 36.7 us  [ring_pieces(): lax.ppermute(values, axis, [(i, (i + shift) % count) for i in range(count)])]
    all_to_all x1, starting transfers between devices: 15 us -> 4.94 us  [body(): lax.all_to_all(jnp.broadcast_to(packet[None], (slabs,) + packet.shape), '...]
    neg x1 -> x0, local copies, waits for them, and re-layouts: 9.26 us -> none  [inverse_row_tables(): table = jnp.concatenate([cos_t, -sin_t], axis=0).reshape(2 * kept, columns)]
    sub x1 -> x0, local copies, waits for them, and re-layouts: 9.16 us -> none  [inverse_row_tables(): cos_a[:, :, None] * cos_b[:, None, :]]
    sub x1 -> x0, other arithmetic: 7.02 us -> none  [inverse_row_tables(): cos_a[:, :, None] * cos_b[:, None, :]]
    ppermute x9, waiting for transfers between devices: 33.1 us -> 27.3 us  [ring_pieces(): lax.ppermute(values, axis, [(i, (i + shift) % count) for i in range(count)])]
    all_to_all x1, starting transfers between devices: 7.43 us -> 4.61 us  [body(): lax.all_to_all(back.reshape(2, slabs, slab_rows, lanes), 'rows', split_ax...]
    all_to_all x1, waiting for transfers between devices: 7.88 us -> 10.6 us  [body(): lax.all_to_all(wire.astype(jnp.bfloat16), 'rows', split_axis=1, concat_ax...]
  transfers between devices with their start and end apart: 14 -> 14, of which waited for: 6 -> 7; matrix products, arithmetic and copies ran while one was open for 41% -> 20% of each run, Pallas kernels for 0% -> 0%
where the time goes in v3:
time: 204 us; the launch traced here: 203 us
  starting transfers between devices  66.3 us (32%)
  waiting for transfers between devices  56.3 us (28%)
  local copies, waits for them, and re-layouts  28.5 us (14%)
  matrix products  20.5 us (10%)
  blocking collectives  17.6 us (9%)
  other arithmetic  12.7 us (6%)
    ppermute x9, starting transfers between devices, ring_pieces(): lax.ppermute(values, axis, [(i, (i + shift) % count) for i in range(count)])  36.7 us
    ppermute x9, waiting for transfers between devices, ring_pieces(): lax.ppermute(values, axis, [(i, (i + shift) % count) for i in range(count)])  27.3 us
    all_to_all x1, blocking collectives, body(): lax.all_to_all(jnp.stack([exp_sums, picked], axis=1).reshape(slabs, quart...  17.6 us
    dot_general x4, matrix products, two_pass(): jnp.einsum(eq, left, part, preferred_element_type=jnp.float32)  16.4 us
    all_to_all x1, waiting for transfers between devices, body(): lax.all_to_all(jnp.broadcast_to(packet[None], (slabs,) + packet.shape), '...  16.1 us
    all_to_all x1, starting transfers between devices, body(): lax.all_to_all(wire.astype(jnp.bfloat16), 'rows', split_axis=1, concat_ax...  13.6 us
    all_to_all x1, waiting for transfers between devices, body(): lax.all_to_all(wire.astype(jnp.bfloat16), 'rows', split_axis=1, concat_ax...  10.6 us
    convert_element_type x3, local copies, waits for them, and re-layouts, body(): wire.astype(jnp.bfloat16)  6.93 us
  transfers between devices with their start and end apart: 14, of which 7 were waited for; matrix products, arithmetic and copies ran while one was open for 20% of the time, Pallas kernels for 0%

profile of v3, /device:TPU:1, one launch (start us, length us, event | category | flops | bytes accessed | tf_op | source)
XLA Modules:
  0.0 203.1 jit_solution(935982071133782188)
XLA Ops:
  0.6 1.1 fusion.119
  1.7 4.5 %collective-permute-start = (bf16[2,24,2048]{2,1,0:T(8,128)(2,1)S(1)}, bf16[2,24,2048]{2,1,0:T(8,128)(2,1)S(1)}, u32[]{:S(2)}, u32[]{:S(2)}) collective-permute-start(bf16[2,24,2048]{2,1,0:T(8,128)(2,1)S(1)} %get-tuple-element.20), channel_id=1, source_target_pairs={{0,4},{4,8},{8,12},{12,16},{16,20},{20,24},{24,28},{28,32},{32,36}... | collective-permute-start | bytes 589832 | tf_op jit(solution)/shard_map/ppermute | solution.py:21
  6.2 1.9 collective-permute-start.1
  8.1 1.0 fusion.76
  9.2 0.5 fusion.84
  9.8 0.9 fusion.120
  11.0 1.0 slice_bitcast_fusion.8
  12.0 1.2 collective-permute-done.1
  13.2 1.3 fusion.30
  14.5 2.3 %fusion.39 = bf16[4,24,2048]{2,1,0:T(8,128)(2,1)S(1)} fusion(bf16[4,24,2048]{2,1,0:T(8,128)(2,1)} %param.10, bf16[8,24,2052]{2,1,0:T(8,128)(2,1)S(1)} %fusion.30, bf16[2,24,2048]{2,1,0:T(8,128)(2,1)S(1)} %collective-permute-done.1, bf16[2,24,2048]{2,1,0:T(8,128)(2,1)S(1)} %collective-permute-done, f32[24]{0:T(128)S(1)} %get-tuple-element.33, ...), kind=kLoop, calls=%fused_computation.57 | loop fusion | flops 5898240 | bytes 3539808 | tf_op jit(solution)/shard_map/convert_element_type | solution.py:147
  16.8 1.7 collective-permute-start.2
  18.5 3.0 %collective-permute-start.3 = (bf16[4,24,2048]{2,1,0:T(8,128)(2,1)S(1)}, bf16[4,24,2048]{2,1,0:T(8,128)(2,1)S(1)}, u32[]{:S(2)}, u32[]{:S(2)}) collective-permute-start(bf16[4,24,2048]{2,1,0:T(8,128)(2,1)S(1)} %fusion.39), channel_id=1, source_target_pairs={{0,2},{1,3},{2,0},{3,1},{4,6},{5,7},{6,4},{7,5},{8,10},{9,11},{10,... | collective-permute-start | bytes 1179656 | tf_op jit(solution)/shard_map/ppermute | solution.py:35
  21.5 0.7 collective-permute-start.4
  22.2 2.5 %multiply_subtract_fusion = (f32[32,64,1024]{2,1,0:T(8,128)S(1)}, f32[32,64,1024]{2,1,0:T(8,128)S(1)}) fusion(f32[64,1024]{1,0:T(8,128)S(1)} %get-tuple-element.11, f32[32,1024]{1,0:T(8,128)S(1)} %get-tuple-element.10, f32[64,1024]{1,0:T(8,128)S(1)} %get-tuple-element.9, f32[32,1024]{1,0:T(8,128)S(1)} %get-tuple-element.8), kind=kLoop, calls=%fused_computation.7 | loop fusion | flops 14680064 | bytes 17563648 | tf_op jit(solution)/shard_map/sub | solution.py:71
  24.7 7.0 %collective-permute-done.2 = bf16[4,24,2048]{2,1,0:T(8,128)(2,1)S(1)} collective-permute-done((bf16[4,24,2048]{2,1,0:T(8,128)(2,1)S(1)}, bf16[4,24,2048]{2,1,0:T(8,128)(2,1)S(1)}, u32[]{:S(2)}, u32[]{:S(2)}) %collective-permute-start.2) | collective-permute-done | bytes 393248 | tf_op jit(solution)/shard_map/ppermute | solution.py:35
  31.7 15.7 %collective-permute-done.3 = bf16[4,24,2048]{2,1,0:T(8,128)(2,1)S(1)} collective-permute-done((bf16[4,24,2048]{2,1,0:T(8,128)(2,1)S(1)}, bf16[4,24,2048]{2,1,0:T(8,128)(2,1)S(1)}, u32[]{:S(2)}, u32[]{:S(2)}) %collective-permute-start.3) | collective-permute-done | bytes 393248 | tf_op jit(solution)/shard_map/ppermute | solution.py:35
  47.9 1.5 fusion.19
  49.4 1.5 fusion.4
  50.9 2.5 %convert_element_type.147 = bf16[4,24,2,64,16]{4,3,2,1,0:T(8,128)(2,1)S(1)} reshape(bf16[4,24,2048]{2,1,0:T(8,128)(2,1)S(1)} %fusion.4) | data formatting | bytes 786432 | tf_op jit(solution)/shard_map/convert_element_type | solution.py:173
  53.5 2.2 %copy.68 = bf16[2,64,4,24,16]{1,4,3,2,0:T(8,128)(2,1)} copy(bf16[2,64,4,24,16]{4,1,0,3,2:T(8,128)(2,1)S(1)} %bitcast.75) | data formatting | bytes 786432 | tf_op jit(solution)/shard_map/convert_element_type | solution.py:173
  55.7 2.2 %copy.69 = bf16[2,64,4,384]{3,2,0,1:T(4,128)(2,1)} copy(bf16[2,64,4,384]{1,3,2,0:T(8,128)(2,1)} %bitcast.76) | data formatting | bytes 786432 | tf_op jit(solution)/shard_map/convert_element_type | solution.py:173
  57.8 13.6 %all-to-all-start = ((bf16[2,64,4,384]{3,2,0,1:T(4,128)(2,1)}), bf16[2,64,4,384]{3,2,0,1:T(4,128)(2,1)S(1)}, u32[]{:S(2)}, u32[]{:S(2)}) async-start(bf16[2,64,4,384]{3,2,0,1:T(4,128)(2,1)} %copy.69), calls=%async_computation | async-start | bytes 786432 | tf_op jit(solution)/shard_map/all_to_all | solution.py:172
  71.5 1.0 bitcast_convert_fusion
  72.6 1.0 bitcast_convert_fusion.1
  73.8 1.0 fusion.75
  74.8 1.0 broadcast_multiply_fusion.1
  75.8 10.6 %all-to-all-done = bf16[2,64,4,384]{3,2,0,1:T(4,128)(2,1)S(1)} async-done(((bf16[2,64,4,384]{3,2,0,1:T(4,128)(2,1)}), bf16[2,64,4,384]{3,2,0,1:T(4,128)(2,1)S(1)}, u32[]{:S(2)}, u32[]{:S(2)}) %all-to-all-start) | async-done | bytes 393248 | tf_op jit(solution)/shard_map/all_to_all | solution.py:172
  87.6 1.8 fusion.14
  89.5 0.9 copy.75
  90.4 4.6 %all-to-all-start.1 = ((bf16[2,64,4,384]{3,2,0,1:T(4,128)(2,1)}), bf16[2,64,4,384]{3,2,0,1:T(4,128)(2,1)S(1)}, u32[]{:S(2)}, u32[]{:S(2)}) async-start(bf16[2,64,4,384]{3,2,0,1:T(4,128)(2,1)} %copy.75), calls=%async_computation.1 | async-start | bytes 786432 | tf_op jit(solution)/shard_map/all_to_all | solution.py:197
  95.0 11.7 %collective-permute-start.10 = (bf16[24,256]{1,0:T(8,128)(2,1)S(1)}, bf16[24,256]{1,0:T(8,128)(2,1)S(1)}, u32[]{:S(2)}, u32[]{:S(2)}) collective-permute-start(bf16[24,256]{1,0:T(8,128)(2,1)S(1)} %constant_dynamic-update-slice_fusion), channel_id=1, source_target_pairs={{0,3},{1,0},{2,1},{3,2},{4,7},{5,4},{6,5},{7,6},{8,11},{9,8},{10,9... | collective-permute-start | bytes 36872 | tf_op jit(solution)/shard_map/ppermute | solution.py:35
  106.7 0.7 collective-permute-start.8
  107.4 1.1 collective-permute-start.9
  108.7 1.1 all-to-all-done.1
  110.3 2.8 %copy.77 = bf16[4,24,2,64,16]{4,3,2,1,0:T(8,128)(2,1)} copy(bf16[4,24,2,64,16]{3,4,1,0,2:T(8,128)(2,1)S(1)} %bitcast.77) | data formatting | bytes 786432 | tf_op jit(solution)/shard_map/transpose | solution.py:200
  113.1 6.4 %reshape.343 = bf16[4,24,2048]{2,1,0:T(8,128)(2,1)S(1)} reshape(bf16[4,24,2,64,16]{4,3,2,1,0:T(8,128)(2,1)} %copy.77) | data formatting | bytes 786432 | tf_op jit(solution)/shard_map/reshape | solution.py:200
  119.6 8.3 %fusion.17 = f32[4,24,2048]{2,1,0:T(8,128)S(1)} fusion(bf16[4,24,2048]{2,1,0:T(8,128)(2,1)S(1)} %broadcast_multiply_fusion, f32[2048,1024]{1,0:T(8,128)} %bitcast.73, f32[2048,1024]{1,0:T(8,128)} %bitcast.67), kind=kOutput, calls=%fused_computation.32 | convolution fusion | flops 822083584 | bytes 17956864 | tf_op jit(solution)/shard_map/rck,xk->rcx/dot_general | solution.py:79
  128.0 5.1 %fusion.5 = bf16[4,24,2048]{2,1,0:T(8,128)(2,1)S(1)} fusion(f32[4,24,2048]{2,1,0:T(8,128)S(1)} %fusion.17, bf16[4,24,2048]{2,1,0:T(8,128)(2,1)S(1)} %broadcast_multiply_fusion, f32[2048,1024]{1,0:T(8,128)} %bitcast.74, f32[2048,1024]{1,0:T(8,128)S(1)} %bitcast.70, bf16[4,24,2048]{2,1,0:T(8,128)(2,1)S(1)} %copy-done.4), kind=kOutput, calls=%fused_computation.15 | convolution fusion | flops 827064320 | bytes 18743296 | tf_op jit(solution)/shard_map/rck,xk->rcx/dot_general | solution.py:79
  133.1 1.0 copy.78
  134.1 4.9 %gather_fusion = bf16[320,24]{1,0:T(8,128)(2,1)S(1)} fusion(bf16[4,24,2048]{1,2,0:T(8,128)(2,1)S(1)} %copy.78, s32[320]{0:T(512)S(1)} %fusion.105), kind=kCustom, calls=%fused_computation | custom fusion | bytes 33280 | tf_op jit(solution)/shard_map/gather | solution.py:214
  139.0 15.6 %collective-permute-start.5 = (bf16[320,24]{1,0:T(8,128)(2,1)S(1)}, bf16[320,24]{1,0:T(8,128)(2,1)S(1)}, u32[]{:S(2)}, u32[]{:S(2)}) collective-permute-start(bf16[320,24]{1,0:T(8,128)(2,1)S(1)} %gather_fusion), channel_id=1, source_target_pairs={{0,1},{1,2},{2,3},{3,0},{4,5},{5,6},{6,7},{7,4},{8,9},{9,10},{10,1... | collective-permute-start | bytes 46088 | tf_op jit(solution)/shard_map/ppermute | solution.py:35
  154.6 2.2 %collective-permute-start.7 = (bf16[320,24]{1,0:T(8,128)(2,1)S(1)}, bf16[320,24]{1,0:T(8,128)(2,1)S(1)}, u32[]{:S(2)}, u32[]{:S(2)}) collective-permute-start(bf16[320,24]{1,0:T(8,128)(2,1)S(1)} %gather_fusion), channel_id=1, source_target_pairs={{0,3},{1,0},{2,1},{3,2},{4,7},{5,4},{6,5},{7,6},{8,11},{9,8},{10,9... | collective-permute-start | bytes 46088 | tf_op jit(solution)/shard_map/ppermute | solution.py:35
  156.8 4.6 %collective-permute-done.6 = bf16[320,24]{1,0:T(8,128)(2,1)S(1)} collective-permute-done((bf16[320,24]{1,0:T(8,128)(2,1)S(1)}, bf16[320,24]{1,0:T(8,128)(2,1)S(1)}, u32[]{:S(2)}, u32[]{:S(2)}) %collective-permute-start.6) | collective-permute-done | bytes 15392 | tf_op jit(solution)/shard_map/ppermute | solution.py:35
  161.9 0.8 broadcast_in_dim.18
  162.7 4.9 %all-to-all-start.2 = ((bf16[64,17,128]{2,1,0:T(8,128)(2,1)}), bf16[64,17,128]{2,1,0:T(8,128)(2,1)S(1)}, u32[]{:S(2)}, u32[]{:S(2)}) async-start(bf16[64,17,128]{2,1,0:T(8,128)(2,1)} %broadcast_in_dim.18), calls=%async_computation.2 | async-start | bytes 786432 | tf_op jit(solution)/shard_map/all_to_all | solution.py:228
  167.9 16.1 %all-to-all-done.2 = bf16[64,17,128]{2,1,0:T(8,128)(2,1)S(1)} async-done(((bf16[64,17,128]{2,1,0:T(8,128)(2,1)}), bf16[64,17,128]{2,1,0:T(8,128)(2,1)S(1)}, u32[]{:S(2)}, u32[]{:S(2)}) %all-to-all-start.2) | async-done | bytes 278560 | tf_op jit(solution)/shard_map/all_to_all | solution.py:228
  184.9 17.6 %all_to_all.20 = f32[64,16,2]{1,2,0:T(2,128)S(1)} all-to-all(f32[64,16,2]{1,2,0:T(2,128)S(1)} %copy.79), channel_id=1, replica_groups=mesh['rows'=64,'ch'=4] {'rows'}, dimensions={0} | all-to-all | bytes 16384 | tf_op jit(solution)/shard_map/all_to_all | solution.py:245
  202.6 0.5 subtract_bitcast_fusion
  (74 shorter events, 4.9 us)
Async XLA Ops:
  1.7 10.3 %collective-permute-start = (bf16[2,24,2048]{2,1,0:T(8,128)(2,1)S(1)}, bf16[2,24,2048]{2,1,0:T(8,128)(2,1)S(1)}, u32[]{:S(2)}, u32[]{:S(2)}) collective-permute-start(bf16[2,24,2048]{2,1,0:T(8,128)(2,1)S(1)} %get-tuple-element.20), channel_id=1, source_target_pairs={{0,4},{4,8},{8,12},{12,16},{16,20},{20,24},{24,28},{28,32},{32,36}... | collective-permute-start | bytes 589832 | tf_op jit(solution)/shard_map/ppermute | solution.py:21
  6.2 7.0 %collective-permute-start.1 = (bf16[2,24,2048]{2,1,0:T(8,128)(2,1)S(1)}, bf16[2,24,2048]{2,1,0:T(8,128)(2,1)S(1)}, u32[]{:S(2)}, u32[]{:S(2)}) collective-permute-start(bf16[2,24,2048]{2,1,0:T(8,128)(2,1)S(1)} %get-tuple-element.21), channel_id=1, source_target_pairs={{4,0},{8,4},{12,8},{16,12},{20,16},{24,20},{28,24},{32,28},{36,32}... | collective-permute-start | bytes 589832 | tf_op jit(solution)/shard_map/ppermute | solution.py:23
  16.8 14.9 %collective-permute-start.2 = (bf16[4,24,2048]{2,1,0:T(8,128)(2,1)S(1)}, bf16[4,24,2048]{2,1,0:T(8,128)(2,1)S(1)}, u32[]{:S(2)}, u32[]{:S(2)}) collective-permute-start(bf16[4,24,2048]{2,1,0:T(8,128)(2,1)S(1)} %fusion.39), channel_id=1, source_target_pairs={{0,1},{1,2},{2,3},{3,0},{4,5},{5,6},{6,7},{7,4},{8,9},{9,10},{10,1... | collective-permute-start | bytes 1179656 | tf_op jit(solution)/shard_map/ppermute | solution.py:35
  18.5 28.9 %collective-permute-start.3 = (bf16[4,24,2048]{2,1,0:T(8,128)(2,1)S(1)}, bf16[4,24,2048]{2,1,0:T(8,128)(2,1)S(1)}, u32[]{:S(2)}, u32[]{:S(2)}) collective-permute-start(bf16[4,24,2048]{2,1,0:T(8,128)(2,1)S(1)} %fusion.39), channel_id=1, source_target_pairs={{0,2},{1,3},{2,0},{3,1},{4,6},{5,7},{6,4},{7,5},{8,10},{9,11},{10,... | collective-permute-start | bytes 1179656 | tf_op jit(solution)/shard_map/ppermute | solution.py:35
  21.5 25.9 %collective-permute-start.4 = (bf16[4,24,2048]{2,1,0:T(8,128)(2,1)S(1)}, bf16[4,24,2048]{2,1,0:T(8,128)(2,1)S(1)}, u32[]{:S(2)}, u32[]{:S(2)}) collective-permute-start(bf16[4,24,2048]{2,1,0:T(8,128)(2,1)S(1)} %fusion.39), channel_id=1, source_target_pairs={{0,3},{1,0},{2,1},{3,2},{4,7},{5,4},{6,5},{7,6},{8,11},{9,8},{10,9... | collective-permute-start | bytes 1179656 | tf_op jit(solution)/shard_map/ppermute | solution.py:35
  24.7 24.7 %copy-start = (f32[32,64,1024]{2,1,0:T(8,128)}, f32[32,64,1024]{2,1,0:T(8,128)S(1)}, u32[]{:S(2)}) copy-start(f32[32,64,1024]{2,1,0:T(8,128)S(1)} %get-tuple-element.18) | copy-start | bytes 25165828
  24.7 24.7 %copy-start.1 = (f32[32,64,1024]{2,1,0:T(8,128)}, f32[32,64,1024]{2,1,0:T(8,128)S(1)}, u32[]{:S(2)}) copy-start(f32[32,64,1024]{2,1,0:T(8,128)S(1)} %get-tuple-element.19) | copy-start | bytes 25165828
  47.9 1.5 copy-start.3
  57.8 28.5 %all-to-all-start = ((bf16[2,64,4,384]{3,2,0,1:T(4,128)(2,1)}), bf16[2,64,4,384]{3,2,0,1:T(4,128)(2,1)S(1)}, u32[]{:S(2)}, u32[]{:S(2)}) async-start(bf16[2,64,4,384]{3,2,0,1:T(4,128)(2,1)} %copy.69), calls=%async_computation | async-start | bytes 786432 | tf_op jit(solution)/shard_map/all_to_all | solution.py:172
  73.6 21.4 %copy-start.5 = (bf16[24,128]{1,0:T(8,128)(2,1)S(1)}, bf16[24,128]{1,0:T(8,128)(2,1)}, u32[]{:S(2)}) copy-start(bf16[24,128]{1,0:T(8,128)(2,1)} %param.16) | copy-start | bytes 18436
  73.6 21.4 %copy-start.6 = (bf16[24,128]{1,0:T(8,128)(2,1)S(1)}, bf16[24,128]{1,0:T(8,128)(2,1)}, u32[]{:S(2)}) copy-start(bf16[24,128]{1,0:T(8,128)(2,1)} %param.15) | copy-start | bytes 18436
  73.6 34.9 %copy-start.7 = (s32[256]{0:T(256)S(1)}, s32[256]{0:T(256)}, u32[]{:S(2)}) copy-start(s32[256]{0:T(256)} %param.18) | copy-start | bytes 3076
  73.6 34.9 %copy-start.8 = (s32[64]{0:T(128)S(1)}, s32[64]{0:T(128)}, u32[]{:S(2)}) copy-start(s32[64]{0:T(128)} %param.17) | copy-start | bytes 772
  73.6 34.9 %copy-start.9 = (s32[64]{0:T(128)S(1)}, s32[64]{0:T(128)}, u32[]{:S(2)}) copy-start(s32[64]{0:T(128)} %param.19) | copy-start | bytes 772
  90.4 19.5 %all-to-all-start.1 = ((bf16[2,64,4,384]{3,2,0,1:T(4,128)(2,1)}), bf16[2,64,4,384]{3,2,0,1:T(4,128)(2,1)S(1)}, u32[]{:S(2)}, u32[]{:S(2)}) async-start(bf16[2,64,4,384]{3,2,0,1:T(4,128)(2,1)} %copy.75), calls=%async_computation.1 | async-start | bytes 786432 | tf_op jit(solution)/shard_map/all_to_all | solution.py:197
  95.0 59.6 %collective-permute-start.10 = (bf16[24,256]{1,0:T(8,128)(2,1)S(1)}, bf16[24,256]{1,0:T(8,128)(2,1)S(1)}, u32[]{:S(2)}, u32[]{:S(2)}) collective-permute-start(bf16[24,256]{1,0:T(8,128)(2,1)S(1)} %constant_dynamic-update-slice_fusion), channel_id=1, source_target_pairs={{0,3},{1,0},{2,1},{3,2},{4,7},{5,4},{6,5},{7,6},{8,11},{9,8},{10,9... | collective-permute-start | bytes 36872 | tf_op jit(solution)/shard_map/ppermute | solution.py:35
  106.7 50.1 %collective-permute-start.8 = (bf16[24,256]{1,0:T(8,128)(2,1)S(1)}, bf16[24,256]{1,0:T(8,128)(2,1)S(1)}, u32[]{:S(2)}, u32[]{:S(2)}) collective-permute-start(bf16[24,256]{1,0:T(8,128)(2,1)S(1)} %constant_dynamic-update-slice_fusion), channel_id=1, source_target_pairs={{0,1},{1,2},{2,3},{3,0},{4,5},{5,6},{6,7},{7,4},{8,9},{9,10},{10,1... | collective-permute-start | bytes 36872 | tf_op jit(solution)/shard_map/ppermute | solution.py:35
  107.4 49.4 %collective-permute-start.9 = (bf16[24,256]{1,0:T(8,128)(2,1)S(1)}, bf16[24,256]{1,0:T(8,128)(2,1)S(1)}, u32[]{:S(2)}, u32[]{:S(2)}) collective-permute-start(bf16[24,256]{1,0:T(8,128)(2,1)S(1)} %constant_dynamic-update-slice_fusion), channel_id=1, source_target_pairs={{0,2},{1,3},{2,0},{3,1},{4,6},{5,7},{6,4},{7,5},{8,10},{9,11},{10,... | collective-permute-start | bytes 36872 | tf_op jit(solution)/shard_map/ppermute | solution.py:35
  119.5 8.4 %slice-start = ((s8[8388608]{0:T(1024)(128)(4,1)}), s8[4194304]{0:T(1024)(128)(4,1)S(1)}, s32[]{:S(2)}) async-start(s8[8388608]{0:T(1024)(128)(4,1)} %bitcast.68), calls=%async_computation.4 | async-start | bytes 8388608
  119.6 8.3 %slice-start.1 = ((s8[8388608]{0:T(1024)(128)(4,1)}), s8[4194304]{0:T(1024)(128)(4,1)S(1)}, s32[]{:S(2)}) async-start(s8[8388608]{0:T(1024)(128)(4,1)} %bitcast.68), calls=%async_computation.5 | async-start | bytes 8388608
  119.6 8.3 %copy-start.4 = (bf16[4,24,2048]{2,1,0:T(8,128)(2,1)S(1)}, bf16[4,24,2048]{2,1,0:T(8,128)(2,1)}, u32[]{:S(2)}) copy-start(bf16[4,24,2048]{2,1,0:T(8,128)(2,1)} %copy-done.3) | copy-start | bytes 1179652
  133.1 70.1 %copy-start.2 = (bf16[4,24,2048]{2,1,0:T(8,128)(2,1)}, bf16[4,24,2048]{2,1,0:T(8,128)(2,1)S(1)}, u32[]{:S(2)}) copy-start(bf16[4,24,2048]{2,1,0:T(8,128)(2,1)S(1)} %fusion.5) | copy-start | bytes 1179652
  139.0 17.8 %collective-permute-start.5 = (bf16[320,24]{1,0:T(8,128)(2,1)S(1)}, bf16[320,24]{1,0:T(8,128)(2,1)S(1)}, u32[]{:S(2)}, u32[]{:S(2)}) collective-permute-start(bf16[320,24]{1,0:T(8,128)(2,1)S(1)} %gather_fusion), channel_id=1, source_target_pairs={{0,1},{1,2},{2,3},{3,0},{4,5},{5,6},{6,7},{7,4},{8,9},{9,10},{10,1... | collective-permute-start | bytes 46088 | tf_op jit(solution)/shard_map/ppermute | solution.py:35
  154.6 6.8 %collective-permute-start.6 = (bf16[320,24]{1,0:T(8,128)(2,1)S(1)}, bf16[320,24]{1,0:T(8,128)(2,1)S(1)}, u32[]{:S(2)}, u32[]{:S(2)}) collective-permute-start(bf16[320,24]{1,0:T(8,128)(2,1)S(1)} %gather_fusion), channel_id=1, source_target_pairs={{0,2},{1,3},{2,0},{3,1},{4,6},{5,7},{6,4},{7,5},{8,10},{9,11},{10,... | collective-permute-start | bytes 46088 | tf_op jit(solution)/shard_map/ppermute | solution.py:35
  154.6 6.8 %collective-permute-start.7 = (bf16[320,24]{1,0:T(8,128)(2,1)S(1)}, bf16[320,24]{1,0:T(8,128)(2,1)S(1)}, u32[]{:S(2)}, u32[]{:S(2)}) collective-permute-start(bf16[320,24]{1,0:T(8,128)(2,1)S(1)} %gather_fusion), channel_id=1, source_target_pairs={{0,3},{1,0},{2,1},{3,2},{4,7},{5,4},{6,5},{7,6},{8,11},{9,8},{10,9... | collective-permute-start | bytes 46088 | tf_op jit(solution)/shard_map/ppermute | solution.py:35
  162.7 21.3 %all-to-all-start.2 = ((bf16[64,17,128]{2,1,0:T(8,128)(2,1)}), bf16[64,17,128]{2,1,0:T(8,128)(2,1)S(1)}, u32[]{:S(2)}, u32[]{:S(2)}) async-start(bf16[64,17,128]{2,1,0:T(8,128)(2,1)} %broadcast_in_dim.18), calls=%async_computation.2 | async-start | bytes 786432 | tf_op jit(solution)/shard_map/all_to_all | solution.py:228

commit v4 on v3

--- a/solution.py
+++ b/solution.py
@@ -61,16 +61,35 @@
     b = lax.broadcasted_iota(jnp.int32, (inner, kept), 0)
     kb = lax.broadcasted_iota(jnp.int32, (inner, kept), 1)
     cos_b, sin_b = cos_sin(b * kb % columns, columns)
-    return (cos_a, sin_a, cos_b, sin_b)
+    steps = kept // outer
+    k1 = lax.broadcasted_iota(jnp.int32, (steps, columns), 0)
+    x1 = lax.broadcasted_iota(jnp.int32, (steps, columns), 1)
+    cos_u, sin_u = cos_sin(k1 * x1 % (columns // outer), columns // outer)
+    k2 = lax.broadcasted_iota(jnp.int32, (outer, columns), 0)
+    x2 = lax.broadcasted_iota(jnp.int32, (outer, columns), 1)
+    cos_v, sin_v = cos_sin(k2 * x2 % columns, columns)
+    return (cos_a, sin_a, cos_b, sin_b, cos_u, sin_u, cos_v, sin_v)
 
 
 def row_tables(factors):
-    cos_a, sin_a, cos_b, sin_b = factors
+    cos_a, sin_a, cos_b, sin_b = factors[:4]
     columns = cos_a.shape[0] * cos_b.shape[0]
     kept = cos_a.shape[1]
     cos_t = cos_a[:, None, :] * cos_b[None, :, :] - sin_a[:, None, :] * sin_b[None, :, :]
     sin_t = sin_a[:, None, :] * cos_b[None, :, :] + cos_a[:, None, :] * sin_b[None, :, :]
     table = jnp.concatenate([cos_t, -sin_t], axis=2).reshape(columns, 2 * kept)
+    return split_bf16(table)
+
+
+def inverse_row_tables(factors):
+    cos_u, sin_u, cos_v, sin_v = factors[4:]
+    steps, columns = cos_u.shape
+    outer = cos_v.shape[0]
+    cos_t = cos_u[:, None, :] * cos_v[None, :, :] - sin_u[:, None, :] * sin_v[None, :, :]
+    sin_t = sin_u[:, None, :] * cos_v[None, :, :] + cos_u[:, None, :] * sin_v[None, :, :]
+    table = jnp.concatenate(
+        [cos_t.reshape(steps * outer, columns), -sin_t.reshape(steps * outer, columns)], axis=0
+    )
     return split_bf16(table)
 
 
@@ -201,7 +220,7 @@
     doubling = jnp.where(lax.broadcasted_iota(jnp.int32, (1, 1, columns), 2) % half_cols == 0, 1.0, 2.0)
     weighting = doubling * (1.0 / columns)
     row_both = lax.optimization_barrier(rows_both * weighting.astype(jnp.bfloat16))
-    spatial = two_pass("rck,xk->rcx", row_both, table_pair)
+    spatial = two_pass("rck,kx->rcx", row_both, inverse_row_tables(factors))
     encoded = (hidden.astype(jnp.float32) + spatial).astype(jnp.bfloat16)
     key_count = key_pixels.shape[0]
     query_count = query_pixels.shape[0]

time: 204 us -> 221 us (1.083)
  starting transfers between devices: 66.3 us -> 46.8 us
  other arithmetic: 12.7 us -> 28.1 us
  waiting for transfers between devices: 56.3 us -> 71.1 us
  local copies, waits for them, and re-layouts: 28.5 us -> 32 us
  matrix products: 20.5 us -> 23.2 us
    ppermute x9, starting transfers between devices: 36.7 us -> 15.4 us  [ring_pieces(): lax.ppermute(values, axis, [(i, (i + shift) % count) for i in range(count)])]
    all_to_all x1, waiting for transfers between devices: 1.11 us -> 10.6 us  [body(): lax.all_to_all(back.reshape(2, slabs, slab_rows, lanes), 'rows', split_ax...]
    sub x0 -> x1, other arithmetic: none -> 6.98 us  [inverse_row_tables(): cos_u[:, None, :] * cos_v[None, :, :]]
    ppermute x9, waiting for transfers between devices: 27.3 us -> 33.9 us  [ring_pieces(): lax.ppermute(values, axis, [(i, (i + shift) % count) for i in range(count)])]
    sin x2 -> x4, other arithmetic: 1.56 us -> 5.1 us  [cos_sin(): return (jnp.cos(angles), jnp.sin(angles))]
    all_to_all x1, starting transfers between devices: 4.61 us -> 7.43 us  [body(): lax.all_to_all(back.reshape(2, slabs, slab_rows, lanes), 'rows', split_ax...]
  transfers between devices with their start and end apart: 14 -> 14, of which waited for: 7 -> 7; matrix products, arithmetic and copies ran while one was open for 20% -> 36% of each run, Pallas kernels for 0% -> 0%
where the time goes in v4:
time: 221 us; the launch traced here: 220 us
  waiting for transfers between devices  71.1 us (32%)
  starting transfers between devices  46.8 us (21%)
  local copies, waits for them, and re-layouts  32 us (14%)
  other arithmetic  28.1 us (13%)
  matrix products  23.2 us (10%)
  blocking collectives  17.5 us (8%)
    ppermute x9, waiting for transfers between devices, ring_pieces(): lax.ppermute(values, axis, [(i, (i + shift) % count) for i in range(count)])  33.9 us
    all_to_all x1, blocking collectives, body(): lax.all_to_all(jnp.stack([exp_sums, picked], axis=1).reshape(slabs, quart...  17.5 us
    all_to_all x1, waiting for transfers between devices, body(): lax.all_to_all(jnp.broadcast_to(packet[None], (slabs,) + packet.shape), '...  16.3 us
    dot_general x4, matrix products, two_pass(): jnp.einsum(eq, left, part, preferred_element_type=jnp.float32)  15.9 us
    ppermute x9, starting transfers between devices, ring_pieces(): lax.ppermute(values, axis, [(i, (i + shift) % count) for i in range(count)])  15.4 us
    all_to_all x1, starting transfers between devices, body(): lax.all_to_all(wire.astype(jnp.bfloat16), 'rows', split_axis=1, concat_ax...  12.3 us
    all_to_all x1, waiting for transfers between devices, body(): lax.all_to_all(back.reshape(2, slabs, slab_rows, lanes), 'rows', split_ax...  10.6 us
    all_to_all x1, waiting for transfers between devices, body(): lax.all_to_all(wire.astype(jnp.bfloat16), 'rows', split_axis=1, concat_ax...  10.3 us
  transfers between devices with their start and end apart: 14, of which 7 were waited for; matrix products, arithmetic and copies ran while one was open for 36% of the time, Pallas kernels for 0%

profile of v4, /device:TPU:1, one launch (start us, length us, event | category | flops | bytes accessed | tf_op | source)
XLA Modules:
  0.0 219.7 jit_solution(4350284518029902830)
XLA Ops:
  2.0 5.2 %collective-permute-start.10 = (bf16[24,256]{1,0:T(8,128)(2,1)S(1)}, bf16[24,256]{1,0:T(8,128)(2,1)}, u32[]{:S(2)}, u32[]{:S(2)}) collective-permute-start(bf16[24,256]{1,0:T(8,128)(2,1)S(1)} %constant_dynamic-update-slice_fusion), channel_id=1, source_target_pairs={{0,3},{1,0},{2,1},{3,2},{4,7},{5,4},{6,5},{7,6},{8,11},{9,8},{10,9... | collective-permute-start | bytes 36872 | tf_op jit(solution)/shard_map/ppermute | solution.py:35
  7.2 1.0 fusion.151
  8.2 2.9 %collective-permute-start.1 = (bf16[2,24,2048]{2,1,0:T(8,128)(2,1)S(1)}, bf16[2,24,2048]{2,1,0:T(8,128)(2,1)S(1)}, u32[]{:S(2)}, u32[]{:S(2)}) collective-permute-start(bf16[2,24,2048]{2,1,0:T(8,128)(2,1)S(1)} %get-tuple-element.31), channel_id=1, source_target_pairs={{4,0},{8,4},{12,8},{16,12},{20,16},{24,20},{28,24},{32,28},{36,32}... | collective-permute-start | bytes 589832 | tf_op jit(solution)/shard_map/ppermute | solution.py:23
  11.1 3.0 %collective-permute-start = (bf16[2,24,2048]{2,1,0:T(8,128)(2,1)S(1)}, bf16[2,24,2048]{2,1,0:T(8,128)(2,1)S(1)}, u32[]{:S(2)}, u32[]{:S(2)}) collective-permute-start(bf16[2,24,2048]{2,1,0:T(8,128)(2,1)S(1)} %get-tuple-element.30), channel_id=1, source_target_pairs={{0,4},{4,8},{8,12},{12,16},{16,20},{20,24},{24,28},{28,32},{32,36}... | collective-permute-start | bytes 589832 | tf_op jit(solution)/shard_map/ppermute | solution.py:21
  14.7 1.0 fusion.108
  15.7 1.8 fusion.106
  17.5 1.8 fusion.104
  19.2 1.0 bitcast_convert_fusion.1
  20.4 1.0 bitcast_convert_fusion
  21.3 0.9 copy.71
  24.2 1.0 slice_bitcast_fusion.8
  25.2 1.3 fusion.47
  26.5 2.3 %fusion.56 = bf16[4,24,2048]{2,1,0:T(8,128)(2,1)S(1)} fusion(bf16[4,24,2048]{2,1,0:T(8,128)(2,1)} %param.10, bf16[8,24,2052]{2,1,0:T(8,128)(2,1)S(1)} %fusion.47, bf16[2,24,2048]{2,1,0:T(8,128)(2,1)S(1)} %collective-permute-done.1, bf16[2,24,2048]{2,1,0:T(8,128)(2,1)S(1)} %collective-permute-done, f32[24]{0:T(128)S(1)} %get-tuple-element.43, ...), kind=kLoop, calls=%fused_computation.66 | loop fusion | flops 5898240 | bytes 3539808 | tf_op jit(solution)/shard_map/convert_element_type | solution.py:166
  29.0 2.7 %collective-permute-start.3 = (bf16[4,24,2048]{2,1,0:T(8,128)(2,1)S(1)}, bf16[4,24,2048]{2,1,0:T(8,128)(2,1)S(1)}, u32[]{:S(2)}, u32[]{:S(2)}) collective-permute-start(bf16[4,24,2048]{2,1,0:T(8,128)(2,1)S(1)} %fusion.56), channel_id=1, source_target_pairs={{0,2},{1,3},{2,0},{3,1},{4,6},{5,7},{6,4},{7,5},{8,10},{9,11},{10,... | collective-permute-start | bytes 1179656 | tf_op jit(solution)/shard_map/ppermute | solution.py:35
  31.7 1.4 collective-permute-start.2
  33.0 2.5 %multiply_subtract_fusion.1 = (f32[32,64,1024]{2,1,0:T(8,128)S(1)}, f32[32,64,1024]{2,1,0:T(8,128)S(1)}) fusion(f32[64,1024]{1,0:T(8,128)S(1)} %get-tuple-element.15, f32[32,1024]{1,0:T(8,128)S(1)} %get-tuple-element.14, f32[64,1024]{1,0:T(8,128)S(1)} %get-tuple-element.13, f32[32,1024]{1,0:T(8,128)S(1)} %get-tuple-element.12), kind=kLoop, calls=%fused_computation.14 | loop fusion | flops 14680064 | bytes 17563648 | tf_op jit(solution)/shard_map/sub | solution.py:78
  35.5 4.3 %collective-permute-done.4 = bf16[4,24,2048]{2,1,0:T(8,128)(2,1)S(1)} collective-permute-done((bf16[4,24,2048]{2,1,0:T(8,128)(2,1)S(1)}, bf16[4,24,2048]{2,1,0:T(8,128)(2,1)S(1)}, u32[]{:S(2)}, u32[]{:S(2)}) %collective-permute-start.4) | collective-permute-done | bytes 393248 | tf_op jit(solution)/shard_map/ppermute | solution.py:35
  39.8 1.4 collective-permute-start.8
  41.2 24.9 %collective-permute-done.3 = bf16[4,24,2048]{2,1,0:T(8,128)(2,1)S(1)} collective-permute-done((bf16[4,24,2048]{2,1,0:T(8,128)(2,1)S(1)}, bf16[4,24,2048]{2,1,0:T(8,128)(2,1)S(1)}, u32[]{:S(2)}, u32[]{:S(2)}) %collective-permute-start.3) | collective-permute-done | bytes 393248 | tf_op jit(solution)/shard_map/ppermute | solution.py:35
  66.6 1.5 fusion.8
  68.1 2.3 %fusion.26 = bf16[4,24,2048]{2,1,0:T(8,128)(2,1)} fusion(f32[4,24,2048]{2,1,0:T(8,128)S(1)} %fusion.8, bf16[4,24,2048]{2,1,0:T(8,128)(2,1)S(1)} %fusion.66, f32[2048,1024]{1,0:T(8,128)S(1)} %bitcast.84, f32[2048,1024]{1,0:T(8,128)S(1)} %bitcast.82), kind=kOutput, calls=%fused_computation.26 | convolution fusion | flops 822476800 | bytes 18350080 | tf_op jit(solution)/shard_map/rcx,xk->rck/dot_general | solution.py:98
  70.4 3.3 %convert_element_type.168 = bf16[4,24,2,64,16]{4,3,2,1,0:T(8,128)(2,1)S(1)} reshape(bf16[4,24,2048]{2,1,0:T(8,128)(2,1)} %fusion.26) | data formatting | bytes 786432 | tf_op jit(solution)/shard_map/convert_element_type | solution.py:192
  73.8 2.2 %copy.68 = bf16[2,64,4,24,16]{1,4,3,2,0:T(8,128)(2,1)} copy(bf16[2,64,4,24,16]{4,1,0,3,2:T(8,128)(2,1)S(1)} %bitcast.91) | data formatting | bytes 786432 | tf_op jit(solution)/shard_map/convert_element_type | solution.py:192
  76.0 2.2 %copy.69 = bf16[2,64,4,384]{3,2,0,1:T(4,128)(2,1)} copy(bf16[2,64,4,384]{1,3,2,0:T(8,128)(2,1)} %bitcast.92) | data formatting | bytes 786432 | tf_op jit(solution)/shard_map/convert_element_type | solution.py:192
  78.2 12.3 %all-to-all-start = ((bf16[2,64,4,384]{3,2,0,1:T(4,128)(2,1)}), bf16[2,64,4,384]{3,2,0,1:T(4,128)(2,1)S(1)}, u32[]{:S(2)}, u32[]{:S(2)}) async-start(bf16[2,64,4,384]{3,2,0,1:T(4,128)(2,1)} %copy.69), calls=%async_computation | async-start | bytes 786432 | tf_op jit(solution)/shard_map/all_to_all | solution.py:191
  92.5 1.0 fusion.103
  93.5 1.7 broadcast_multiply_fusion.1
  95.2 10.3 %all-to-all-done = bf16[2,64,4,384]{3,2,0,1:T(4,128)(2,1)S(1)} async-done(((bf16[2,64,4,384]{3,2,0,1:T(4,128)(2,1)}), bf16[2,64,4,384]{3,2,0,1:T(4,128)(2,1)S(1)}, u32[]{:S(2)}, u32[]{:S(2)}) %all-to-all-start) | async-done | bytes 393248 | tf_op jit(solution)/shard_map/all_to_all | solution.py:191
  105.7 1.4 fusion.74
  107.1 1.4 convolution_add_fusion
  108.6 3.0 %fusion.37 = bf16[512,384]{1,0:T(8,128)(2,1)S(1)} fusion(f32[256,256]{1,0:T(8,128)} %copy-done.8, f32[256,256]{1,0:T(8,128)} %get-tuple-element.58, f32[256,256]{1,0:T(8,128)} %copy-done.9, f32[256,384]{1,0:T(8,128)S(1)} %get-tuple-element.25, f32[256,384]{1,0:T(8,128)S(1)} %get-tuple-element.24), kind=kOutput, calls=%fused_computation.42 | convolution fusion | flops 1209335808 | bytes 1966080 | tf_op jit(solution)/shard_map/ym,mn->yn/dot_general | solution.py:211
  112.6 7.4 %all-to-all-start.1 = ((bf16[2,64,4,384]{3,2,0,1:T(4,128)(2,1)}), bf16[2,64,4,384]{3,2,0,1:T(4,128)(2,1)S(1)}, u32[]{:S(2)}, u32[]{:S(2)}) async-start(bf16[2,64,4,384]{3,2,0,1:T(4,128)(2,1)} %copy.75), calls=%async_computation.1 | async-start | bytes 786432 | tf_op jit(solution)/shard_map/all_to_all | solution.py:216
  120.1 7.0 %multiply_subtract_fusion = (f32[32,32,2048]{2,1,0:T(8,128)}, f32[32,32,2048]{2,1,0:T(8,128)}) fusion(f32[32,2048]{1,0:T(8,128)S(1)} %copy-done.6, f32[32,2048]{1,0:T(8,128)S(1)} %copy-done.4, f32[32,2048]{1,0:T(8,128)S(1)} %copy-done.7, f32[32,2048]{1,0:T(8,128)S(1)} %copy-done.5), kind=kLoop, calls=%fused_computation.12 | loop fusion | flops 14680064 | bytes 17825792 | tf_op jit(solution)/shard_map/sub | solution.py:88
  127.1 10.6 %all-to-all-done.1 = bf16[2,64,4,384]{3,2,0,1:T(4,128)(2,1)S(1)} async-done(((bf16[2,64,4,384]{3,2,0,1:T(4,128)(2,1)}), bf16[2,64,4,384]{3,2,0,1:T(4,128)(2,1)S(1)}, u32[]{:S(2)}, u32[]{:S(2)}) %all-to-all-start.1) | async-done | bytes 393248 | tf_op jit(solution)/shard_map/all_to_all | solution.py:216
  137.7 1.3 copy.76
  138.9 3.0 %copy.77 = bf16[4,24,2,64,16]{4,3,2,1,0:T(8,128)(2,1)S(1)} copy(bf16[4,24,2,64,16]{3,4,1,0,2:T(8,128)(2,1)} %bitcast.93) | data formatting | bytes 786432 | tf_op jit(solution)/shard_map/transpose | solution.py:219
  141.9 5.4 %reshape.364 = bf16[4,24,2048]{2,1,0:T(8,128)(2,1)S(1)} reshape(bf16[4,24,2,64,16]{4,3,2,1,0:T(8,128)(2,1)S(1)} %copy.77) | data formatting | bytes 786432 | tf_op jit(solution)/shard_map/reshape | solution.py:219
  148.3 7.1 %fusion.6 = f32[4,24,2048]{2,1,0:T(8,128)S(1)} fusion(bf16[4,24,2048]{2,1,0:T(8,128)(2,1)S(1)} %broadcast_multiply_fusion, f32[1024,2048]{1,0:T(8,128)} %bitcast.89, f32[1024,2048]{1,0:T(8,128)} %bitcast.85), kind=kOutput, calls=%fused_computation.15 | convolution fusion | flops 826277888 | bytes 17956864 | tf_op jit(solution)/shard_map/rck,kx->rcx/dot_general | solution.py:98
  155.9 5.1 %fusion.23 = bf16[4,24,2048]{2,1,0:T(8,128)(2,1)S(1)} fusion(f32[4,24,2048]{2,1,0:T(8,128)S(1)} %fusion.6, bf16[4,24,2048]{2,1,0:T(8,128)(2,1)S(1)} %broadcast_multiply_fusion, f32[1024,2048]{1,0:T(8,128)} %bitcast.90, f32[1024,2048]{1,0:T(8,128)S(1)} %bitcast.88, bf16[4,24,2048]{2,1,0:T(8,128)(2,1)S(1)} %copy-done.3), kind=kOutput, calls=%fused_computation.25 | convolution fusion | flops 822870016 | bytes 18743296 | tf_op jit(solution)/shard_map/rck,kx->rcx/dot_general | solution.py:98
  161.0 1.1 copy.78
  162.1 4.9 %gather_fusion = bf16[320,24]{1,0:T(8,128)(2,1)S(1)} fusion(bf16[4,24,2048]{1,2,0:T(8,128)(2,1)S(1)} %copy.78, s32[320]{0:T(512)S(1)} %fusion.137), kind=kCustom, calls=%fused_computation | custom fusion | bytes 33280 | tf_op jit(solution)/shard_map/gather | solution.py:233
  167.0 3.2 %collective-permute-start.6 = (bf16[320,24]{1,0:T(8,128)(2,1)S(1)}, bf16[320,24]{1,0:T(8,128)(2,1)S(1)}, u32[]{:S(2)}, u32[]{:S(2)}) collective-permute-start(bf16[320,24]{1,0:T(8,128)(2,1)S(1)} %gather_fusion), channel_id=1, source_target_pairs={{0,2},{1,3},{2,0},{3,1},{4,6},{5,7},{6,4},{7,5},{8,10},{9,11},{10,... | collective-permute-start | bytes 46088 | tf_op jit(solution)/shard_map/ppermute | solution.py:35
  170.2 1.4 collective-permute-start.5
  172.3 2.8 %collective-permute-done.6 = bf16[320,24]{1,0:T(8,128)(2,1)S(1)} collective-permute-done((bf16[320,24]{1,0:T(8,128)(2,1)S(1)}, bf16[320,24]{1,0:T(8,128)(2,1)S(1)}, u32[]{:S(2)}, u32[]{:S(2)}) %collective-permute-start.6) | collective-permute-done | bytes 15392 | tf_op jit(solution)/shard_map/ppermute | solution.py:35
  175.1 1.9 collective-permute-done.5
  178.4 5.8 %all-to-all-start.2 = ((bf16[64,17,128]{2,1,0:T(8,128)(2,1)}), bf16[64,17,128]{2,1,0:T(8,128)(2,1)S(1)}, u32[]{:S(2)}, u32[]{:S(2)}) async-start(bf16[64,17,128]{2,1,0:T(8,128)(2,1)} %broadcast_in_dim.18), calls=%async_computation.2 | async-start | bytes 786432 | tf_op jit(solution)/shard_map/all_to_all | solution.py:247
  184.4 16.3 %all-to-all-done.2 = bf16[64,17,128]{2,1,0:T(8,128)(2,1)S(1)} async-done(((bf16[64,17,128]{2,1,0:T(8,128)(2,1)}), bf16[64,17,128]{2,1,0:T(8,128)(2,1)S(1)}, u32[]{:S(2)}, u32[]{:S(2)}) %all-to-all-start.2) | async-done | bytes 278560 | tf_op jit(solution)/shard_map/all_to_all | solution.py:247
  201.6 17.5 %all_to_all.20 = f32[64,16,2]{1,2,0:T(2,128)S(1)} all-to-all(f32[64,16,2]{1,2,0:T(2,128)S(1)} %copy.79), channel_id=1, replica_groups=mesh['rows'=64,'ch'=4] {'rows'}, dimensions={0} | all-to-all | bytes 16384 | tf_op jit(solution)/shard_map/all_to_all | solution.py:264
  (79 shorter events, 13.2 us)
Async XLA Ops:
  2.0 168.2 %collective-permute-start.10 = (bf16[24,256]{1,0:T(8,128)(2,1)S(1)}, bf16[24,256]{1,0:T(8,128)(2,1)}, u32[]{:S(2)}, u32[]{:S(2)}) collective-permute-start(bf16[24,256]{1,0:T(8,128)(2,1)S(1)} %constant_dynamic-update-slice_fusion), channel_id=1, source_target_pairs={{0,3},{1,0},{2,1},{3,2},{4,7},{5,4},{6,5},{7,6},{8,11},{9,8},{10,9... | collective-permute-start | bytes 36872 | tf_op jit(solution)/shard_map/ppermute | solution.py:35
  7.2 164.4 %collective-permute-start.9 = (bf16[24,256]{1,0:T(8,128)(2,1)S(1)}, bf16[24,256]{1,0:T(8,128)(2,1)}, u32[]{:S(2)}, u32[]{:S(2)}) collective-permute-start(bf16[24,256]{1,0:T(8,128)(2,1)S(1)} %constant_dynamic-update-slice_fusion), channel_id=1, source_target_pairs={{0,2},{1,3},{2,0},{3,1},{4,6},{5,7},{6,4},{7,5},{8,10},{9,11},{10,... | collective-permute-start | bytes 36872 | tf_op jit(solution)/shard_map/ppermute | solution.py:35
  8.2 16.9 %collective-permute-start.1 = (bf16[2,24,2048]{2,1,0:T(8,128)(2,1)S(1)}, bf16[2,24,2048]{2,1,0:T(8,128)(2,1)S(1)}, u32[]{:S(2)}, u32[]{:S(2)}) collective-permute-start(bf16[2,24,2048]{2,1,0:T(8,128)(2,1)S(1)} %get-tuple-element.31), channel_id=1, source_target_pairs={{4,0},{8,4},{12,8},{16,12},{20,16},{24,20},{28,24},{32,28},{36,32}... | collective-permute-start | bytes 589832 | tf_op jit(solution)/shard_map/ppermute | solution.py:23
  11.1 14.1 %collective-permute-start = (bf16[2,24,2048]{2,1,0:T(8,128)(2,1)S(1)}, bf16[2,24,2048]{2,1,0:T(8,128)(2,1)S(1)}, u32[]{:S(2)}, u32[]{:S(2)}) collective-permute-start(bf16[2,24,2048]{2,1,0:T(8,128)(2,1)S(1)} %get-tuple-element.30), channel_id=1, source_target_pairs={{0,4},{4,8},{8,12},{12,16},{16,20},{20,24},{24,28},{28,32},{32,36}... | collective-permute-start | bytes 589832 | tf_op jit(solution)/shard_map/ppermute | solution.py:21
  28.8 11.0 %collective-permute-start.4 = (bf16[4,24,2048]{2,1,0:T(8,128)(2,1)S(1)}, bf16[4,24,2048]{2,1,0:T(8,128)(2,1)S(1)}, u32[]{:S(2)}, u32[]{:S(2)}) collective-permute-start(bf16[4,24,2048]{2,1,0:T(8,128)(2,1)S(1)} %fusion.56), channel_id=1, source_target_pairs={{0,3},{1,0},{2,1},{3,2},{4,7},{5,4},{6,5},{7,6},{8,11},{9,8},{10,9... | collective-permute-start | bytes 1179656 | tf_op jit(solution)/shard_map/ppermute | solution.py:35
  29.0 37.1 %collective-permute-start.3 = (bf16[4,24,2048]{2,1,0:T(8,128)(2,1)S(1)}, bf16[4,24,2048]{2,1,0:T(8,128)(2,1)S(1)}, u32[]{:S(2)}, u32[]{:S(2)}) collective-permute-start(bf16[4,24,2048]{2,1,0:T(8,128)(2,1)S(1)} %fusion.56), channel_id=1, source_target_pairs={{0,2},{1,3},{2,0},{3,1},{4,6},{5,7},{6,4},{7,5},{8,10},{9,11},{10,... | collective-permute-start | bytes 1179656 | tf_op jit(solution)/shard_map/ppermute | solution.py:35
  31.7 34.4 %collective-permute-start.2 = (bf16[4,24,2048]{2,1,0:T(8,128)(2,1)S(1)}, bf16[4,24,2048]{2,1,0:T(8,128)(2,1)S(1)}, u32[]{:S(2)}, u32[]{:S(2)}) collective-permute-start(bf16[4,24,2048]{2,1,0:T(8,128)(2,1)S(1)} %fusion.56), channel_id=1, source_target_pairs={{0,1},{1,2},{2,3},{3,0},{4,5},{5,6},{6,7},{7,4},{8,9},{9,10},{10,1... | collective-permute-start | bytes 1179656 | tf_op jit(solution)/shard_map/ppermute | solution.py:35
  39.8 131.8 %collective-permute-start.8 = (bf16[24,256]{1,0:T(8,128)(2,1)S(1)}, bf16[24,256]{1,0:T(8,128)(2,1)}, u32[]{:S(2)}, u32[]{:S(2)}) collective-permute-start(bf16[24,256]{1,0:T(8,128)(2,1)S(1)} %constant_dynamic-update-slice_fusion), channel_id=1, source_target_pairs={{0,1},{1,2},{2,3},{3,0},{4,5},{5,6},{6,7},{7,4},{8,9},{9,10},{10,1... | collective-permute-start | bytes 36872 | tf_op jit(solution)/shard_map/ppermute | solution.py:35
  66.6 1.5 copy-start.2
  76.0 32.5 %copy-start = (f32[256,384]{1,0:T(8,128)S(1)}, f32[256,384]{1,0:T(8,128)}, u32[]{:S(2)}) copy-start(f32[256,384]{1,0:T(8,128)} %copy.71) | copy-start | bytes 1179652
  78.2 41.8 %copy-start.4 = (f32[32,2048]{1,0:T(8,128)S(1)}, f32[32,2048]{1,0:T(8,128)}, u32[]{:S(2)}) copy-start(f32[32,2048]{1,0:T(8,128)} %get-tuple-element.18) | copy-start | bytes 786436
  78.2 41.8 %copy-start.5 = (f32[32,2048]{1,0:T(8,128)S(1)}, f32[32,2048]{1,0:T(8,128)}, u32[]{:S(2)}) copy-start(f32[32,2048]{1,0:T(8,128)} %get-tuple-element.16) | copy-start | bytes 786436
  78.2 41.8 %copy-start.6 = (f32[32,2048]{1,0:T(8,128)S(1)}, f32[32,2048]{1,0:T(8,128)}, u32[]{:S(2)}) copy-start(f32[32,2048]{1,0:T(8,128)} %get-tuple-element.19) | copy-start | bytes 786436
  78.2 41.8 %copy-start.7 = (f32[32,2048]{1,0:T(8,128)S(1)}, f32[32,2048]{1,0:T(8,128)}, u32[]{:S(2)}) copy-start(f32[32,2048]{1,0:T(8,128)} %get-tuple-element.17) | copy-start | bytes 786436
  78.2 27.2 %all-to-all-start = ((bf16[2,64,4,384]{3,2,0,1:T(4,128)(2,1)}), bf16[2,64,4,384]{3,2,0,1:T(4,128)(2,1)S(1)}, u32[]{:S(2)}, u32[]{:S(2)}) async-start(bf16[2,64,4,384]{3,2,0,1:T(4,128)(2,1)} %copy.69), calls=%async_computation | async-start | bytes 786432 | tf_op jit(solution)/shard_map/all_to_all | solution.py:191
  93.5 13.6 %copy-start.8 = (f32[256,256]{1,0:T(8,128)}, f32[256,256]{1,0:T(8,128)S(1)}, u32[]{:S(2)}) copy-start(f32[256,256]{1,0:T(8,128)S(1)} %fusion.103) | copy-start | bytes 786436
  95.2 11.9 %copy-start.9 = (f32[256,256]{1,0:T(8,128)}, f32[256,256]{1,0:T(8,128)S(1)}, u32[]{:S(2)}) copy-start(f32[256,256]{1,0:T(8,128)S(1)} %get-tuple-element.57) | copy-start | bytes 786436
  112.6 25.1 %all-to-all-start.1 = ((bf16[2,64,4,384]{3,2,0,1:T(4,128)(2,1)}), bf16[2,64,4,384]{3,2,0,1:T(4,128)(2,1)S(1)}, u32[]{:S(2)}, u32[]{:S(2)}) async-start(bf16[2,64,4,384]{3,2,0,1:T(4,128)(2,1)} %copy.75), calls=%async_computation.1 | async-start | bytes 786432 | tf_op jit(solution)/shard_map/all_to_all | solution.py:216
  147.4 8.0 %slice-start = ((s8[8388608]{0:T(1024)(128)(4,1)}), s8[4194304]{0:T(1024)(128)(4,1)S(1)}, s32[]{:S(2)}) async-start(s8[8388608]{0:T(1024)(128)(4,1)} %bitcast.86), calls=%async_computation.4 | async-start | bytes 8388608
  148.2 7.7 %slice-start.1 = ((s8[8388608]{0:T(1024)(128)(4,1)}), s8[4194304]{0:T(1024)(128)(4,1)S(1)}, s32[]{:S(2)}) async-start(s8[8388608]{0:T(1024)(128)(4,1)} %bitcast.86), calls=%async_computation.5 | async-start | bytes 8388608
  148.2 7.6 %copy-start.3 = (bf16[4,24,2048]{2,1,0:T(8,128)(2,1)S(1)}, bf16[4,24,2048]{2,1,0:T(8,128)(2,1)}, u32[]{:S(2)}) copy-start(bf16[4,24,2048]{2,1,0:T(8,128)(2,1)} %copy-done.2) | copy-start | bytes 1179652
  155.9 21.6 %copy-start.10 = (bf16[1,128]{1,0:T(2,128)(2,1)S(1)}, bf16[1,128]{1,0:T(2,128)(2,1)}, u32[]{:S(2)}) copy-start(bf16[1,128]{1,0:T(2,128)(2,1)} %fusion.140) | copy-start | bytes 772
  161.0 58.8 %copy-start.1 = (bf16[4,24,2048]{2,1,0:T(8,128)(2,1)}, bf16[4,24,2048]{2,1,0:T(8,128)(2,1)S(1)}, u32[]{:S(2)}) copy-start(bf16[4,24,2048]{2,1,0:T(8,128)(2,1)S(1)} %fusion.23) | copy-start | bytes 1179652
  167.0 5.4 %collective-permute-start.7 = (bf16[320,24]{1,0:T(8,128)(2,1)S(1)}, bf16[320,24]{1,0:T(8,128)(2,1)S(1)}, u32[]{:S(2)}, u32[]{:S(2)}) collective-permute-start(bf16[320,24]{1,0:T(8,128)(2,1)S(1)} %gather_fusion), channel_id=1, source_target_pairs={{0,3},{1,0},{2,1},{3,2},{4,7},{5,4},{6,5},{7,6},{8,11},{9,8},{10,9... | collective-permute-start | bytes 46088 | tf_op jit(solution)/shard_map/ppermute | solution.py:35
  167.0 8.1 %collective-permute-start.6 = (bf16[320,24]{1,0:T(8,128)(2,1)S(1)}, bf16[320,24]{1,0:T(8,128)(2,1)S(1)}, u32[]{:S(2)}, u32[]{:S(2)}) collective-permute-start(bf16[320,24]{1,0:T(8,128)(2,1)S(1)} %gather_fusion), channel_id=1, source_target_pairs={{0,2},{1,3},{2,0},{3,1},{4,6},{5,7},{6,4},{7,5},{8,10},{9,11},{10,... | collective-permute-start | bytes 46088 | tf_op jit(solution)/shard_map/ppermute | solution.py:35
  170.2 6.9 %collective-permute-start.5 = (bf16[320,24]{1,0:T(8,128)(2,1)S(1)}, bf16[320,24]{1,0:T(8,128)(2,1)S(1)}, u32[]{:S(2)}, u32[]{:S(2)}) collective-permute-start(bf16[320,24]{1,0:T(8,128)(2,1)S(1)} %gather_fusion), channel_id=1, source_target_pairs={{0,1},{1,2},{2,3},{3,0},{4,5},{5,6},{6,7},{7,4},{8,9},{9,10},{10,1... | collective-permute-start | bytes 46088 | tf_op jit(solution)/shard_map/ppermute | solution.py:35
  178.4 22.3 %all-to-all-start.2 = ((bf16[64,17,128]{2,1,0:T(8,128)(2,1)}), bf16[64,17,128]{2,1,0:T(8,128)(2,1)S(1)}, u32[]{:S(2)}, u32[]{:S(2)}) async-start(bf16[64,17,128]{2,1,0:T(8,128)(2,1)} %broadcast_in_dim.18), calls=%async_computation.2 | async-start | bytes 786432 | tf_op jit(solution)/shard_map/all_to_all | solution.py:247

commit v5 on v3

--- a/solution.py
+++ b/solution.py
@@ -201,7 +201,11 @@
     doubling = jnp.where(lax.broadcasted_iota(jnp.int32, (1, 1, columns), 2) % half_cols == 0, 1.0, 2.0)
     weighting = doubling * (1.0 / columns)
     row_both = lax.optimization_barrier(rows_both * weighting.astype(jnp.bfloat16))
-    spatial = two_pass("rck,xk->rcx", row_both, table_pair)
+    parity = lax.broadcasted_iota(jnp.int32, (1, 1, columns), 2) % 2
+    signs = jnp.where(parity == 0, 1.0, -1.0).astype(jnp.bfloat16)
+    both_halves = jnp.concatenate([row_both, row_both * signs], axis=0)
+    halves = two_pass("rck,xk->rcx", both_halves, tuple(part[:half_cols] for part in table_pair))
+    spatial = jnp.concatenate([halves[:slab_rows], halves[slab_rows:]], axis=2)
     encoded = (hidden.astype(jnp.float32) + spatial).astype(jnp.bfloat16)
     key_count = key_pixels.shape[0]
     query_count = query_pixels.shape[0]

time: 204 us -> 211 us (1.034)
  other arithmetic: 12.7 us -> 28.1 us
  waiting for transfers between devices: 56.3 us -> 42.6 us
  local copies, waits for them, and re-layouts: 28.5 us -> 33.2 us
  starting transfers between devices: 66.3 us -> 70.5 us
  matrix products: 20.5 us -> 16.4 us
    ppermute x9, waiting for transfers between devices: 27.3 us -> 9.72 us  [ring_pieces(): lax.ppermute(values, axis, [(i, (i + shift) % count) for i in range(count)])]
    convert_element_type x0 -> x4, other arithmetic: none -> 11.8 us  [the longest x1 9.13 us: split_bf16(): high = table.astype(jnp.bfloat16)]
    ppermute x9, starting transfers between devices: 36.7 us -> 43 us  [ring_pieces(): lax.ppermute(values, axis, [(i, (i + shift) % count) for i in range(count)])]
    dot_general x4, matrix products: 16.4 us -> 11.2 us  [two_pass(): jnp.einsum(eq, left, part, preferred_element_type=jnp.float32)]
    all_to_all x1, waiting for transfers between devices: 1.11 us -> 5.04 us  [body(): lax.all_to_all(back.reshape(2, slabs, slab_rows, lanes), 'rows', split_ax...]
  transfers between devices with their start and end apart: 14 -> 14, of which waited for: 7 -> 5; matrix products, arithmetic and copies ran while one was open for 20% -> 35% of each run, Pallas kernels for 0% -> 0%
where the time goes in v5:
time: 211 us; the launch traced here: 210 us
  starting transfers between devices  70.5 us (33%)
  waiting for transfers between devices  42.6 us (20%)
  local copies, waits for them, and re-layouts  33.2 us (16%)
  other arithmetic  28.1 us (13%)
  blocking collectives  17.7 us (8%)
  matrix products  16.4 us (8%)
    ppermute x9, starting transfers between devices, ring_pieces(): lax.ppermute(values, axis, [(i, (i + shift) % count) for i in range(count)])  43 us
    all_to_all x1, blocking collectives, body(): lax.all_to_all(jnp.stack([exp_sums, picked], axis=1).reshape(slabs, quart...  17.7 us
    all_to_all x1, waiting for transfers between devices, body(): lax.all_to_all(jnp.broadcast_to(packet[None], (slabs,) + packet.shape), '...  16.3 us
    all_to_all x1, starting transfers between devices, body(): lax.all_to_all(wire.astype(jnp.bfloat16), 'rows', split_axis=1, concat_ax...  12.4 us
    all_to_all x1, waiting for transfers between devices, body(): lax.all_to_all(wire.astype(jnp.bfloat16), 'rows', split_axis=1, concat_ax...  11.6 us
    dot_general x4, matrix products, two_pass(): jnp.einsum(eq, left, part, preferred_element_type=jnp.float32)  11.2 us
    ppermute x9, waiting for transfers between devices, ring_pieces(): lax.ppermute(values, axis, [(i, (i + shift) % count) for i in range(count)])  9.72 us
    convert_element_type x1, other arithmetic, split_bf16(): high = table.astype(jnp.bfloat16)  9.13 us
  transfers between devices with their start and end apart: 14, of which 5 were waited for; matrix products, arithmetic and copies ran while one was open for 35% of the time, Pallas kernels for 0%

profile of v5, /device:TPU:1, one launch (start us, length us, event | category | flops | bytes accessed | tf_op | source)
XLA Modules:
  0.0 209.8 jit_solution(1680590538420395321)
XLA Ops:
  2.0 5.2 %collective-permute-start.10 = (bf16[24,256]{1,0:T(8,128)(2,1)S(1)}, bf16[24,256]{1,0:T(8,128)(2,1)}, u32[]{:S(2)}, u32[]{:S(2)}) collective-permute-start(bf16[24,256]{1,0:T(8,128)(2,1)S(1)} %constant_dynamic-update-slice_fusion), channel_id=1, source_target_pairs={{0,3},{1,0},{2,1},{3,2},{4,7},{5,4},{6,5},{7,6},{8,11},{9,8},{10,9... | collective-permute-start | bytes 36872 | tf_op jit(solution)/shard_map/ppermute | solution.py:35
  7.2 1.0 fusion.126
  8.2 4.0 %collective-permute-start = (bf16[2,24,2048]{2,1,0:T(8,128)(2,1)S(1)}, bf16[2,24,2048]{2,1,0:T(8,128)(2,1)S(1)}, u32[]{:S(2)}, u32[]{:S(2)}) collective-permute-start(bf16[2,24,2048]{2,1,0:T(8,128)(2,1)S(1)} %get-tuple-element.22), channel_id=1, source_target_pairs={{0,4},{4,8},{8,12},{12,16},{16,20},{20,24},{24,28},{28,32},{32,36}... | collective-permute-start | bytes 589832 | tf_op jit(solution)/shard_map/ppermute | solution.py:21
  12.2 1.9 collective-permute-start.1
  14.1 1.0 fusion.79
  15.8 0.9 fusion.127
  17.0 1.0 bitcast_convert_fusion
  18.0 0.9 copy.71
  18.9 1.0 bitcast_convert_fusion.1
  19.9 0.9 copy.72
  20.8 1.0 slice_bitcast_fusion.14
  21.8 1.3 fusion.32
  23.1 2.3 %fusion.41 = bf16[4,24,2048]{2,1,0:T(8,128)(2,1)S(1)} fusion(bf16[4,24,2048]{2,1,0:T(8,128)(2,1)} %param.10, bf16[8,24,2052]{2,1,0:T(8,128)(2,1)S(1)} %fusion.32, bf16[2,24,2048]{2,1,0:T(8,128)(2,1)S(1)} %collective-permute-done.1, bf16[2,24,2048]{2,1,0:T(8,128)(2,1)S(1)} %collective-permute-done, f32[24]{0:T(128)S(1)} %get-tuple-element.35, ...), kind=kLoop, calls=%fused_computation.59 | loop fusion | flops 5898240 | bytes 3539808 | tf_op jit(solution)/shard_map/convert_element_type | solution.py:147
  25.4 3.8 %collective-permute-start.3 = (bf16[4,24,2048]{2,1,0:T(8,128)(2,1)S(1)}, bf16[4,24,2048]{2,1,0:T(8,128)(2,1)S(1)}, u32[]{:S(2)}, u32[]{:S(2)}) collective-permute-start(bf16[4,24,2048]{2,1,0:T(8,128)(2,1)S(1)} %fusion.41), channel_id=1, source_target_pairs={{0,2},{1,3},{2,0},{3,1},{4,6},{5,7},{6,4},{7,5},{8,10},{9,11},{10,... | collective-permute-start | bytes 1179656 | tf_op jit(solution)/shard_map/ppermute | solution.py:35
  29.3 2.5 %multiply_subtract_fusion = (f32[32,64,1024]{2,1,0:T(8,128)S(1)}, f32[32,64,1024]{2,1,0:T(8,128)S(1)}) fusion(f32[64,1024]{1,0:T(8,128)S(1)} %get-tuple-element.11, f32[32,1024]{1,0:T(8,128)S(1)} %get-tuple-element.10, f32[64,1024]{1,0:T(8,128)S(1)} %get-tuple-element.9, f32[32,1024]{1,0:T(8,128)S(1)} %get-tuple-element.8), kind=kLoop, calls=%fused_computation.9 | loop fusion | flops 14680064 | bytes 17563648 | tf_op jit(solution)/shard_map/sub | solution.py:71
  31.7 2.0 subtract_convert_fusion
  33.7 5.8 %collective-permute-done.2 = bf16[4,24,2048]{2,1,0:T(8,128)(2,1)S(1)} collective-permute-done((bf16[4,24,2048]{2,1,0:T(8,128)(2,1)S(1)}, bf16[4,24,2048]{2,1,0:T(8,128)(2,1)S(1)}, u32[]{:S(2)}, u32[]{:S(2)}) %collective-permute-start.2) | collective-permute-done | bytes 393248 | tf_op jit(solution)/shard_map/ppermute | solution.py:35
  39.6 16.2 %collective-permute-start.9 = (bf16[24,256]{1,0:T(8,128)(2,1)S(1)}, bf16[24,256]{1,0:T(8,128)(2,1)}, u32[]{:S(2)}, u32[]{:S(2)}) collective-permute-start(bf16[24,256]{1,0:T(8,128)(2,1)S(1)} %constant_dynamic-update-slice_fusion), channel_id=1, source_target_pairs={{0,2},{1,3},{2,0},{3,1},{4,6},{5,7},{6,4},{7,5},{8,10},{9,11},{10,... | collective-permute-start | bytes 36872 | tf_op jit(solution)/shard_map/ppermute | solution.py:35
  56.3 1.5 fusion.1
  57.8 2.3 %fusion.10 = bf16[4,24,2048]{2,1,0:T(8,128)(2,1)} fusion(f32[4,24,2048]{2,1,0:T(8,128)S(1)} %fusion.1, bf16[4,24,2048]{2,1,0:T(8,128)(2,1)S(1)} %fusion.51, f32[2048,1024]{1,0:T(8,128)S(1)} %bitcast.77, f32[2048,1024]{1,0:T(8,128)S(1)} %bitcast.74), kind=kOutput, calls=%fused_computation.18 | convolution fusion | flops 822476800 | bytes 18350080 | tf_op jit(solution)/shard_map/rcx,xk->rck/dot_general | solution.py:79
  60.1 3.4 %convert_element_type.155 = bf16[4,24,2,64,16]{4,3,2,1,0:T(8,128)(2,1)S(1)} reshape(bf16[4,24,2048]{2,1,0:T(8,128)(2,1)} %fusion.10) | data formatting | bytes 786432 | tf_op jit(solution)/shard_map/convert_element_type | solution.py:173
  63.5 2.3 %copy.68 = bf16[2,64,4,24,16]{1,4,3,2,0:T(8,128)(2,1)} copy(bf16[2,64,4,24,16]{4,1,0,3,2:T(8,128)(2,1)S(1)} %bitcast.79) | data formatting | bytes 786432 | tf_op jit(solution)/shard_map/convert_element_type | solution.py:173
  65.8 2.3 %copy.69 = bf16[2,64,4,384]{3,2,0,1:T(4,128)(2,1)} copy(bf16[2,64,4,384]{1,3,2,0:T(8,128)(2,1)} %bitcast.80) | data formatting | bytes 786432 | tf_op jit(solution)/shard_map/convert_element_type | solution.py:173
  68.0 12.4 %all-to-all-start = ((bf16[2,64,4,384]{3,2,0,1:T(4,128)(2,1)}), bf16[2,64,4,384]{3,2,0,1:T(4,128)(2,1)S(1)}, u32[]{:S(2)}, u32[]{:S(2)}) async-start(bf16[2,64,4,384]{3,2,0,1:T(4,128)(2,1)} %copy.69), calls=%async_computation | async-start | bytes 786432 | tf_op jit(solution)/shard_map/all_to_all | solution.py:172
  81.7 1.0 fusion.78
  82.7 1.0 broadcast_multiply_fusion.2
  83.7 11.6 %all-to-all-done = bf16[2,64,4,384]{3,2,0,1:T(4,128)(2,1)S(1)} async-done(((bf16[2,64,4,384]{3,2,0,1:T(4,128)(2,1)}), bf16[2,64,4,384]{3,2,0,1:T(4,128)(2,1)S(1)}, u32[]{:S(2)}, u32[]{:S(2)}) %all-to-all-start) | async-done | bytes 393248 | tf_op jit(solution)/shard_map/all_to_all | solution.py:172
  96.6 2.8 %fusion.22 = bf16[512,384]{1,0:T(8,128)(2,1)S(1)} fusion(f32[256,256]{1,0:T(8,128)S(1)} %fusion.78, f32[256,256]{1,0:T(8,128)} %copy-done.7, f32[256,256]{1,0:T(8,128)} %copy-done.6, f32[256,384]{1,0:T(8,128)S(1)} %get-tuple-element.17, f32[256,384]{1,0:T(8,128)S(1)} %get-tuple-element.16), kind=kOutput, calls=%fused_computation.35 | convolution fusion | flops 1209335808 | bytes 1966080 | tf_op jit(solution)/shard_map/ym,mn->yn/dot_general | solution.py:192
  99.5 0.9 copy.75
  100.4 4.6 %all-to-all-start.1 = ((bf16[2,64,4,384]{3,2,0,1:T(4,128)(2,1)}), bf16[2,64,4,384]{3,2,0,1:T(4,128)(2,1)S(1)}, u32[]{:S(2)}, u32[]{:S(2)}) async-start(bf16[2,64,4,384]{3,2,0,1:T(4,128)(2,1)} %copy.75), calls=%async_computation.1 | async-start | bytes 786432 | tf_op jit(solution)/shard_map/all_to_all | solution.py:197
  105.7 9.1 %fusion = bf16[2048,2048]{1,0:T(8,128)(2,1)} fusion(f32[2048,1024]{1,0:T(8,128)} %bitcast.78, f32[2048,1024]{1,0:T(8,128)} %bitcast.75), kind=kLoop, calls=%fused_computation.3 | loop fusion | flops 16777216 | bytes 25165824 | tf_op jit(solution)/shard_map/convert_element_type | solution.py:50
  114.8 5.0 %all-to-all-done.1 = bf16[2,64,4,384]{3,2,0,1:T(4,128)(2,1)S(1)} async-done(((bf16[2,64,4,384]{3,2,0,1:T(4,128)(2,1)}), bf16[2,64,4,384]{3,2,0,1:T(4,128)(2,1)S(1)}, u32[]{:S(2)}, u32[]{:S(2)}) %all-to-all-start.1) | async-done | bytes 393248 | tf_op jit(solution)/shard_map/all_to_all | solution.py:197
  119.9 1.4 copy.76
  121.2 3.0 %copy.77 = bf16[4,24,2,64,16]{4,3,2,1,0:T(8,128)(2,1)S(1)} copy(bf16[4,24,2,64,16]{3,4,1,0,2:T(8,128)(2,1)} %bitcast.81) | data formatting | bytes 786432 | tf_op jit(solution)/shard_map/transpose | solution.py:200
  124.2 6.1 %reshape.364 = bf16[4,24,2048]{2,1,0:T(8,128)(2,1)} reshape(bf16[4,24,2,64,16]{4,3,2,1,0:T(8,128)(2,1)S(1)} %copy.77) | data formatting | bytes 786432 | tf_op jit(solution)/shard_map/reshape | solution.py:200
  130.3 1.0 broadcast_multiply_fusion.1
  132.0 3.7 %fusion.5 = f32[8,24,1024]{2,1,0:T(8,128)S(1)} fusion(bf16[2048,2048]{1,0:T(8,128)(2,1)} %copy-done.2, bf16[4,24,2048]{2,1,0:T(8,128)(2,1)S(1)} %broadcast_multiply_fusion, bf16[4,24,2048]{2,1,0:T(8,128)(2,1)S(1)} %broadcast_multiply_fusion.1), kind=kOutput, calls=%fused_computation.11 | convolution fusion | flops 805699584 | bytes 5767168 | tf_op jit(solution)/shard_map/rck,xk->rcx/dot_general | solution.py:79
  135.8 3.7 %fusion.21 = f32[8,24,1024]{2,1,0:T(8,128)S(1)} fusion(f32[8,24,1024]{2,1,0:T(8,128)S(1)} %fusion.5, bf16[2048,2048]{1,0:T(8,128)(2,1)} %fusion, bf16[4,24,2048]{2,1,0:T(8,128)(2,1)S(1)} %broadcast_multiply_fusion, bf16[4,24,2048]{2,1,0:T(8,128)(2,1)S(1)} %broadcast_multiply_fusion.1), kind=kOutput, calls=%fused_computation.34 | convolution fusion | flops 805896192 | bytes 6553600 | tf_op jit(solution)/shard_map/rck,xk->rcx/dot_general | solution.py:79
  139.7 1.1 copy.78
  140.8 4.9 %gather_fusion = bf16[320,24]{1,0:T(8,128)(2,1)S(1)} fusion(bf16[4,24,2048]{1,2,0:T(8,128)(2,1)S(1)} %copy.78, s32[320]{0:T(512)S(1)} %fusion.112), kind=kCustom, calls=%fused_computation | custom fusion | bytes 33280 | tf_op jit(solution)/shard_map/gather | solution.py:218
  145.6 15.5 %collective-permute-start.5 = (bf16[320,24]{1,0:T(8,128)(2,1)S(1)}, bf16[320,24]{1,0:T(8,128)(2,1)S(1)}, u32[]{:S(2)}, u32[]{:S(2)}) collective-permute-start(bf16[320,24]{1,0:T(8,128)(2,1)S(1)} %gather_fusion), channel_id=1, source_target_pairs={{0,1},{1,2},{2,3},{3,0},{4,5},{5,6},{6,7},{7,4},{8,9},{9,10},{10,1... | collective-permute-start | bytes 46088 | tf_op jit(solution)/shard_map/ppermute | solution.py:35
  161.2 2.2 %collective-permute-start.7 = (bf16[320,24]{1,0:T(8,128)(2,1)S(1)}, bf16[320,24]{1,0:T(8,128)(2,1)S(1)}, u32[]{:S(2)}, u32[]{:S(2)}) collective-permute-start(bf16[320,24]{1,0:T(8,128)(2,1)S(1)} %gather_fusion), channel_id=1, source_target_pairs={{0,3},{1,0},{2,1},{3,2},{4,7},{5,4},{6,5},{7,6},{8,11},{9,8},{10,9... | collective-permute-start | bytes 46088 | tf_op jit(solution)/shard_map/ppermute | solution.py:35
  163.3 0.7 pad_maximum_fusion.13
  164.1 3.9 %collective-permute-done.6 = bf16[320,24]{1,0:T(8,128)(2,1)S(1)} collective-permute-done((bf16[320,24]{1,0:T(8,128)(2,1)S(1)}, bf16[320,24]{1,0:T(8,128)(2,1)S(1)}, u32[]{:S(2)}, u32[]{:S(2)}) %collective-permute-start.6) | collective-permute-done | bytes 15392 | tf_op jit(solution)/shard_map/ppermute | solution.py:35
  168.5 0.8 broadcast_in_dim.41
  169.3 4.7 %all-to-all-start.2 = ((bf16[64,17,128]{2,1,0:T(8,128)(2,1)}), bf16[64,17,128]{2,1,0:T(8,128)(2,1)S(1)}, u32[]{:S(2)}, u32[]{:S(2)}) async-start(bf16[64,17,128]{2,1,0:T(8,128)(2,1)} %broadcast_in_dim.41), calls=%async_computation.2 | async-start | bytes 786432 | tf_op jit(solution)/shard_map/all_to_all | solution.py:232
  174.2 16.3 %all-to-all-done.2 = bf16[64,17,128]{2,1,0:T(8,128)(2,1)S(1)} async-done(((bf16[64,17,128]{2,1,0:T(8,128)(2,1)}), bf16[64,17,128]{2,1,0:T(8,128)(2,1)S(1)}, u32[]{:S(2)}, u32[]{:S(2)}) %all-to-all-start.2) | async-done | bytes 278560 | tf_op jit(solution)/shard_map/all_to_all | solution.py:232
  191.4 17.7 %all_to_all.20 = f32[64,16,2]{1,2,0:T(2,128)S(1)} all-to-all(f32[64,16,2]{1,2,0:T(2,128)S(1)} %copy.79), channel_id=1, replica_groups=mesh['rows'=64,'ch'=4] {'rows'}, dimensions={0} | all-to-all | bytes 16384 | tf_op jit(solution)/shard_map/all_to_all | solution.py:249
  (79 shorter events, 9.2 us)
Async XLA Ops:
  2.0 159.1 %collective-permute-start.10 = (bf16[24,256]{1,0:T(8,128)(2,1)S(1)}, bf16[24,256]{1,0:T(8,128)(2,1)}, u32[]{:S(2)}, u32[]{:S(2)}) collective-permute-start(bf16[24,256]{1,0:T(8,128)(2,1)S(1)} %constant_dynamic-update-slice_fusion), channel_id=1, source_target_pairs={{0,3},{1,0},{2,1},{3,2},{4,7},{5,4},{6,5},{7,6},{8,11},{9,8},{10,9... | collective-permute-start | bytes 36872 | tf_op jit(solution)/shard_map/ppermute | solution.py:35
  7.2 156.2 %collective-permute-start.8 = (bf16[24,256]{1,0:T(8,128)(2,1)S(1)}, bf16[24,256]{1,0:T(8,128)(2,1)}, u32[]{:S(2)}, u32[]{:S(2)}) collective-permute-start(bf16[24,256]{1,0:T(8,128)(2,1)S(1)} %constant_dynamic-update-slice_fusion), channel_id=1, source_target_pairs={{0,1},{1,2},{2,3},{3,0},{4,5},{5,6},{6,7},{7,4},{8,9},{9,10},{10,1... | collective-permute-start | bytes 36872 | tf_op jit(solution)/shard_map/ppermute | solution.py:35
  8.2 13.5 %collective-permute-start = (bf16[2,24,2048]{2,1,0:T(8,128)(2,1)S(1)}, bf16[2,24,2048]{2,1,0:T(8,128)(2,1)S(1)}, u32[]{:S(2)}, u32[]{:S(2)}) collective-permute-start(bf16[2,24,2048]{2,1,0:T(8,128)(2,1)S(1)} %get-tuple-element.22), channel_id=1, source_target_pairs={{0,4},{4,8},{8,12},{12,16},{16,20},{20,24},{24,28},{28,32},{32,36}... | collective-permute-start | bytes 589832 | tf_op jit(solution)/shard_map/ppermute | solution.py:21
  12.2 9.6 %collective-permute-start.1 = (bf16[2,24,2048]{2,1,0:T(8,128)(2,1)S(1)}, bf16[2,24,2048]{2,1,0:T(8,128)(2,1)S(1)}, u32[]{:S(2)}, u32[]{:S(2)}) collective-permute-start(bf16[2,24,2048]{2,1,0:T(8,128)(2,1)S(1)} %get-tuple-element.23), channel_id=1, source_target_pairs={{4,0},{8,4},{12,8},{16,12},{20,16},{24,20},{28,24},{32,28},{36,32}... | collective-permute-start | bytes 589832 | tf_op jit(solution)/shard_map/ppermute | solution.py:23
  25.4 14.2 %collective-permute-start.2 = (bf16[4,24,2048]{2,1,0:T(8,128)(2,1)S(1)}, bf16[4,24,2048]{2,1,0:T(8,128)(2,1)S(1)}, u32[]{:S(2)}, u32[]{:S(2)}) collective-permute-start(bf16[4,24,2048]{2,1,0:T(8,128)(2,1)S(1)} %fusion.41), channel_id=1, source_target_pairs={{0,1},{1,2},{2,3},{3,0},{4,5},{5,6},{6,7},{7,4},{8,9},{9,10},{10,1... | collective-permute-start | bytes 1179656 | tf_op jit(solution)/shard_map/ppermute | solution.py:35
  25.4 30.3 %collective-permute-start.3 = (bf16[4,24,2048]{2,1,0:T(8,128)(2,1)S(1)}, bf16[4,24,2048]{2,1,0:T(8,128)(2,1)S(1)}, u32[]{:S(2)}, u32[]{:S(2)}) collective-permute-start(bf16[4,24,2048]{2,1,0:T(8,128)(2,1)S(1)} %fusion.41), channel_id=1, source_target_pairs={{0,2},{1,3},{2,0},{3,1},{4,6},{5,7},{6,4},{7,5},{8,10},{9,11},{10,... | collective-permute-start | bytes 1179656 | tf_op jit(solution)/shard_map/ppermute | solution.py:35
  29.3 26.5 %collective-permute-start.4 = (bf16[4,24,2048]{2,1,0:T(8,128)(2,1)S(1)}, bf16[4,24,2048]{2,1,0:T(8,128)(2,1)S(1)}, u32[]{:S(2)}, u32[]{:S(2)}) collective-permute-start(bf16[4,24,2048]{2,1,0:T(8,128)(2,1)S(1)} %fusion.41), channel_id=1, source_target_pairs={{0,3},{1,0},{2,1},{3,2},{4,7},{5,4},{6,5},{7,6},{8,11},{9,8},{10,9... | collective-permute-start | bytes 1179656 | tf_op jit(solution)/shard_map/ppermute | solution.py:35
  31.7 26.1 %copy-start = (f32[32,64,1024]{2,1,0:T(8,128)}, f32[32,64,1024]{2,1,0:T(8,128)S(1)}, u32[]{:S(2)}) copy-start(f32[32,64,1024]{2,1,0:T(8,128)S(1)} %get-tuple-element.20) | copy-start | bytes 25165828
  31.7 26.1 %copy-start.1 = (f32[32,64,1024]{2,1,0:T(8,128)}, f32[32,64,1024]{2,1,0:T(8,128)S(1)}, u32[]{:S(2)}) copy-start(f32[32,64,1024]{2,1,0:T(8,128)S(1)} %get-tuple-element.21) | copy-start | bytes 25165828
  33.7 22.6 %copy-start.2 = (bf16[2048,2048]{1,0:T(8,128)(2,1)}, bf16[2048,2048]{1,0:T(8,128)(2,1)S(1)}, u32[]{:S(2)}) copy-start(bf16[2048,2048]{1,0:T(8,128)(2,1)S(1)} %subtract_convert_fusion) | copy-start | bytes 25165828
  39.6 123.8 %collective-permute-start.9 = (bf16[24,256]{1,0:T(8,128)(2,1)S(1)}, bf16[24,256]{1,0:T(8,128)(2,1)}, u32[]{:S(2)}, u32[]{:S(2)}) collective-permute-start(bf16[24,256]{1,0:T(8,128)(2,1)S(1)} %constant_dynamic-update-slice_fusion), channel_id=1, source_target_pairs={{0,2},{1,3},{2,0},{3,1},{4,6},{5,7},{6,4},{7,5},{8,10},{9,11},{10,... | collective-permute-start | bytes 36872 | tf_op jit(solution)/shard_map/ppermute | solution.py:35
  60.1 20.3 %copy-start.10 = (s32[64]{0:T(128)S(1)}, s32[64]{0:T(128)}, u32[]{:S(2)}) copy-start(s32[64]{0:T(128)} %param.19) | copy-start | bytes 772
  65.8 30.7 %copy-start.3 = (f32[256,384]{1,0:T(8,128)S(1)}, f32[256,384]{1,0:T(8,128)}, u32[]{:S(2)}) copy-start(f32[256,384]{1,0:T(8,128)} %copy.71) | copy-start | bytes 1179652
  65.8 30.7 %copy-start.4 = (f32[256,384]{1,0:T(8,128)S(1)}, f32[256,384]{1,0:T(8,128)}, u32[]{:S(2)}) copy-start(f32[256,384]{1,0:T(8,128)} %copy.72) | copy-start | bytes 1179652
  68.0 37.0 %copy-start.8 = (s32[256]{0:T(256)S(1)}, s32[256]{0:T(256)}, u32[]{:S(2)}) copy-start(s32[256]{0:T(256)} %param.18) | copy-start | bytes 3076
  68.0 37.0 %copy-start.9 = (s32[64]{0:T(128)S(1)}, s32[64]{0:T(128)}, u32[]{:S(2)}) copy-start(s32[64]{0:T(128)} %param.17) | copy-start | bytes 772
  68.0 27.3 %all-to-all-start = ((bf16[2,64,4,384]{3,2,0,1:T(4,128)(2,1)}), bf16[2,64,4,384]{3,2,0,1:T(4,128)(2,1)S(1)}, u32[]{:S(2)}, u32[]{:S(2)}) async-start(bf16[2,64,4,384]{3,2,0,1:T(4,128)(2,1)} %copy.69), calls=%async_computation | async-start | bytes 786432 | tf_op jit(solution)/shard_map/all_to_all | solution.py:172
  83.7 12.3 %copy-start.6 = (f32[256,256]{1,0:T(8,128)}, f32[256,256]{1,0:T(8,128)S(1)}, u32[]{:S(2)}) copy-start(f32[256,256]{1,0:T(8,128)S(1)} %get-tuple-element.45) | copy-start | bytes 786436
  83.7 12.3 %copy-start.7 = (f32[256,256]{1,0:T(8,128)}, f32[256,256]{1,0:T(8,128)S(1)}, u32[]{:S(2)}) copy-start(f32[256,256]{1,0:T(8,128)S(1)} %get-tuple-element.46) | copy-start | bytes 786436
  100.4 19.5 %all-to-all-start.1 = ((bf16[2,64,4,384]{3,2,0,1:T(4,128)(2,1)}), bf16[2,64,4,384]{3,2,0,1:T(4,128)(2,1)S(1)}, u32[]{:S(2)}, u32[]{:S(2)}) async-start(bf16[2,64,4,384]{3,2,0,1:T(4,128)(2,1)} %copy.75), calls=%async_computation.1 | async-start | bytes 786432 | tf_op jit(solution)/shard_map/all_to_all | solution.py:197
  135.7 32.7 %copy-start.11 = (bf16[1,128]{1,0:T(2,128)(2,1)S(1)}, bf16[1,128]{1,0:T(2,128)(2,1)}, u32[]{:S(2)}) copy-start(bf16[1,128]{1,0:T(2,128)(2,1)} %fusion.115) | copy-start | bytes 772
  139.7 70.1 %copy-start.5 = (bf16[4,24,2048]{2,1,0:T(8,128)(2,1)}, bf16[4,24,2048]{2,1,0:T(8,128)(2,1)S(1)}, u32[]{:S(2)}) copy-start(bf16[4,24,2048]{2,1,0:T(8,128)(2,1)S(1)} %fusion.57) | copy-start | bytes 1179652
  145.6 18.4 %collective-permute-start.5 = (bf16[320,24]{1,0:T(8,128)(2,1)S(1)}, bf16[320,24]{1,0:T(8,128)(2,1)S(1)}, u32[]{:S(2)}, u32[]{:S(2)}) collective-permute-start(bf16[320,24]{1,0:T(8,128)(2,1)S(1)} %gather_fusion), channel_id=1, source_target_pairs={{0,1},{1,2},{2,3},{3,0},{4,5},{5,6},{6,7},{7,4},{8,9},{9,10},{10,1... | collective-permute-start | bytes 46088 | tf_op jit(solution)/shard_map/ppermute | solution.py:35
  161.2 6.8 %collective-permute-start.6 = (bf16[320,24]{1,0:T(8,128)(2,1)S(1)}, bf16[320,24]{1,0:T(8,128)(2,1)S(1)}, u32[]{:S(2)}, u32[]{:S(2)}) collective-permute-start(bf16[320,24]{1,0:T(8,128)(2,1)S(1)} %gather_fusion), channel_id=1, source_target_pairs={{0,2},{1,3},{2,0},{3,1},{4,6},{5,7},{6,4},{7,5},{8,10},{9,11},{10,... | collective-permute-start | bytes 46088 | tf_op jit(solution)/shard_map/ppermute | solution.py:35
  161.2 6.8 %collective-permute-start.7 = (bf16[320,24]{1,0:T(8,128)(2,1)S(1)}, bf16[320,24]{1,0:T(8,128)(2,1)S(1)}, u32[]{:S(2)}, u32[]{:S(2)}) collective-permute-start(bf16[320,24]{1,0:T(8,128)(2,1)S(1)} %gather_fusion), channel_id=1, source_target_pairs={{0,3},{1,0},{2,1},{3,2},{4,7},{5,4},{6,5},{7,6},{8,11},{9,8},{10,9... | collective-permute-start | bytes 46088 | tf_op jit(solution)/shard_map/ppermute | solution.py:35
  169.3 21.3 %all-to-all-start.2 = ((bf16[64,17,128]{2,1,0:T(8,128)(2,1)}), bf16[64,17,128]{2,1,0:T(8,128)(2,1)S(1)}, u32[]{:S(2)}, u32[]{:S(2)}) async-start(bf16[64,17,128]{2,1,0:T(8,128)(2,1)} %broadcast_in_dim.41), calls=%async_computation.2 | async-start | bytes 786432 | tf_op jit(solution)/shard_map/all_to_all | solution.py:232

commit v6 on v3

--- a/solution.py
+++ b/solution.py
@@ -211,7 +211,12 @@
         ring_pieces(jnp.concatenate([key_weight, query_weight], axis=1), "ch"), axis=0
     )
     sampled = jnp.concatenate([key_pixels, query_pixels])
-    features = encoded[sampled // columns, :, sampled % columns]
+    places = lax.broadcasted_iota(jnp.int32, (1, slab_rows, columns), 1) * columns
+    places = places + lax.broadcasted_iota(jnp.int32, (1, slab_rows, columns), 2)
+    chosen = (sampled[:, None, None] == places).astype(jnp.bfloat16)
+    features = jnp.einsum(
+        "npx,pcx->nc", chosen, encoded, preferred_element_type=jnp.float32
+    ).astype(jnp.bfloat16)
     features = jnp.concatenate(ring_pieces(features, "ch"), axis=1)
     key_dim = key_weight.shape[1]
     key_unit = unit_rows(

time: 204 us -> 204 us (level)
  waiting for transfers between devices: 56.3 us -> 48.8 us
  starting transfers between devices: 66.3 us -> 70.8 us
  local copies, waits for them, and re-layouts: 28.5 us -> 24.6 us
  matrix products: 20.5 us -> 23.2 us
  other arithmetic: 12.7 us -> 15.1 us
  blocking collectives: 17.6 us -> 19.8 us
    ppermute x9, waiting for transfers between devices: 27.3 us -> 9.43 us  [ring_pieces(): lax.ppermute(values, axis, [(i, (i + shift) % count) for i in range(count)])]
    all_to_all x1, waiting for transfers between devices: 1.11 us -> 13 us  [body(): lax.all_to_all(back.reshape(2, slabs, slab_rows, lanes), 'rows', split_ax...]
    ppermute x9, starting transfers between devices: 36.7 us -> 42 us  [ring_pieces(): lax.ppermute(values, axis, [(i, (i + shift) % count) for i in range(count)])]
    gather x1 -> x0, local copies, waits for them, and re-layouts: 4.87 us -> none  [body(): features = encoded[sampled // columns, :, sampled % columns]]
    all_to_all x1, blocking collectives: 17.6 us -> 19.8 us  [body(): lax.all_to_all(jnp.stack([exp_sums, picked], axis=1).reshape(slabs, quart...]
  transfers between devices with their start and end apart: 14 -> 14, of which waited for: 7 -> 6; matrix products, arithmetic and copies ran while one was open for 20% -> 29% of each run, Pallas kernels for 0% -> 0%
where the time goes in v6:
time: 204 us; the launch traced here: 203 us
  starting transfers between devices  70.8 us (35%)
  waiting for transfers between devices  48.8 us (24%)
  local copies, waits for them, and re-layouts  24.6 us (12%)
  matrix products  23.2 us (11%)
  blocking collectives  19.8 us (10%)
  other arithmetic  15.1 us (7%)
    ppermute x9, starting transfers between devices, ring_pieces(): lax.ppermute(values, axis, [(i, (i + shift) % count) for i in range(count)])  42 us
    all_to_all x1, blocking collectives, body(): lax.all_to_all(jnp.stack([exp_sums, picked], axis=1).reshape(slabs, quart...  19.8 us
    dot_general x4, matrix products, two_pass(): jnp.einsum(eq, left, part, preferred_element_type=jnp.float32)  17.1 us
    all_to_all x1, waiting for transfers between devices, body(): lax.all_to_all(jnp.broadcast_to(packet[None], (slabs,) + packet.shape), '...  14.7 us
    all_to_all x1, waiting for transfers between devices, body(): lax.all_to_all(back.reshape(2, slabs, slab_rows, lanes), 'rows', split_ax...  13 us
    all_to_all x1, starting transfers between devices, body(): lax.all_to_all(wire.astype(jnp.bfloat16), 'rows', split_axis=1, concat_ax...  12.4 us
    all_to_all x1, waiting for transfers between devices, body(): lax.all_to_all(wire.astype(jnp.bfloat16), 'rows', split_axis=1, concat_ax...  11.4 us
    ppermute x9, waiting for transfers between devices, ring_pieces(): lax.ppermute(values, axis, [(i, (i + shift) % count) for i in range(count)])  9.43 us
  transfers between devices with their start and end apart: 14, of which 6 were waited for; matrix products, arithmetic and copies ran while one was open for 29% of the time, Pallas kernels for 0%

profile of v6, /device:TPU:1, one launch (start us, length us, event | category | flops | bytes accessed | tf_op | source)
XLA Modules:
  0.0 203.4 jit_solution(14258131277883104593)
XLA Ops:
  0.6 0.7 constant_dynamic-update-slice_fusion.1
  1.3 0.7 constant_dynamic-update-slice_fusion
  2.0 5.2 %collective-permute-start.10 = (bf16[24,256]{1,0:T(8,128)(2,1)S(1)}, bf16[24,256]{1,0:T(8,128)(2,1)}, u32[]{:S(2)}, u32[]{:S(2)}) collective-permute-start(bf16[24,256]{1,0:T(8,128)(2,1)S(1)} %constant_dynamic-update-slice_fusion), channel_id=1, source_target_pairs={{0,3},{1,0},{2,1},{3,2},{4,7},{5,4},{6,5},{7,6},{8,11},{9,8},{10,9... | collective-permute-start | bytes 36872 | tf_op jit(solution)/shard_map/ppermute | solution.py:35
  7.2 1.0 fusion.123
  8.2 4.0 %collective-permute-start = (bf16[2,24,2048]{2,1,0:T(8,128)(2,1)S(1)}, bf16[2,24,2048]{2,1,0:T(8,128)(2,1)S(1)}, u32[]{:S(2)}, u32[]{:S(2)}) collective-permute-start(bf16[2,24,2048]{2,1,0:T(8,128)(2,1)S(1)} %get-tuple-element.20), channel_id=1, source_target_pairs={{0,4},{4,8},{8,12},{12,16},{16,20},{20,24},{24,28},{28,32},{32,36}... | collective-permute-start | bytes 589832 | tf_op jit(solution)/shard_map/ppermute | solution.py:21
  12.2 1.9 collective-permute-start.1
  14.1 1.0 fusion.86
  15.2 0.5 fusion.92
  15.8 0.9 fusion.124
  17.0 1.0 bitcast_convert_fusion
  18.0 1.0 slice_bitcast_fusion.8
  19.2 1.3 fusion.40
  20.5 2.3 %fusion.49 = bf16[4,24,2048]{2,1,0:T(8,128)(2,1)S(1)} fusion(bf16[4,24,2048]{2,1,0:T(8,128)(2,1)} %param.10, bf16[8,24,2052]{2,1,0:T(8,128)(2,1)S(1)} %fusion.40, bf16[2,24,2048]{2,1,0:T(8,128)(2,1)S(1)} %collective-permute-done.1, bf16[2,24,2048]{2,1,0:T(8,128)(2,1)S(1)} %collective-permute-done, f32[24]{0:T(128)S(1)} %get-tuple-element.33, ...), kind=kLoop, calls=%fused_computation.62 | loop fusion | flops 5898240 | bytes 3539808 | tf_op jit(solution)/shard_map/convert_element_type | solution.py:147
  22.9 3.8 %collective-permute-start.3 = (bf16[4,24,2048]{2,1,0:T(8,128)(2,1)S(1)}, bf16[4,24,2048]{2,1,0:T(8,128)(2,1)S(1)}, u32[]{:S(2)}, u32[]{:S(2)}) collective-permute-start(bf16[4,24,2048]{2,1,0:T(8,128)(2,1)S(1)} %fusion.49), channel_id=1, source_target_pairs={{0,2},{1,3},{2,0},{3,1},{4,6},{5,7},{6,4},{7,5},{8,10},{9,11},{10,... | collective-permute-start | bytes 1179656 | tf_op jit(solution)/shard_map/ppermute | solution.py:35
  26.7 2.5 %multiply_subtract_fusion = (f32[32,64,1024]{2,1,0:T(8,128)S(1)}, f32[32,64,1024]{2,1,0:T(8,128)S(1)}) fusion(f32[64,1024]{1,0:T(8,128)S(1)} %get-tuple-element.11, f32[32,1024]{1,0:T(8,128)S(1)} %get-tuple-element.10, f32[64,1024]{1,0:T(8,128)S(1)} %get-tuple-element.9, f32[32,1024]{1,0:T(8,128)S(1)} %get-tuple-element.8), kind=kLoop, calls=%fused_computation.8 | loop fusion | flops 14680064 | bytes 17563648 | tf_op jit(solution)/shard_map/sub | solution.py:71
  29.2 8.8 %collective-permute-done.2 = bf16[4,24,2048]{2,1,0:T(8,128)(2,1)S(1)} collective-permute-done((bf16[4,24,2048]{2,1,0:T(8,128)(2,1)S(1)}, bf16[4,24,2048]{2,1,0:T(8,128)(2,1)S(1)}, u32[]{:S(2)}, u32[]{:S(2)}) %collective-permute-start.2) | collective-permute-done | bytes 393248 | tf_op jit(solution)/shard_map/ppermute | solution.py:35
  38.0 15.2 %collective-permute-start.9 = (bf16[24,256]{1,0:T(8,128)(2,1)S(1)}, bf16[24,256]{1,0:T(8,128)(2,1)}, u32[]{:S(2)}, u32[]{:S(2)}) collective-permute-start(bf16[24,256]{1,0:T(8,128)(2,1)S(1)} %constant_dynamic-update-slice_fusion), channel_id=1, source_target_pairs={{0,2},{1,3},{2,0},{3,1},{4,6},{5,7},{6,4},{7,5},{8,10},{9,11},{10,... | collective-permute-start | bytes 36872 | tf_op jit(solution)/shard_map/ppermute | solution.py:35
  53.7 1.5 fusion.23
  55.2 2.2 %fusion.8 = bf16[4,24,2048]{2,1,0:T(8,128)(2,1)} fusion(f32[4,24,2048]{2,1,0:T(8,128)S(1)} %fusion.23, bf16[4,24,2048]{2,1,0:T(8,128)(2,1)S(1)} %fusion.59, f32[2048,1024]{1,0:T(8,128)S(1)} %bitcast.75, f32[2048,1024]{1,0:T(8,128)S(1)} %bitcast.69), kind=kOutput, calls=%fused_computation.17 | convolution fusion | flops 826671104 | bytes 18350080 | tf_op jit(solution)/shard_map/rcx,xk->rck/dot_general | solution.py:79
  57.5 3.4 %convert_element_type.151 = bf16[4,24,2,64,16]{4,3,2,1,0:T(8,128)(2,1)S(1)} reshape(bf16[4,24,2048]{2,1,0:T(8,128)(2,1)} %fusion.8) | data formatting | bytes 786432 | tf_op jit(solution)/shard_map/convert_element_type | solution.py:173
  60.9 2.2 %copy.63 = bf16[2,64,4,24,16]{1,4,3,2,0:T(8,128)(2,1)} copy(bf16[2,64,4,24,16]{4,1,0,3,2:T(8,128)(2,1)S(1)} %bitcast.78) | data formatting | bytes 786432 | tf_op jit(solution)/shard_map/convert_element_type | solution.py:173
  63.1 2.2 %copy.64 = bf16[2,64,4,384]{3,2,0,1:T(4,128)(2,1)} copy(bf16[2,64,4,384]{1,3,2,0:T(8,128)(2,1)} %bitcast.79) | data formatting | bytes 786432 | tf_op jit(solution)/shard_map/convert_element_type | solution.py:173
  65.3 12.4 %all-to-all-start = ((bf16[2,64,4,384]{3,2,0,1:T(4,128)(2,1)}), bf16[2,64,4,384]{3,2,0,1:T(4,128)(2,1)S(1)}, u32[]{:S(2)}, u32[]{:S(2)}) async-start(bf16[2,64,4,384]{3,2,0,1:T(4,128)(2,1)} %copy.64), calls=%async_computation | async-start | bytes 786432 | tf_op jit(solution)/shard_map/all_to_all | solution.py:172
  77.7 1.0 bitcast_convert_fusion.1
  79.1 1.0 fusion.85
  80.1 1.0 broadcast_multiply_fusion.1
  81.1 11.4 %all-to-all-done = bf16[2,64,4,384]{3,2,0,1:T(4,128)(2,1)S(1)} async-done(((bf16[2,64,4,384]{3,2,0,1:T(4,128)(2,1)}), bf16[2,64,4,384]{3,2,0,1:T(4,128)(2,1)S(1)}, u32[]{:S(2)}, u32[]{:S(2)}) %all-to-all-start) | async-done | bytes 393248 | tf_op jit(solution)/shard_map/all_to_all | solution.py:172
  93.8 1.8 fusion.18
  95.7 0.9 copy.70
  96.6 4.6 %all-to-all-start.1 = ((bf16[2,64,4,384]{3,2,0,1:T(4,128)(2,1)}), bf16[2,64,4,384]{3,2,0,1:T(4,128)(2,1)S(1)}, u32[]{:S(2)}, u32[]{:S(2)}) async-start(bf16[2,64,4,384]{3,2,0,1:T(4,128)(2,1)} %copy.70), calls=%async_computation.1 | async-start | bytes 786432 | tf_op jit(solution)/shard_map/all_to_all | solution.py:197
  101.2 0.6 fusion.112
  101.8 0.6 pad_add_fusion
  102.4 0.7 iota_add_fusion
  103.1 13.0 %all-to-all-done.1 = bf16[2,64,4,384]{3,2,0,1:T(4,128)(2,1)S(1)} async-done(((bf16[2,64,4,384]{3,2,0,1:T(4,128)(2,1)}), bf16[2,64,4,384]{3,2,0,1:T(4,128)(2,1)S(1)}, u32[]{:S(2)}, u32[]{:S(2)}) %all-to-all-start.1) | async-done | bytes 393248 | tf_op jit(solution)/shard_map/all_to_all | solution.py:197
  116.1 1.3 copy.71
  117.3 2.8 %copy.72 = bf16[4,24,2,64,16]{4,3,2,1,0:T(8,128)(2,1)S(1)} copy(bf16[4,24,2,64,16]{3,4,1,0,2:T(8,128)(2,1)} %bitcast.80) | data formatting | bytes 786432 | tf_op jit(solution)/shard_map/transpose | solution.py:200
  120.2 5.4 %reshape.140 = bf16[4,24,2048]{2,1,0:T(8,128)(2,1)S(1)} reshape(bf16[4,24,2,64,16]{4,3,2,1,0:T(8,128)(2,1)S(1)} %copy.72) | data formatting | bytes 786432 | tf_op jit(solution)/shard_map/reshape | solution.py:200
  125.6 8.3 %fusion.21 = f32[4,24,2048]{2,1,0:T(8,128)S(1)} fusion(bf16[4,24,2048]{2,1,0:T(8,128)(2,1)S(1)} %broadcast_multiply_fusion, f32[2048,1024]{1,0:T(8,128)} %bitcast.76, f32[2048,1024]{1,0:T(8,128)} %bitcast.70), kind=kOutput, calls=%fused_computation.35 | convolution fusion | flops 822083584 | bytes 17956864 | tf_op jit(solution)/shard_map/rck,xk->rcx/dot_general | solution.py:79
  134.0 5.1 %fusion.9 = bf16[4,24,2048]{2,1,0:T(8,128)(2,1)S(1)} fusion(f32[4,24,2048]{2,1,0:T(8,128)S(1)} %fusion.21, bf16[4,24,2048]{2,1,0:T(8,128)(2,1)S(1)} %broadcast_multiply_fusion, f32[2048,1024]{1,0:T(8,128)} %bitcast.77, f32[2048,1024]{1,0:T(8,128)S(1)} %bitcast.73, bf16[4,24,2048]{2,1,0:T(8,128)(2,1)S(1)} %copy-done.3), kind=kOutput, calls=%fused_computation.18 | convolution fusion | flops 827064320 | bytes 18743296 | tf_op jit(solution)/shard_map/rck,xk->rcx/dot_general | solution.py:79
  139.2 1.7 fusion.28
  140.9 15.6 %collective-permute-start.5 = (bf16[320,24]{0,1:T(8,128)(2,1)S(1)}, bf16[320,24]{0,1:T(8,128)(2,1)S(1)}, u32[]{:S(2)}, u32[]{:S(2)}) collective-permute-start(bf16[320,24]{0,1:T(8,128)(2,1)S(1)} %fusion.28), channel_id=1, source_target_pairs={{0,1},{1,2},{2,3},{3,0},{4,5},{5,6},{6,7},{7,4},{8,9},{9,10},{10,1... | collective-permute-start | bytes 46088 | tf_op jit(solution)/shard_map/ppermute | solution.py:35
  156.5 2.2 %collective-permute-start.7 = (bf16[320,24]{0,1:T(8,128)(2,1)S(1)}, bf16[320,24]{0,1:T(8,128)(2,1)S(1)}, u32[]{:S(2)}, u32[]{:S(2)}) collective-permute-start(bf16[320,24]{0,1:T(8,128)(2,1)S(1)} %fusion.28), channel_id=1, source_target_pairs={{0,3},{1,0},{2,1},{3,2},{4,7},{5,4},{6,5},{7,6},{8,11},{9,8},{10,9... | collective-permute-start | bytes 46088 | tf_op jit(solution)/shard_map/ppermute | solution.py:35
  158.7 0.7 pad_maximum_fusion.10
  159.5 0.6 collective-permute-done.6
  160.5 0.8 broadcast_in_dim.18
  161.3 5.8 %all-to-all-start.2 = ((bf16[64,17,128]{2,1,0:T(8,128)(2,1)}), bf16[64,17,128]{2,1,0:T(8,128)(2,1)S(1)}, u32[]{:S(2)}, u32[]{:S(2)}) async-start(bf16[64,17,128]{2,1,0:T(8,128)(2,1)} %broadcast_in_dim.18), calls=%async_computation.2 | async-start | bytes 786432 | tf_op jit(solution)/shard_map/all_to_all | solution.py:233
  167.4 14.7 %all-to-all-done.2 = bf16[64,17,128]{2,1,0:T(8,128)(2,1)S(1)} async-done(((bf16[64,17,128]{2,1,0:T(8,128)(2,1)}), bf16[64,17,128]{2,1,0:T(8,128)(2,1)S(1)}, u32[]{:S(2)}, u32[]{:S(2)}) %all-to-all-start.2) | async-done | bytes 278560 | tf_op jit(solution)/shard_map/all_to_all | solution.py:233
  183.0 19.8 %all_to_all.20 = f32[64,16,2]{1,2,0:T(2,128)S(1)} all-to-all(f32[64,16,2]{1,2,0:T(2,128)S(1)} %copy.73), channel_id=1, replica_groups=mesh['rows'=64,'ch'=4] {'rows'}, dimensions={0} | all-to-all | bytes 16384 | tf_op jit(solution)/shard_map/all_to_all | solution.py:250
  (77 shorter events, 5.2 us)
Async XLA Ops:
  2.0 154.5 %collective-permute-start.10 = (bf16[24,256]{1,0:T(8,128)(2,1)S(1)}, bf16[24,256]{1,0:T(8,128)(2,1)}, u32[]{:S(2)}, u32[]{:S(2)}) collective-permute-start(bf16[24,256]{1,0:T(8,128)(2,1)S(1)} %constant_dynamic-update-slice_fusion), channel_id=1, source_target_pairs={{0,3},{1,0},{2,1},{3,2},{4,7},{5,4},{6,5},{7,6},{8,11},{9,8},{10,9... | collective-permute-start | bytes 36872 | tf_op jit(solution)/shard_map/ppermute | solution.py:35
  7.2 151.5 %collective-permute-start.8 = (bf16[24,256]{1,0:T(8,128)(2,1)S(1)}, bf16[24,256]{1,0:T(8,128)(2,1)}, u32[]{:S(2)}, u32[]{:S(2)}) collective-permute-start(bf16[24,256]{1,0:T(8,128)(2,1)S(1)} %constant_dynamic-update-slice_fusion), channel_id=1, source_target_pairs={{0,1},{1,2},{2,3},{3,0},{4,5},{5,6},{6,7},{7,4},{8,9},{9,10},{10,1... | collective-permute-start | bytes 36872 | tf_op jit(solution)/shard_map/ppermute | solution.py:35
  8.2 10.7 %collective-permute-start = (bf16[2,24,2048]{2,1,0:T(8,128)(2,1)S(1)}, bf16[2,24,2048]{2,1,0:T(8,128)(2,1)S(1)}, u32[]{:S(2)}, u32[]{:S(2)}) collective-permute-start(bf16[2,24,2048]{2,1,0:T(8,128)(2,1)S(1)} %get-tuple-element.20), channel_id=1, source_target_pairs={{0,4},{4,8},{8,12},{12,16},{16,20},{20,24},{24,28},{28,32},{32,36}... | collective-permute-start | bytes 589832 | tf_op jit(solution)/shard_map/ppermute | solution.py:21
  12.2 7.0 %collective-permute-start.1 = (bf16[2,24,2048]{2,1,0:T(8,128)(2,1)S(1)}, bf16[2,24,2048]{2,1,0:T(8,128)(2,1)S(1)}, u32[]{:S(2)}, u32[]{:S(2)}) collective-permute-start(bf16[2,24,2048]{2,1,0:T(8,128)(2,1)S(1)} %get-tuple-element.21), channel_id=1, source_target_pairs={{4,0},{8,4},{12,8},{16,12},{20,16},{24,20},{28,24},{32,28},{36,32}... | collective-permute-start | bytes 589832 | tf_op jit(solution)/shard_map/ppermute | solution.py:23
  22.8 15.2 %collective-permute-start.2 = (bf16[4,24,2048]{2,1,0:T(8,128)(2,1)S(1)}, bf16[4,24,2048]{2,1,0:T(8,128)(2,1)S(1)}, u32[]{:S(2)}, u32[]{:S(2)}) collective-permute-start(bf16[4,24,2048]{2,1,0:T(8,128)(2,1)S(1)} %fusion.49), channel_id=1, source_target_pairs={{0,1},{1,2},{2,3},{3,0},{4,5},{5,6},{6,7},{7,4},{8,9},{9,10},{10,1... | collective-permute-start | bytes 1179656 | tf_op jit(solution)/shard_map/ppermute | solution.py:35
  22.9 30.3 %collective-permute-start.3 = (bf16[4,24,2048]{2,1,0:T(8,128)(2,1)S(1)}, bf16[4,24,2048]{2,1,0:T(8,128)(2,1)S(1)}, u32[]{:S(2)}, u32[]{:S(2)}) collective-permute-start(bf16[4,24,2048]{2,1,0:T(8,128)(2,1)S(1)} %fusion.49), channel_id=1, source_target_pairs={{0,2},{1,3},{2,0},{3,1},{4,6},{5,7},{6,4},{7,5},{8,10},{9,11},{10,... | collective-permute-start | bytes 1179656 | tf_op jit(solution)/shard_map/ppermute | solution.py:35
  26.7 26.5 %collective-permute-start.4 = (bf16[4,24,2048]{2,1,0:T(8,128)(2,1)S(1)}, bf16[4,24,2048]{2,1,0:T(8,128)(2,1)S(1)}, u32[]{:S(2)}, u32[]{:S(2)}) collective-permute-start(bf16[4,24,2048]{2,1,0:T(8,128)(2,1)S(1)} %fusion.49), channel_id=1, source_target_pairs={{0,3},{1,0},{2,1},{3,2},{4,7},{5,4},{6,5},{7,6},{8,11},{9,8},{10,9... | collective-permute-start | bytes 1179656 | tf_op jit(solution)/shard_map/ppermute | solution.py:35
  29.1 26.1 %copy-start = (f32[32,64,1024]{2,1,0:T(8,128)}, f32[32,64,1024]{2,1,0:T(8,128)S(1)}, u32[]{:S(2)}) copy-start(f32[32,64,1024]{2,1,0:T(8,128)S(1)} %get-tuple-element.18) | copy-start | bytes 25165828
  29.2 26.1 %copy-start.1 = (f32[32,64,1024]{2,1,0:T(8,128)}, f32[32,64,1024]{2,1,0:T(8,128)S(1)}, u32[]{:S(2)}) copy-start(f32[32,64,1024]{2,1,0:T(8,128)S(1)} %get-tuple-element.19) | copy-start | bytes 25165828
  38.0 120.7 %collective-permute-start.9 = (bf16[24,256]{1,0:T(8,128)(2,1)S(1)}, bf16[24,256]{1,0:T(8,128)(2,1)}, u32[]{:S(2)}, u32[]{:S(2)}) collective-permute-start(bf16[24,256]{1,0:T(8,128)(2,1)S(1)} %constant_dynamic-update-slice_fusion), channel_id=1, source_target_pairs={{0,2},{1,3},{2,0},{3,1},{4,6},{5,7},{6,4},{7,5},{8,10},{9,11},{10,... | collective-permute-start | bytes 36872 | tf_op jit(solution)/shard_map/ppermute | solution.py:35
  53.7 1.5 copy-start.2
  57.5 21.6 %copy-start.8 = (s32[64]{0:T(128)S(1)}, s32[64]{0:T(128)}, u32[]{:S(2)}) copy-start(s32[64]{0:T(128)} %param.19) | copy-start | bytes 772
  65.3 27.3 %all-to-all-start = ((bf16[2,64,4,384]{3,2,0,1:T(4,128)(2,1)}), bf16[2,64,4,384]{3,2,0,1:T(4,128)(2,1)S(1)}, u32[]{:S(2)}, u32[]{:S(2)}) async-start(bf16[2,64,4,384]{3,2,0,1:T(4,128)(2,1)} %copy.64), calls=%async_computation | async-start | bytes 786432 | tf_op jit(solution)/shard_map/all_to_all | solution.py:172
  78.8 23.0 %copy-start.6 = (s32[256]{0:T(256)S(1)}, s32[256]{0:T(256)}, u32[]{:S(2)}) copy-start(s32[256]{0:T(256)} %param.18) | copy-start | bytes 3076
  78.8 23.0 %copy-start.7 = (s32[64]{0:T(128)S(1)}, s32[64]{0:T(128)}, u32[]{:S(2)}) copy-start(s32[64]{0:T(128)} %param.17) | copy-start | bytes 772
  96.6 19.5 %all-to-all-start.1 = ((bf16[2,64,4,384]{3,2,0,1:T(4,128)(2,1)}), bf16[2,64,4,384]{3,2,0,1:T(4,128)(2,1)S(1)}, u32[]{:S(2)}, u32[]{:S(2)}) async-start(bf16[2,64,4,384]{3,2,0,1:T(4,128)(2,1)} %copy.70), calls=%async_computation.1 | async-start | bytes 786432 | tf_op jit(solution)/shard_map/all_to_all | solution.py:197
  125.6 8.4 %slice-start = ((s8[8388608]{0:T(1024)(128)(4,1)}), s8[4194304]{0:T(1024)(128)(4,1)S(1)}, s32[]{:S(2)}) async-start(s8[8388608]{0:T(1024)(128)(4,1)} %bitcast.71), calls=%async_computation.4 | async-start | bytes 8388608
  125.6 8.3 %slice-start.1 = ((s8[8388608]{0:T(1024)(128)(4,1)}), s8[4194304]{0:T(1024)(128)(4,1)S(1)}, s32[]{:S(2)}) async-start(s8[8388608]{0:T(1024)(128)(4,1)} %bitcast.71), calls=%async_computation.5 | async-start | bytes 8388608
  125.6 8.3 %copy-start.3 = (bf16[4,24,2048]{2,1,0:T(8,128)(2,1)S(1)}, bf16[4,24,2048]{2,1,0:T(8,128)(2,1)}, u32[]{:S(2)}) copy-start(bf16[4,24,2048]{2,1,0:T(8,128)(2,1)} %copy-done.2) | copy-start | bytes 1179652
  134.0 5.2 %copy-start.4 = (s32[4,2048]{1,0:T(4,128)S(1)}, s32[4,2048]{1,0:T(4,128)}, u32[]{:S(2)}) copy-start(s32[4,2048]{1,0:T(4,128)} %iota_add_fusion) | copy-start | bytes 98308
  134.0 5.2 %copy-start.5 = (s32[320]{0:T(512)S(1)}, s32[320]{0:T(512)}, u32[]{:S(2)}) copy-start(s32[320]{0:T(512)} %pad_add_fusion) | copy-start | bytes 3844
  134.0 26.5 %copy-start.9 = (bf16[1,128]{1,0:T(2,128)(2,1)S(1)}, bf16[1,128]{1,0:T(2,128)(2,1)}, u32[]{:S(2)}) copy-start(bf16[1,128]{1,0:T(2,128)(2,1)} %fusion.112) | copy-start | bytes 772
  139.2 64.2 %copy-start.10 = (bf16[4,24,2048]{2,1,0:T(8,128)(2,1)}, bf16[4,24,2048]{2,1,0:T(8,128)(2,1)S(1)}, u32[]{:S(2)}) copy-start(bf16[4,24,2048]{2,1,0:T(8,128)(2,1)S(1)} %fusion.9) | copy-start | bytes 1179652
  140.9 18.5 %collective-permute-start.5 = (bf16[320,24]{0,1:T(8,128)(2,1)S(1)}, bf16[320,24]{0,1:T(8,128)(2,1)S(1)}, u32[]{:S(2)}, u32[]{:S(2)}) collective-permute-start(bf16[320,24]{0,1:T(8,128)(2,1)S(1)} %fusion.28), channel_id=1, source_target_pairs={{0,1},{1,2},{2,3},{3,0},{4,5},{5,6},{6,7},{7,4},{8,9},{9,10},{10,1... | collective-permute-start | bytes 46088 | tf_op jit(solution)/shard_map/ppermute | solution.py:35
  156.5 3.5 %collective-permute-start.6 = (bf16[320,24]{0,1:T(8,128)(2,1)S(1)}, bf16[320,24]{0,1:T(8,128)(2,1)S(1)}, u32[]{:S(2)}, u32[]{:S(2)}) collective-permute-start(bf16[320,24]{0,1:T(8,128)(2,1)S(1)} %fusion.28), channel_id=1, source_target_pairs={{0,2},{1,3},{2,0},{3,1},{4,6},{5,7},{6,4},{7,5},{8,10},{9,11},{10,... | collective-permute-start | bytes 46088 | tf_op jit(solution)/shard_map/ppermute | solution.py:35
  156.5 3.5 %collective-permute-start.7 = (bf16[320,24]{0,1:T(8,128)(2,1)S(1)}, bf16[320,24]{0,1:T(8,128)(2,1)S(1)}, u32[]{:S(2)}, u32[]{:S(2)}) collective-permute-start(bf16[320,24]{0,1:T(8,128)(2,1)S(1)} %fusion.28), channel_id=1, source_target_pairs={{0,3},{1,0},{2,1},{3,2},{4,7},{5,4},{6,5},{7,6},{8,11},{9,8},{10,9... | collective-permute-start | bytes 46088 | tf_op jit(solution)/shard_map/ppermute | solution.py:35
  161.3 20.8 %all-to-all-start.2 = ((bf16[64,17,128]{2,1,0:T(8,128)(2,1)}), bf16[64,17,128]{2,1,0:T(8,128)(2,1)S(1)}, u32[]{:S(2)}, u32[]{:S(2)}) async-start(bf16[64,17,128]{2,1,0:T(8,128)(2,1)} %broadcast_in_dim.18), calls=%async_computation.2 | async-start | bytes 786432 | tf_op jit(solution)/shard_map/all_to_all | solution.py:233

commit v7 on v6

--- a/solution.py
+++ b/solution.py
@@ -227,19 +227,21 @@
         jnp.dot(own_queries, weights_all[:, key_dim:], preferred_element_type=jnp.float32)
     ).astype(jnp.bfloat16)
     targets = lax.dynamic_slice_in_dim(positives, channel * quarter, quarter, 0)
-    coded = jnp.concatenate([targets // 128, targets % 128]).astype(jnp.bfloat16)
-    coded = jnp.pad(coded, (0, key_dim - 2 * quarter))[None, :]
-    packet = jnp.concatenate([query_unit, coded], axis=0)
     gathered = lax.all_to_all(
-        jnp.broadcast_to(packet[None], (slabs,) + packet.shape),
+        jnp.broadcast_to(query_unit[None], (slabs,) + query_unit.shape),
         "rows",
         split_axis=0,
         concat_axis=0,
         tiled=True,
     )
-    all_queries = gathered[:, :quarter, :].reshape(-1, key_dim)
-    coded_all = gathered[:, quarter, :].astype(jnp.int32)
-    all_targets = (coded_all[:, :quarter] * 128 + coded_all[:, quarter : 2 * quarter]).reshape(-1)
+    all_queries = gathered.reshape(-1, key_dim)
+    all_targets = lax.all_to_all(
+        jnp.broadcast_to(targets[None], (slabs, quarter)),
+        "rows",
+        split_axis=0,
+        concat_axis=0,
+        tiled=True,
+    ).reshape(-1)
     scores = (
         jnp.einsum("qd,kd->qk", all_queries, key_unit, preferred_element_type=jnp.float32)
         * score_scale

time: 204 us -> 209 us (1.025)
  starting transfers between devices: 70.8 us -> 76.5 us
    ppermute x9, starting transfers between devices: 42 us -> 22.3 us  [ring_pieces(): lax.ppermute(values, axis, [(i, (i + shift) % count) for i in range(count)])]
    all_to_all x1 -> x2, starting transfers between devices: 5.79 us -> 21.1 us  [the longest x1 14.1 us: body(): lax.all_to_all(jnp.broadcast_to(query_unit[None], (slabs,) + query_unit.s...]
    ppermute x9, waiting for transfers between devices: 9.43 us -> 24 us  [ring_pieces(): lax.ppermute(values, axis, [(i, (i + shift) % count) for i in range(count)])]
    all_to_all x1, waiting for transfers between devices: 11.4 us -> 0.01 us  [body(): lax.all_to_all(wire.astype(jnp.bfloat16), 'rows', split_axis=1, concat_ax...]
    all_to_all x1, starting transfers between devices: 4.62 us -> 13.4 us  [body(): lax.all_to_all(back.reshape(2, slabs, slab_rows, lanes), 'rows', split_ax...]
    all_to_all x1 -> x2, waiting for transfers between devices: 14.7 us -> 11.3 us  [the longest x1 11.3 us: body(): lax.all_to_all(jnp.broadcast_to(query_unit[None], (slabs,) + query_unit.s...]
  transfers between devices with their start and end apart: 14 -> 15, of which waited for: 6 -> 6; matrix products, arithmetic and copies ran while one was open for 29% -> 22% of each run, Pallas kernels for 0% -> 0%
where the time goes in v7:
time: 209 us; the launch traced here: 208 us
  starting transfers between devices  76.5 us (37%)
  waiting for transfers between devices  49.4 us (24%)
  local copies, waits for them, and re-layouts  25 us (12%)
  matrix products  22.4 us (11%)
  blocking collectives  18 us (9%)
  other arithmetic  15.8 us (8%)
    ppermute x9, waiting for transfers between devices, ring_pieces(): lax.ppermute(values, axis, [(i, (i + shift) % count) for i in range(count)])  24 us
    ppermute x9, starting transfers between devices, ring_pieces(): lax.ppermute(values, axis, [(i, (i + shift) % count) for i in range(count)])  22.3 us
    all_to_all x1, blocking collectives, body(): lax.all_to_all(jnp.stack([exp_sums, picked], axis=1).reshape(slabs, quart...  18 us
    dot_general x4, matrix products, two_pass(): jnp.einsum(eq, left, part, preferred_element_type=jnp.float32)  16.4 us
    all_to_all x1, starting transfers between devices, body(): lax.all_to_all(jnp.broadcast_to(query_unit[None], (slabs,) + query_unit.s...  14.1 us
    all_to_all x1, waiting for transfers between devices, body(): lax.all_to_all(back.reshape(2, slabs, slab_rows, lanes), 'rows', split_ax...  13.6 us
    all_to_all x1, starting transfers between devices, body(): lax.all_to_all(back.reshape(2, slabs, slab_rows, lanes), 'rows', split_ax...  13.4 us
    all_to_all x1, starting transfers between devices, body(): lax.all_to_all(wire.astype(jnp.bfloat16), 'rows', split_axis=1, concat_ax...  13.4 us
  transfers between devices with their start and end apart: 15, of which 6 were waited for; matrix products, arithmetic and copies ran while one was open for 22% of the time, Pallas kernels for 0%

profile of v7, /device:TPU:1, one launch (start us, length us, event | category | flops | bytes accessed | tf_op | source)
XLA Modules:
  0.0 208.3 jit_solution(14432909118341670674)
XLA Ops:
  0.6 1.1 fusion.119
  1.7 4.5 %collective-permute-start = (bf16[2,24,2048]{2,1,0:T(8,128)(2,1)S(1)}, bf16[2,24,2048]{2,1,0:T(8,128)(2,1)S(1)}, u32[]{:S(2)}, u32[]{:S(2)}) collective-permute-start(bf16[2,24,2048]{2,1,0:T(8,128)(2,1)S(1)} %get-tuple-element.18), channel_id=1, source_target_pairs={{0,4},{4,8},{8,12},{12,16},{16,20},{20,24},{24,28},{28,32},{32,36}... | collective-permute-start | bytes 589832 | tf_op jit(solution)/shard_map/ppermute | solution.py:21
  6.2 1.9 collective-permute-start.1
  8.1 1.0 fusion.86
  9.8 0.9 fusion.120
  11.0 0.7 constant_dynamic-update-slice_fusion.1
  11.7 1.0 slice_bitcast_fusion.8
  13.2 1.3 fusion.40
  14.5 2.3 %fusion.49 = bf16[4,24,2048]{2,1,0:T(8,128)(2,1)S(1)} fusion(bf16[4,24,2048]{2,1,0:T(8,128)(2,1)} %param.10, bf16[8,24,2052]{2,1,0:T(8,128)(2,1)S(1)} %fusion.40, bf16[2,24,2048]{2,1,0:T(8,128)(2,1)S(1)} %collective-permute-done.1, bf16[2,24,2048]{2,1,0:T(8,128)(2,1)S(1)} %collective-permute-done, f32[24]{0:T(128)S(1)} %get-tuple-element.31, ...), kind=kLoop, calls=%fused_computation.62 | loop fusion | flops 5898240 | bytes 3539808 | tf_op jit(solution)/shard_map/convert_element_type | solution.py:147
  16.8 1.7 collective-permute-start.2
  18.5 3.0 %collective-permute-start.3 = (bf16[4,24,2048]{2,1,0:T(8,128)(2,1)S(1)}, bf16[4,24,2048]{2,1,0:T(8,128)(2,1)S(1)}, u32[]{:S(2)}, u32[]{:S(2)}) collective-permute-start(bf16[4,24,2048]{2,1,0:T(8,128)(2,1)S(1)} %fusion.49), channel_id=1, source_target_pairs={{0,2},{1,3},{2,0},{3,1},{4,6},{5,7},{6,4},{7,5},{8,10},{9,11},{10,... | collective-permute-start | bytes 1179656 | tf_op jit(solution)/shard_map/ppermute | solution.py:35
  21.5 0.7 collective-permute-start.4
  22.2 2.5 %multiply_subtract_fusion = (f32[32,64,1024]{2,1,0:T(8,128)S(1)}, f32[32,64,1024]{2,1,0:T(8,128)S(1)}) fusion(f32[64,1024]{1,0:T(8,128)S(1)} %get-tuple-element.11, f32[32,1024]{1,0:T(8,128)S(1)} %get-tuple-element.10, f32[64,1024]{1,0:T(8,128)S(1)} %get-tuple-element.9, f32[32,1024]{1,0:T(8,128)S(1)} %get-tuple-element.8), kind=kLoop, calls=%fused_computation.8 | loop fusion | flops 14680064 | bytes 17563648 | tf_op jit(solution)/shard_map/sub | solution.py:71
  24.7 7.1 %collective-permute-done.2 = bf16[4,24,2048]{2,1,0:T(8,128)(2,1)S(1)} collective-permute-done((bf16[4,24,2048]{2,1,0:T(8,128)(2,1)S(1)}, bf16[4,24,2048]{2,1,0:T(8,128)(2,1)S(1)}, u32[]{:S(2)}, u32[]{:S(2)}) %collective-permute-start.2) | collective-permute-done | bytes 393248 | tf_op jit(solution)/shard_map/ppermute | solution.py:35
  31.7 16.3 %collective-permute-done.3 = bf16[4,24,2048]{2,1,0:T(8,128)(2,1)S(1)} collective-permute-done((bf16[4,24,2048]{2,1,0:T(8,128)(2,1)S(1)}, bf16[4,24,2048]{2,1,0:T(8,128)(2,1)S(1)}, u32[]{:S(2)}, u32[]{:S(2)}) %collective-permute-start.3) | collective-permute-done | bytes 393248 | tf_op jit(solution)/shard_map/ppermute | solution.py:35
  48.6 1.5 fusion.23
  50.1 1.5 fusion.8
  51.7 2.5 %convert_element_type.142 = bf16[4,24,2,64,16]{4,3,2,1,0:T(8,128)(2,1)S(1)} reshape(bf16[4,24,2048]{2,1,0:T(8,128)(2,1)S(1)} %fusion.8) | data formatting | bytes 786432 | tf_op jit(solution)/shard_map/convert_element_type | solution.py:173
  54.2 2.3 %copy.63 = bf16[2,64,4,24,16]{1,4,3,2,0:T(8,128)(2,1)} copy(bf16[2,64,4,24,16]{4,1,0,3,2:T(8,128)(2,1)S(1)} %bitcast.75) | data formatting | bytes 786432 | tf_op jit(solution)/shard_map/convert_element_type | solution.py:173
  56.5 2.2 %copy.64 = bf16[2,64,4,384]{3,2,0,1:T(4,128)(2,1)} copy(bf16[2,64,4,384]{1,3,2,0:T(8,128)(2,1)} %bitcast.76) | data formatting | bytes 786432 | tf_op jit(solution)/shard_map/convert_element_type | solution.py:173
  58.6 13.4 %all-to-all-start = ((bf16[2,64,4,384]{3,2,0,1:T(4,128)(2,1)}), bf16[2,64,4,384]{3,2,0,1:T(4,128)(2,1)S(1)}, u32[]{:S(2)}, u32[]{:S(2)}) async-start(bf16[2,64,4,384]{3,2,0,1:T(4,128)(2,1)} %copy.64), calls=%async_computation | async-start | bytes 786432 | tf_op jit(solution)/shard_map/all_to_all | solution.py:172
  72.0 0.7 constant_dynamic-update-slice_fusion
  72.7 8.2 %collective-permute-start.10 = (bf16[24,256]{1,0:T(8,128)(2,1)S(1)}, bf16[24,256]{1,0:T(8,128)(2,1)}, u32[]{:S(2)}, u32[]{:S(2)}) collective-permute-start(bf16[24,256]{1,0:T(8,128)(2,1)S(1)} %constant_dynamic-update-slice_fusion), channel_id=1, source_target_pairs={{0,3},{1,0},{2,1},{3,2},{4,7},{5,4},{6,5},{7,6},{8,11},{9,8},{10,9... | collective-permute-start | bytes 36872 | tf_op jit(solution)/shard_map/ppermute | solution.py:35
  81.4 1.2 collective-permute-start.9
  82.6 1.0 bitcast_convert_fusion
  83.7 1.0 bitcast_convert_fusion.1
  85.0 1.0 fusion.85
  85.9 1.0 broadcast_multiply_fusion.1
  88.2 1.8 fusion.18
  90.1 0.9 copy.70
  91.0 13.4 %all-to-all-start.1 = ((bf16[2,64,4,384]{3,2,0,1:T(4,128)(2,1)}), bf16[2,64,4,384]{3,2,0,1:T(4,128)(2,1)S(1)}, u32[]{:S(2)}, u32[]{:S(2)}) async-start(bf16[2,64,4,384]{3,2,0,1:T(4,128)(2,1)} %copy.70), calls=%async_computation.1 | async-start | bytes 786432 | tf_op jit(solution)/shard_map/all_to_all | solution.py:197
  104.9 0.7 iota_add_fusion
  105.6 13.6 %all-to-all-done.1 = bf16[2,64,4,384]{3,2,0,1:T(4,128)(2,1)S(1)} async-done(((bf16[2,64,4,384]{3,2,0,1:T(4,128)(2,1)}), bf16[2,64,4,384]{3,2,0,1:T(4,128)(2,1)S(1)}, u32[]{:S(2)}, u32[]{:S(2)}) %all-to-all-start.1) | async-done | bytes 393248 | tf_op jit(solution)/shard_map/all_to_all | solution.py:197
  119.9 7.0 %all-to-all-start.3 = ((s32[64,1,16]{2,1,0:T(1,128)}), s32[64,1,16]{2,1,0:T(1,128)}, u32[]{:S(2)}, u32[]{:S(2)}) async-start(s32[64,1,16]{2,1,0:T(1,128)} %broadcast_in_dim.18), calls=%async_computation.3 | async-start | bytes 65536 | tf_op jit(solution)/shard_map/all_to_all | solution.py:238
  126.9 1.3 copy.71
  128.2 2.8 %copy.72 = bf16[4,24,2,64,16]{4,3,2,1,0:T(8,128)(2,1)S(1)} copy(bf16[4,24,2,64,16]{3,4,1,0,2:T(8,128)(2,1)} %bitcast.77) | data formatting | bytes 786432 | tf_op jit(solution)/shard_map/transpose | solution.py:200
  131.0 5.4 %reshape.145 = bf16[4,24,2048]{2,1,0:T(8,128)(2,1)S(1)} reshape(bf16[4,24,2,64,16]{4,3,2,1,0:T(8,128)(2,1)S(1)} %copy.72) | data formatting | bytes 786432 | tf_op jit(solution)/shard_map/reshape | solution.py:200
  136.5 8.3 %fusion.21 = f32[4,24,2048]{2,1,0:T(8,128)S(1)} fusion(bf16[4,24,2048]{2,1,0:T(8,128)(2,1)S(1)} %broadcast_multiply_fusion, f32[2048,1024]{1,0:T(8,128)} %bitcast.73, f32[2048,1024]{1,0:T(8,128)} %bitcast.67), kind=kOutput, calls=%fused_computation.35 | convolution fusion | flops 822083584 | bytes 17956864 | tf_op jit(solution)/shard_map/rck,xk->rcx/dot_general | solution.py:79
  144.9 5.1 %fusion.9 = bf16[4,24,2048]{2,1,0:T(8,128)(2,1)S(1)} fusion(f32[4,24,2048]{2,1,0:T(8,128)S(1)} %fusion.21, bf16[4,24,2048]{2,1,0:T(8,128)(2,1)S(1)} %broadcast_multiply_fusion, f32[2048,1024]{1,0:T(8,128)} %bitcast.74, f32[2048,1024]{1,0:T(8,128)S(1)} %bitcast.70, bf16[4,24,2048]{2,1,0:T(8,128)(2,1)S(1)} %copy-done.3), kind=kOutput, calls=%fused_computation.18 | convolution fusion | flops 827064320 | bytes 18743296 | tf_op jit(solution)/shard_map/rck,xk->rcx/dot_general | solution.py:79
  150.0 1.7 fusion.28
  151.8 4.8 %collective-permute-start.5 = (bf16[320,24]{0,1:T(8,128)(2,1)S(1)}, bf16[320,24]{0,1:T(8,128)(2,1)S(1)}, u32[]{:S(2)}, u32[]{:S(2)}) collective-permute-start(bf16[320,24]{0,1:T(8,128)(2,1)S(1)} %fusion.28), channel_id=1, source_target_pairs={{0,1},{1,2},{2,3},{3,0},{4,5},{5,6},{6,7},{7,4},{8,9},{9,10},{10,1... | collective-permute-start | bytes 46088 | tf_op jit(solution)/shard_map/ppermute | solution.py:35
  156.6 2.2 %collective-permute-start.7 = (bf16[320,24]{0,1:T(8,128)(2,1)S(1)}, bf16[320,24]{0,1:T(8,128)(2,1)S(1)}, u32[]{:S(2)}, u32[]{:S(2)}) collective-permute-start(bf16[320,24]{0,1:T(8,128)(2,1)S(1)} %fusion.28), channel_id=1, source_target_pairs={{0,3},{1,0},{2,1},{3,2},{4,7},{5,4},{6,5},{7,6},{8,11},{9,8},{10,9... | collective-permute-start | bytes 46088 | tf_op jit(solution)/shard_map/ppermute | solution.py:35
  158.7 0.7 pad_maximum_fusion.10
  160.5 0.8 broadcast_in_dim.17
  161.3 14.1 %all-to-all-start.2 = ((bf16[64,16,128]{2,1,0:T(8,128)(2,1)}), bf16[64,16,128]{2,1,0:T(8,128)(2,1)S(1)}, u32[]{:S(2)}, u32[]{:S(2)}) async-start(bf16[64,16,128]{2,1,0:T(8,128)(2,1)} %broadcast_in_dim.17), calls=%async_computation.2 | async-start | bytes 524288 | tf_op jit(solution)/shard_map/all_to_all | solution.py:230
  175.9 1.5 reduce.3
  177.7 11.3 %all-to-all-done.2 = bf16[64,16,128]{2,1,0:T(8,128)(2,1)S(1)} async-done(((bf16[64,16,128]{2,1,0:T(8,128)(2,1)}), bf16[64,16,128]{2,1,0:T(8,128)(2,1)S(1)}, u32[]{:S(2)}, u32[]{:S(2)}) %all-to-all-start.2) | async-done | bytes 262176 | tf_op jit(solution)/shard_map/all_to_all | solution.py:230
  189.7 18.0 %all_to_all.26 = f32[64,16,2]{1,2,0:T(2,128)S(1)} all-to-all(f32[64,16,2]{1,2,0:T(2,128)S(1)} %copy.73), channel_id=1, replica_groups=mesh['rows'=64,'ch'=4] {'rows'}, dimensions={0} | all-to-all | bytes 16384 | tf_op jit(solution)/shard_map/all_to_all | solution.py:252
  (74 shorter events, 8.5 us)
Async XLA Ops:
  1.7 11.0 %collective-permute-start = (bf16[2,24,2048]{2,1,0:T(8,128)(2,1)S(1)}, bf16[2,24,2048]{2,1,0:T(8,128)(2,1)S(1)}, u32[]{:S(2)}, u32[]{:S(2)}) collective-permute-start(bf16[2,24,2048]{2,1,0:T(8,128)(2,1)S(1)} %get-tuple-element.18), channel_id=1, source_target_pairs={{0,4},{4,8},{8,12},{12,16},{16,20},{20,24},{24,28},{28,32},{32,36}... | collective-permute-start | bytes 589832 | tf_op jit(solution)/shard_map/ppermute | solution.py:21
  6.2 7.0 %collective-permute-start.1 = (bf16[2,24,2048]{2,1,0:T(8,128)(2,1)S(1)}, bf16[2,24,2048]{2,1,0:T(8,128)(2,1)S(1)}, u32[]{:S(2)}, u32[]{:S(2)}) collective-permute-start(bf16[2,24,2048]{2,1,0:T(8,128)(2,1)S(1)} %get-tuple-element.19), channel_id=1, source_target_pairs={{4,0},{8,4},{12,8},{16,12},{20,16},{24,20},{28,24},{32,28},{36,32}... | collective-permute-start | bytes 589832 | tf_op jit(solution)/shard_map/ppermute | solution.py:23
  16.8 15.0 %collective-permute-start.2 = (bf16[4,24,2048]{2,1,0:T(8,128)(2,1)S(1)}, bf16[4,24,2048]{2,1,0:T(8,128)(2,1)S(1)}, u32[]{:S(2)}, u32[]{:S(2)}) collective-permute-start(bf16[4,24,2048]{2,1,0:T(8,128)(2,1)S(1)} %fusion.49), channel_id=1, source_target_pairs={{0,1},{1,2},{2,3},{3,0},{4,5},{5,6},{6,7},{7,4},{8,9},{9,10},{10,1... | collective-permute-start | bytes 1179656 | tf_op jit(solution)/shard_map/ppermute | solution.py:35
  18.5 29.6 %collective-permute-start.3 = (bf16[4,24,2048]{2,1,0:T(8,128)(2,1)S(1)}, bf16[4,24,2048]{2,1,0:T(8,128)(2,1)S(1)}, u32[]{:S(2)}, u32[]{:S(2)}) collective-permute-start(bf16[4,24,2048]{2,1,0:T(8,128)(2,1)S(1)} %fusion.49), channel_id=1, source_target_pairs={{0,2},{1,3},{2,0},{3,1},{4,6},{5,7},{6,4},{7,5},{8,10},{9,11},{10,... | collective-permute-start | bytes 1179656 | tf_op jit(solution)/shard_map/ppermute | solution.py:35
  21.5 26.6 %collective-permute-start.4 = (bf16[4,24,2048]{2,1,0:T(8,128)(2,1)S(1)}, bf16[4,24,2048]{2,1,0:T(8,128)(2,1)S(1)}, u32[]{:S(2)}, u32[]{:S(2)}) collective-permute-start(bf16[4,24,2048]{2,1,0:T(8,128)(2,1)S(1)} %fusion.49), channel_id=1, source_target_pairs={{0,3},{1,0},{2,1},{3,2},{4,7},{5,4},{6,5},{7,6},{8,11},{9,8},{10,9... | collective-permute-start | bytes 1179656 | tf_op jit(solution)/shard_map/ppermute | solution.py:35
  24.7 25.5 %copy-start = (f32[32,64,1024]{2,1,0:T(8,128)}, f32[32,64,1024]{2,1,0:T(8,128)S(1)}, u32[]{:S(2)}) copy-start(f32[32,64,1024]{2,1,0:T(8,128)S(1)} %get-tuple-element.16) | copy-start | bytes 25165828
  24.7 25.5 %copy-start.1 = (f32[32,64,1024]{2,1,0:T(8,128)}, f32[32,64,1024]{2,1,0:T(8,128)S(1)}, u32[]{:S(2)}) copy-start(f32[32,64,1024]{2,1,0:T(8,128)S(1)} %get-tuple-element.17) | copy-start | bytes 25165828
  48.6 1.5 copy-start.2
  51.6 33.3 %copy-start.8 = (s32[64]{0:T(128)S(1)}, s32[64]{0:T(128)}, u32[]{:S(2)}) copy-start(s32[64]{0:T(128)} %param.19) | copy-start | bytes 772
  58.6 28.3 %all-to-all-start = ((bf16[2,64,4,384]{3,2,0,1:T(4,128)(2,1)}), bf16[2,64,4,384]{3,2,0,1:T(4,128)(2,1)S(1)}, u32[]{:S(2)}, u32[]{:S(2)}) async-start(bf16[2,64,4,384]{3,2,0,1:T(4,128)(2,1)} %copy.64), calls=%async_computation | async-start | bytes 786432 | tf_op jit(solution)/shard_map/all_to_all | solution.py:172
  72.7 83.8 %collective-permute-start.10 = (bf16[24,256]{1,0:T(8,128)(2,1)S(1)}, bf16[24,256]{1,0:T(8,128)(2,1)}, u32[]{:S(2)}, u32[]{:S(2)}) collective-permute-start(bf16[24,256]{1,0:T(8,128)(2,1)S(1)} %constant_dynamic-update-slice_fusion), channel_id=1, source_target_pairs={{0,3},{1,0},{2,1},{3,2},{4,7},{5,4},{6,5},{7,6},{8,11},{9,8},{10,9... | collective-permute-start | bytes 36872 | tf_op jit(solution)/shard_map/ppermute | solution.py:35
  80.9 77.8 %collective-permute-start.8 = (bf16[24,256]{1,0:T(8,128)(2,1)S(1)}, bf16[24,256]{1,0:T(8,128)(2,1)}, u32[]{:S(2)}, u32[]{:S(2)}) collective-permute-start(bf16[24,256]{1,0:T(8,128)(2,1)S(1)} %constant_dynamic-update-slice_fusion), channel_id=1, source_target_pairs={{0,1},{1,2},{2,3},{3,0},{4,5},{5,6},{6,7},{7,4},{8,9},{9,10},{10,1... | collective-permute-start | bytes 36872 | tf_op jit(solution)/shard_map/ppermute | solution.py:35
  81.4 77.3 %collective-permute-start.9 = (bf16[24,256]{1,0:T(8,128)(2,1)S(1)}, bf16[24,256]{1,0:T(8,128)(2,1)}, u32[]{:S(2)}, u32[]{:S(2)}) collective-permute-start(bf16[24,256]{1,0:T(8,128)(2,1)S(1)} %constant_dynamic-update-slice_fusion), channel_id=1, source_target_pairs={{0,2},{1,3},{2,0},{3,1},{4,6},{5,7},{6,4},{7,5},{8,10},{9,11},{10,... | collective-permute-start | bytes 36872 | tf_op jit(solution)/shard_map/ppermute | solution.py:35
  84.7 19.7 %copy-start.6 = (s32[256]{0:T(256)S(1)}, s32[256]{0:T(256)}, u32[]{:S(2)}) copy-start(s32[256]{0:T(256)} %param.18) | copy-start | bytes 3076
  84.7 19.7 %copy-start.7 = (s32[64]{0:T(128)S(1)}, s32[64]{0:T(128)}, u32[]{:S(2)}) copy-start(s32[64]{0:T(128)} %param.17) | copy-start | bytes 772
  91.0 28.3 %all-to-all-start.1 = ((bf16[2,64,4,384]{3,2,0,1:T(4,128)(2,1)}), bf16[2,64,4,384]{3,2,0,1:T(4,128)(2,1)S(1)}, u32[]{:S(2)}, u32[]{:S(2)}) async-start(bf16[2,64,4,384]{3,2,0,1:T(4,128)(2,1)} %copy.70), calls=%async_computation.1 | async-start | bytes 786432 | tf_op jit(solution)/shard_map/all_to_all | solution.py:197
  119.9 40.6 %all-to-all-start.3 = ((s32[64,1,16]{2,1,0:T(1,128)}), s32[64,1,16]{2,1,0:T(1,128)}, u32[]{:S(2)}, u32[]{:S(2)}) async-start(s32[64,1,16]{2,1,0:T(1,128)} %broadcast_in_dim.18), calls=%async_computation.3 | async-start | bytes 65536 | tf_op jit(solution)/shard_map/all_to_all | solution.py:238
  136.4 8.4 %slice-start = ((s8[8388608]{0:T(1024)(128)(4,1)}), s8[4194304]{0:T(1024)(128)(4,1)S(1)}, s32[]{:S(2)}) async-start(s8[8388608]{0:T(1024)(128)(4,1)} %bitcast.68), calls=%async_computation.5 | async-start | bytes 8388608
  136.5 8.3 %slice-start.1 = ((s8[8388608]{0:T(1024)(128)(4,1)}), s8[4194304]{0:T(1024)(128)(4,1)S(1)}, s32[]{:S(2)}) async-start(s8[8388608]{0:T(1024)(128)(4,1)} %bitcast.68), calls=%async_computation.6 | async-start | bytes 8388608
  136.5 8.3 %copy-start.3 = (bf16[4,24,2048]{2,1,0:T(8,128)(2,1)S(1)}, bf16[4,24,2048]{2,1,0:T(8,128)(2,1)}, u32[]{:S(2)}) copy-start(bf16[4,24,2048]{2,1,0:T(8,128)(2,1)} %copy-done.2) | copy-start | bytes 1179652
  144.8 5.2 %copy-start.4 = (s32[4,2048]{1,0:T(4,128)S(1)}, s32[4,2048]{1,0:T(4,128)}, u32[]{:S(2)}) copy-start(s32[4,2048]{1,0:T(4,128)} %iota_add_fusion) | copy-start | bytes 98308
  144.8 5.2 %copy-start.5 = (s32[320]{0:T(512)S(1)}, s32[320]{0:T(512)}, u32[]{:S(2)}) copy-start(s32[320]{0:T(512)} %pad_add_fusion) | copy-start | bytes 3844
  150.0 58.3 %copy-start.9 = (bf16[4,24,2048]{2,1,0:T(8,128)(2,1)}, bf16[4,24,2048]{2,1,0:T(8,128)(2,1)S(1)}, u32[]{:S(2)}) copy-start(bf16[4,24,2048]{2,1,0:T(8,128)(2,1)S(1)} %fusion.9) | copy-start | bytes 1179652
  151.8 7.7 %collective-permute-start.5 = (bf16[320,24]{0,1:T(8,128)(2,1)S(1)}, bf16[320,24]{0,1:T(8,128)(2,1)S(1)}, u32[]{:S(2)}, u32[]{:S(2)}) collective-permute-start(bf16[320,24]{0,1:T(8,128)(2,1)S(1)} %fusion.28), channel_id=1, source_target_pairs={{0,1},{1,2},{2,3},{3,0},{4,5},{5,6},{6,7},{7,4},{8,9},{9,10},{10,1... | collective-permute-start | bytes 46088 | tf_op jit(solution)/shard_map/ppermute | solution.py:35
  156.6 3.5 %collective-permute-start.6 = (bf16[320,24]{0,1:T(8,128)(2,1)S(1)}, bf16[320,24]{0,1:T(8,128)(2,1)S(1)}, u32[]{:S(2)}, u32[]{:S(2)}) collective-permute-start(bf16[320,24]{0,1:T(8,128)(2,1)S(1)} %fusion.28), channel_id=1, source_target_pairs={{0,2},{1,3},{2,0},{3,1},{4,6},{5,7},{6,4},{7,5},{8,10},{9,11},{10,... | collective-permute-start | bytes 46088 | tf_op jit(solution)/shard_map/ppermute | solution.py:35
  156.6 3.5 %collective-permute-start.7 = (bf16[320,24]{0,1:T(8,128)(2,1)S(1)}, bf16[320,24]{0,1:T(8,128)(2,1)S(1)}, u32[]{:S(2)}, u32[]{:S(2)}) collective-permute-start(bf16[320,24]{0,1:T(8,128)(2,1)S(1)} %fusion.28), channel_id=1, source_target_pairs={{0,3},{1,0},{2,1},{3,2},{4,7},{5,4},{6,5},{7,6},{8,11},{9,8},{10,9... | collective-permute-start | bytes 46088 | tf_op jit(solution)/shard_map/ppermute | solution.py:35
  161.3 27.7 %all-to-all-start.2 = ((bf16[64,16,128]{2,1,0:T(8,128)(2,1)}), bf16[64,16,128]{2,1,0:T(8,128)(2,1)S(1)}, u32[]{:S(2)}, u32[]{:S(2)}) async-start(bf16[64,16,128]{2,1,0:T(8,128)(2,1)} %broadcast_in_dim.17), calls=%async_computation.2 | async-start | bytes 524288 | tf_op jit(solution)/shard_map/all_to_all | solution.py:230
